TPU v7x, 32 devices: a whole 2x2x4 slice. The times are simulated.
32 devices in a mesh: tm: 16 (over z, y, x), space: 2 (over core).
Axes of the slice: x: 2, y: 2, z: 4, core: 2. Of those that a mesh axis runs over, the one named last changes fastest.
Arguments:
- frames_feat: bfloat16 [16, 4, 64, 256], P('tm', 'space'), may hold values from -16 to 16
- prompt_labels: int32 [4, 64], P('space'), may hold values from 0 to 3
- label_table: float32 [4, 256], replicated, may hold values from -6 to 6
- enc_qkv: bfloat16 [256, 768], replicated, may hold values from -0.375 to 0.375
- enc_out: bfloat16 [256, 256], replicated, may hold values from -0.375 to 0.375
- norm_gain: float32 [256], replicated, may hold values from 0.25 to 1.75
- key_proj: bfloat16 [256, 1024], replicated, may hold values from -0.375 to 0.375
- value_proj: bfloat16 [256, 1024], replicated, may hold values from -0.375 to 0.375
- read_proj: bfloat16 [1024, 256], replicated, may hold values from -0.1875 to 0.1875
- decay: float32 [16, 8], P('tm'), may hold values from 0.1 to 1
- dec_conv: bfloat16 [3, 3, 256, 64], replicated, may hold values from -0.125 to 0.125
- dec_up: bfloat16 [64, 16], replicated, may hold values from -0.75 to 0.75
Outputs:
- mask_logits: float32 [16, 16, 256], P('tm', 'space')
All inputs are finite; a program needn't handle non-finite values.
Results may differ from a plain program's by a relative error of at most 0.011.
The roundings to bfloat16 on the way count: a program that leaves them out, or rounds other values in their place, can miss the bound.
Values may be sent and summed in bfloat16 or wider, within the bound.
No kernel may reach another device: no remote copies, remote signals or barrier semaphores. Data moves between devices by JAX's collectives and lax.ppermute only.
A program may use at most 64 MiB of HBM per device.

v0:
```python
import jax
import jax.numpy as jnp
from jax import lax
from jax.sharding import PartitionSpec as P

ENC_HEADS = 8
UP = 4


epsilon = 1e-06
lowest = -1e30
precise_result = lax.Precision.HIGHEST


def entering(x, axis, combine, identity):
    devices, place = (lax.axis_size(axis), lax.axis_index(axis))
    everything = jax.tree.map(lambda part: lax.all_gather(part, axis), x)
    start = jax.tree.map(
        lambda part, zero: jnp.broadcast_to(jnp.asarray(zero, part.dtype), part.shape), x, identity
    )

    def hop(k, before):
        reached = k < place
        new = combine(before, jax.tree.map(lambda part: part[k], everything))
        return jax.tree.map(lambda a, b: jnp.where(reached, a, b), new, before)

    return lax.fori_loop(0, devices, hop, start)


def extended(cells, sides, width):
    for axis, dim in sides:
        count = lax.axis_size(axis)
        ends = count - 1
        head = lax.slice_in_dim(cells, 0, width, axis=dim)
        tail = lax.slice_in_dim(cells, cells.shape[dim] - width, cells.shape[dim], axis=dim)
        cells = jnp.concatenate(
            [
                lax.ppermute(tail, axis, [(i, (i + 1) % count) for i in range(ends)]),
                cells,
                lax.ppermute(head, axis, [((i + 1) % count, i) for i in range(ends)]),
            ],
            axis=dim,
        )
    return cells


def pool_pairs(features):
    frame_count, height, breadth, channels = features.shape
    grouped = features.astype(jnp.float32).reshape(
        frame_count, height // 2, 2, breadth // 2, 2, channels
    )
    return jnp.mean(grouped, axis=(2, 4)).astype(jnp.bfloat16)


def gain_norm(hidden, gain_row):
    return (
        hidden * lax.rsqrt(jnp.mean(hidden * hidden, axis=-1, keepdims=True) + epsilon) * gain_row
    )


def attend_block(carried, key_part, value_part, query_heads, head_size):
    peak, totals, summed = carried
    frame_count = key_part.shape[0]
    key_head_rows = key_part.reshape(frame_count, -1, ENC_HEADS, head_size)
    value_head_rows = value_part.reshape(frame_count, -1, ENC_HEADS, head_size)
    scores = jnp.einsum(
        "ftha,fnha->fhtn", query_heads, key_head_rows, preferred_element_type=jnp.float32
    ) * head_size ** (-0.5)
    newest = jnp.maximum(peak, jnp.max(scores, axis=-1))
    weights = jnp.exp(scores - newest[..., None])
    totals = jnp.sum(weights, axis=-1)
    summed = jnp.einsum(
        "fhtn,fnha->fhta",
        weights.astype(jnp.bfloat16),
        value_head_rows,
        preferred_element_type=jnp.float32,
    )
    return (newest, totals, summed)


def link(earlier, later):
    return (earlier[0] * later[0], later[0][:, None, None] * earlier[1] + later[1])


def local_chain(rate_rows, states):
    product = jnp.ones(rate_rows.shape[1:], jnp.float32)
    summed = jnp.zeros(states.shape[1:], jnp.float32)
    product = product * rate_rows[0]
    summed = rate_rows[0][:, None, None] * summed + states[0]
    return (product, summed)


def spread_chain(rate_rows, incoming):
    memory = rate_rows[0][:, None, None] * incoming
    memories = [memory]
    return jnp.stack(memories, axis=0)


def shards(
    frames_feat,
    prompt_labels,
    label_table,
    enc_qkv,
    enc_out,
    norm_gain,
    key_proj,
    value_proj,
    read_proj,
    decay,
    dec_conv,
    dec_up,
):
    frame_count, tile_rows, grid_width, model_dim = frames_feat.shape
    tile_tok = tile_rows * grid_width
    frame_tokens = tile_tok * lax.axis_size("space")
    head_size = model_dim // ENC_HEADS
    flat_rows = frames_feat.reshape(frame_count, tile_tok, model_dim)
    pooled = pool_pairs(frames_feat).reshape(frame_count, tile_tok // 4, model_dim)
    queries = jnp.dot(flat_rows, enc_qkv[:, :model_dim], preferred_element_type=jnp.float32).astype(
        jnp.bfloat16
    )
    query_heads = queries.reshape(frame_count, tile_tok, ENC_HEADS, head_size)
    initial = (
        jnp.full((frame_count, ENC_HEADS, tile_tok), lowest, jnp.float32),
        jnp.zeros((frame_count, ENC_HEADS, tile_tok), jnp.float32),
        jnp.zeros((frame_count, ENC_HEADS, tile_tok, head_size), jnp.float32),
    )
    pair_kv = jnp.dot(pooled, enc_qkv[:, model_dim:], preferred_element_type=jnp.float32).astype(
        jnp.bfloat16
    )
    peak, totals, summed = attend_block(
        initial,
        lax.all_gather(pair_kv[..., :model_dim], "space", axis=1, tiled=True),
        lax.all_gather(pair_kv[..., model_dim:], "space", axis=1, tiled=True),
        query_heads,
        head_size,
    )
    attended = (
        (summed / totals[..., None])
        .transpose(0, 2, 1, 3)
        .reshape(frame_count, tile_tok, model_dim)
        .astype(jnp.bfloat16)
    )
    hidden = flat_rows.astype(jnp.float32) + jnp.dot(
        attended, enc_out, preferred_element_type=jnp.float32
    )
    encoded = gain_norm(hidden, norm_gain).astype(jnp.bfloat16)
    key_rows = jnp.dot(encoded, key_proj, preferred_element_type=jnp.float32).astype(jnp.bfloat16)
    global_frame = lax.axis_index("tm") * frame_count + jnp.arange(frame_count)
    first_flag = (global_frame == 0).astype(jnp.float32)[:, None, None]
    one_hot = (
        prompt_labels.reshape(tile_tok, 1) == jnp.arange(label_table.shape[0])[None, :]
    ).astype(jnp.float32)
    label_rows = jnp.dot(one_hot, label_table, precision=precise_result)
    memory_in = (encoded.astype(jnp.float32) + first_flag * label_rows[None]).astype(jnp.bfloat16)
    value_rows = jnp.dot(memory_in, value_proj, preferred_element_type=jnp.float32).astype(
        jnp.bfloat16
    )
    head_count = decay.shape[1]
    key_head_rows = key_rows.reshape(frame_count, tile_tok, head_count, -1)
    value_head_rows = value_rows.reshape(frame_count, tile_tok, head_count, -1)
    partial_value = jnp.einsum(
        "fthk,fthv->fhkv", key_head_rows, value_head_rows, preferred_element_type=jnp.float32
    ) * frame_tokens ** (-0.5)
    share = head_count // lax.axis_size("space")
    states = lax.psum_scatter(partial_value, "space", scatter_dimension=1, tiled=True)
    rate_rows = lax.dynamic_slice_in_dim(decay, lax.axis_index("space") * share, share, 1)
    product, local_sum = local_chain(rate_rows, states)
    identity = (jnp.ones(product.shape, jnp.float32), jnp.zeros(local_sum.shape, jnp.float32))
    earlier = entering((product, local_sum), "tm", link, identity)
    own_memory = spread_chain(rate_rows, earlier[1]).astype(jnp.bfloat16)
    memory = lax.all_gather(own_memory, "space", axis=1, tiled=True)
    memory_output = jnp.einsum(
        "fthk,fhkv->fthv", key_head_rows, memory, preferred_element_type=jnp.float32
    ) * key_head_rows.shape[-1] ** (-0.5)
    memory_output = memory_output.reshape(frame_count, tile_tok, -1).astype(jnp.bfloat16)
    joined_rows = encoded.astype(jnp.float32) + jnp.dot(
        memory_output, read_proj, preferred_element_type=jnp.float32
    )
    decoder_in = joined_rows.astype(jnp.bfloat16).reshape(
        frame_count, tile_rows, grid_width, model_dim
    )
    padded = extended(decoder_in, (("space", 1),), 1)
    padded = jnp.pad(padded, ((0, 0), (0, 0), (1, 1), (0, 0)))
    convolved = jnp.zeros((frame_count, tile_rows, grid_width, dec_conv.shape[3]), jnp.float32)
    for row_shift in range(3):
        for col_shift in range(3):
            window = padded[
                :, row_shift : row_shift + tile_rows, col_shift : col_shift + grid_width, :
            ]
            convolved = convolved + jnp.dot(
                window, dec_conv[row_shift, col_shift], preferred_element_type=jnp.float32
            )
    mapped = jax.nn.gelu(convolved).astype(jnp.bfloat16)
    pixels = jnp.dot(mapped, dec_up, preferred_element_type=jnp.float32).reshape(
        frame_count, tile_rows, grid_width, UP, UP
    )
    return pixels.transpose(0, 1, 3, 2, 4).reshape(frame_count, tile_rows * UP, grid_width * UP)


def solution(mesh):
    return jax.shard_map(
        shards,
        mesh=mesh,
        in_specs=(
            P("tm", "space", None, None),
            P("space", None),
            P(),
            P(),
            P(),
            P(),
            P(),
            P(),
            P(),
            P("tm", None),
            P(),
            P(),
        ),
        out_specs=P("tm", "space", None),
        check_vma=False,
    )
```

profile of v0, /device:TPU:0, one launch (start us, length us, event | category | flops | bytes accessed | tf_op | source)
XLA Modules:
  0.0 144.1 jit_solution(12451911346946646110)
XLA Ops:
  7.7 1.1 fusion.10
  8.8 2.0 %all_gather.16 = bf16[1,64,256]{2,1,0:T(8,128)(2,1)S(1)} all-gather(bf16[1,32,256]{2,1,0:T(8,128)(2,1)S(1)} %get-tuple-element.157), channel_id=1, replica_groups=mesh['tm'=16,'space'=2] {'space'}, dimensions={1}, use_global_device_ids=true | all-gather | bytes 49152 | tf_op jit(solution)/shard_map/all_gather | solution.py:133
  10.9 1.1 convolution_convert_fusion.2
  12.4 1.8 %all_gather.17 = bf16[1,64,256]{2,1,0:T(8,128)(2,1)S(1)} all-gather(bf16[1,32,256]{2,1,0:T(8,128)(2,1)S(1)} %get-tuple-element.158), channel_id=1, replica_groups=mesh['tm'=16,'space'=2] {'space'}, dimensions={1}, use_global_device_ids=true | all-gather | bytes 49152 | tf_op jit(solution)/shard_map/all_gather | solution.py:134
  14.5 1.2 multiply_reduce_fusion
  18.1 1.1 fusion.1
  19.3 10.5 %reduce-scatter.2.cloned.1.call-done = f32[1,4,128,128]{3,2,1,0:T(8,128)} async-done(((f32[1,8,128,128]{3,2,1,0:T(8,128)}), f32[1,4,128,128]{3,2,1,0:T(8,128)}) %reduce-scatter.2.cloned.1.call-update) | async-done | bytes 262160 | tf_op jit(solution)/shard_map/reduce_scatter | solution.py:166
  29.9 1.7 %broadcast_add_fusion = f32[1,4,128,128]{3,2,1,0:T(8,128)} fusion(f32[1,4,128,128]{3,2,1,0:T(8,128)} %reduce-scatter.2.cloned.1.call-done, f32[4]{0:T(128)S(1)} %get-tuple-element.153), kind=kLoop, calls=%fused_computation.51 | loop fusion | flops 65536 | bytes 524304 | tf_op jit(solution)/shard_map/add | solution.py:89
  31.7 40.8 %all-gather.1 = f32[16,1,4]{2,1,0:T(1,128)S(1)} all-gather(f32[1,1,4]{2,1,0:T(1,128)S(1)} %fusion.74), channel_id=1, replica_groups=mesh['tm'=16,'space'=2] {'tm'}, dimensions={0}, use_global_device_ids=true | all-gather | bytes 272 | tf_op jit(solution)/shard_map/all_gather | solution.py:17
  72.5 36.8 %all-gather.4.cloned.1.call-done = f32[16,4,128,128]{3,2,1,0:T(8,128)} async-done(((f32[1,4,128,128]{3,2,1,0:T(8,128)}), f32[16,4,128,128]{3,2,1,0:T(8,128)}) %all-gather.4.cloned.1.call-update) | async-done | bytes 4194320 | tf_op jit(solution)/shard_map/all_gather | solution.py:17
  109.4 17.5 %while.14 = (s32[]{:T(128)}, f32[4,128,128]{2,1,0:T(8,128)S(1)}, s32[]{:T(128)}, f32[16,4]{1,0:T(8,128)S(1)}, f32[16,4,128,128]{3,2,1,0:T(8,128)}, /*index=5*/s32[]{:T(128)}, s32[]{:T(128)}) while((s32[]{:T(128)}, f32[4,128,128]{2,1,0:T(8,128)S(1)}, s32[]{:T(128)}, f32[16,4]{1,0:T(8,128)S(1)}, f32[16,4,128,128]{3,2,1,0:T(8,128)}, ...), condition=%wide.region_7.8_spmd.clone, body=%wide.region_6.7_spmd.clone.sunk | while | flops 262148 | bytes 786585 | solution.py:27
  109.4 1.1 fusion.105
  110.5 1.1 fusion.105
  111.6 1.1 fusion.105
  114.9 1.1 fusion.105
  115.9 1.1 fusion.105
  117.0 1.1 fusion.105
  120.3 1.1 fusion.105
  121.4 1.1 fusion.105
  124.7 1.1 fusion.105
  126.9 2.0 %all-gather = bf16[8,128,128]{2,1,0:T(8,128)(2,1)S(1)} all-gather(bf16[4,128,128]{2,1,0:T(8,128)(2,1)S(1)} %multiply_convert_fusion), channel_id=2, replica_groups=mesh['tm'=16,'space'=2] {'space'}, dimensions={0}, use_global_device_ids=true | all-gather | bytes 393216 | tf_op jit(solution)/shard_map/all_gather | solution.py:172
  129.6 2.0 %collective-permute-start = (bf16[1,1,64,256]{3,2,1,0:T(8,128)(2,1)S(1)}, bf16[1,1,64,256]{3,2,1,0:T(8,128)(2,1)S(1)}, u32[]{:S(2)}, u32[]{:S(2)}) collective-permute-start(bf16[1,1,64,256]{3,2,1,0:T(8,128)(2,1)S(1)} %get-tuple-element.155), channel_id=1, source_target_pairs={{0,1},{2,3},{4,5},{6,7},{8,9},{10,11},{12,13},{14,15},{16,17},{18,... | collective-permute-start | bytes 98312 | tf_op jit(solution)/shard_map/ppermute | solution.py:38
  131.6 1.3 collective-permute-start.1
  133.0 1.8 %collective-permute-done.1 = bf16[1,1,64,256]{3,2,1,0:T(8,128)(2,1)S(1)} collective-permute-done((bf16[1,1,64,256]{3,2,1,0:T(8,128)(2,1)S(1)}, bf16[1,1,64,256]{3,2,1,0:T(8,128)(2,1)S(1)}, u32[]{:S(2)}, u32[]{:S(2)}) %collective-permute-start.1) | collective-permute-done | bytes 32800 | tf_op jit(solution)/shard_map/ppermute | solution.py:40
  (78 shorter events, 15.1 us)
Async XLA Ops:
  6.5 10.8 %copy-start = (bf16[256,1024]{1,0:T(8,128)(2,1)S(1)}, bf16[256,1024]{1,0:T(8,128)(2,1)}, u32[]{:S(2)}) copy-start(bf16[256,1024]{1,0:T(8,128)(2,1)} %param.20) | copy-start | bytes 1572868
  6.5 11.0 %copy-start.5 = (f32[4,256]{1,0:T(4,128)S(1)}, f32[4,256]{1,0:T(4,128)}, u32[]{:S(2)}) copy-start(f32[4,256]{1,0:T(4,128)} %param.16) | copy-start | bytes 12292
  6.5 11.3 %copy-start.2 = (bf16[256,1024]{1,0:T(8,128)(2,1)S(1)}, bf16[256,1024]{1,0:T(8,128)(2,1)}, u32[]{:S(2)}) copy-start(bf16[256,1024]{1,0:T(8,128)(2,1)} %param.21) | copy-start | bytes 1572868
  6.5 12.7 %copy-start.4 = (f32[1,8]{1,0:T(1,128)S(1)}, f32[1,8]{1,0:T(1,128)}, u32[]{:S(2)}) copy-start(f32[1,8]{1,0:T(1,128)} %param.23) | copy-start | bytes 100
  6.5 23.3 %reduce-scatter.2.cloned.1.call-start = ((), (), s32[]{:S(2)}) async-start(), calls=%async_computation.1 | async-start | bytes 786432 | tf_op jit(solution)/shard_map/reduce_scatter | solution.py:166
  18.1 111.2 %copy-start.1 = (bf16[1024,256]{1,0:T(8,128)(2,1)S(1)}, bf16[1024,256]{1,0:T(8,128)(2,1)}, u32[]{:S(2)}) copy-start(bf16[1024,256]{1,0:T(8,128)(2,1)} %param.22) | copy-start | bytes 1572868
  19.2 115.6 %copy-start.3 = (bf16[3,3,256,64]{2,3,1,0:T(8,128)(2,1)S(1)}, bf16[3,3,256,64]{2,3,1,0:T(8,128)(2,1)}, u32[]{:S(2)}) copy-start(bf16[3,3,256,64]{2,3,1,0:T(8,128)(2,1)} %param.24) | copy-start | bytes 884740
  19.2 90.2 %all-gather.4.cloned.1.call-start = ((), (), s32[]{:S(2)}) async-start(), calls=%async_computation.2 | async-start | bytes 4456448 | tf_op jit(solution)/shard_map/all_gather | solution.py:17
  109.4 26.6 %copy-start.6 = (bf16[64,16]{0,1:T(8,128)(2,1)S(1)}, bf16[64,16]{0,1:T(8,128)(2,1)}, u32[]{:S(2)}) copy-start(bf16[64,16]{0,1:T(8,128)(2,1)} %param.25) | copy-start | bytes 6148
  129.6 3.4 %collective-permute-start = (bf16[1,1,64,256]{3,2,1,0:T(8,128)(2,1)S(1)}, bf16[1,1,64,256]{3,2,1,0:T(8,128)(2,1)S(1)}, u32[]{:S(2)}, u32[]{:S(2)}) collective-permute-start(bf16[1,1,64,256]{3,2,1,0:T(8,128)(2,1)S(1)} %get-tuple-element.155), channel_id=1, source_target_pairs={{0,1},{2,3},{4,5},{6,7},{8,9},{10,11},{12,13},{14,15},{16,17},{18,... | collective-permute-start | bytes 98312 | tf_op jit(solution)/shard_map/ppermute | solution.py:38
  131.6 3.1 %collective-permute-start.1 = (bf16[1,1,64,256]{3,2,1,0:T(8,128)(2,1)S(1)}, bf16[1,1,64,256]{3,2,1,0:T(8,128)(2,1)S(1)}, u32[]{:S(2)}, u32[]{:S(2)}) collective-permute-start(bf16[1,1,64,256]{3,2,1,0:T(8,128)(2,1)S(1)} %get-tuple-element.156), channel_id=1, source_target_pairs={{1,0},{3,2},{5,4},{7,6},{9,8},{11,10},{13,12},{15,14},{17,16},{19,... | collective-permute-start | bytes 98312 | tf_op jit(solution)/shard_map/ppermute | solution.py:40
Sparse Core Ops, SparseCore 0:
  19.3 10.5 reduce-scatter.1
  32.6 76.6 all-gather.3
where the time goes:
time: 145 us; the launch traced here: 144 us
  waiting for transfers between devices  49.2 us (34%)
  blocking collectives  46.6 us (32%)
  other arithmetic  20.6 us (14%)
  between operations  13.7 us (9%)
  matrix products  7.67 us (5%)
  starting transfers between devices  3.42 us (2%)
  local copies, waits for them, and re-layouts  2.35 us (2%)
    all_gather x1, blocking collectives, entering(): everything = jax.tree.map(lambda part: lax.all_gather(part, axis), x)  40.8 us
    all_gather x1, waiting for transfers between devices, entering(): everything = jax.tree.map(lambda part: lax.all_gather(part, axis), x)  36.8 us
    select_n x16, other arithmetic, hop(): return jax.tree.map(lambda a, b: jnp.where(reached, a, b), new, before)  16.8 us
    reduce_scatter x1, waiting for transfers between devices, shards(): lax.psum_scatter(partial_value, 'space', scatter_dimension=1, tiled=True)  10.5 us
  transfers between devices with their start and end apart: 4, of which 3 were waited for; matrix products, arithmetic and copies ran while one was open for 0% of the time, Pallas kernels for 0%

commit v1 on v0

v1 whole, which is shorter than its diff:
```python
import functools

import jax
import jax.numpy as jnp
import numpy as np
from jax import lax
from jax.experimental import pallas as pl
from jax.experimental.pallas import tpu as pltpu
from jax.sharding import PartitionSpec as P

ENC_HEADS = 8
UP = 4
LANES = 128
EPSILON = 1e-06
F32 = jnp.float32
BF16 = jnp.bfloat16
VMEM = pl.BlockSpec(memory_space=pltpu.VMEM)


def dot(a, b):
    return jnp.dot(a, b, preferred_element_type=F32)


def dot_on(a, b, dim_a, dim_b, precision=None):
    return lax.dot_general(
        a, b, (((dim_a,), (dim_b,)), ((), ())), precision=precision, preferred_element_type=F32
    )


def call(body, outs, scratch=()):
    return pl.pallas_call(
        body,
        out_shape=outs,
        out_specs=jax.tree.map(lambda _: VMEM, outs),
        scratch_shapes=scratch,
    )


def carry_rows(share):
    return -(-3 * share // 16) * 16


def write_payload(pay_ref, totals, product, share, key_dim):
    for h in range(share):
        rows = slice(h * key_dim, (h + 1) * key_dim)
        pay_ref[rows, :] = totals[h].astype(BF16)
    high = product.astype(BF16)
    rest = product - high.astype(F32)
    mid = rest.astype(BF16)
    low = (rest - mid.astype(F32)).astype(BF16)
    tail = carry_rows(share)
    parts = [high.astype(F32), mid.astype(F32), low.astype(F32)]
    if tail > 3 * share:
        parts.append(jnp.zeros((tail - 3 * share, product.shape[1]), F32))
    pay_ref[share * key_dim :, :] = jnp.concatenate(parts, axis=0).astype(BF16)


def encode_body(
    width,
    tile_tok,
    share,
    x_ref,
    label_ref,
    table_ref,
    pool_ref,
    qkv_ref,
    out_ref,
    gain_ref,
    key_ref,
    value_ref,
    decay_ref,
    window_ref,
    state_ref,
    pay_ref,
    padded,
):
    tokens, dim = x_ref.shape
    size = dim // ENC_HEADS
    place = lax.axis_index("space")
    x = x_ref[...]
    pooled = dot(pool_ref[...], x).astype(BF16)
    pair = dot(pooled, qkv_ref[:, dim:]).astype(BF16)
    queries = dot(x, qkv_ref[:, :dim]).astype(BF16)
    count = pooled.shape[0]
    lane = lax.broadcasted_iota(jnp.int32, (count, dim), 1)
    masks = [(lane >= h * size) & (lane < (h + 1) * size) for h in range(ENC_HEADS)]
    zero = jnp.zeros((count, dim), BF16)
    keys = jnp.concatenate([jnp.where(m, pair[:, :dim], zero) for m in masks], axis=0)
    values = jnp.concatenate([jnp.where(m, pair[:, dim:], zero) for m in masks], axis=0)
    scores = (dot_on(keys, queries, 1, 1) * size ** (-0.5)).reshape(ENC_HEADS, count, tokens)
    weights = jnp.exp(scores - jnp.max(scores, axis=1, keepdims=True))
    totals = jnp.sum(weights, axis=1, keepdims=True)
    rounded = weights.astype(BF16).reshape(ENC_HEADS * count, tokens)
    summed = dot_on(values, rounded, 0, 0).reshape(ENC_HEADS, size, tokens)
    attended = (summed / totals).reshape(dim, tokens).astype(BF16)
    hidden = x.astype(F32) + dot_on(attended, out_ref[...], 0, 0)
    scale = lax.rsqrt(jnp.mean(hidden * hidden, axis=-1, keepdims=True) + EPSILON)
    encoded = (hidden * scale * gain_ref[...]).astype(BF16)
    edge = jnp.zeros((width, dim), BF16)
    padded[:width, :] = edge
    padded[width : width + tokens, :] = encoded
    padded[width + tokens :, :] = edge
    start = pl.multiple_of(place * tile_tok, width)
    window_ref[...] = padded[pl.ds(start, tile_tok + 2 * width), :]

    flag = (lax.axis_index("tm") == 0).astype(F32)
    kinds = table_ref.shape[0]
    kind = lax.broadcasted_iota(jnp.int32, (kinds, tokens), 0)
    one_hot = (jnp.broadcast_to(label_ref[...], (kinds, tokens)) == kind).astype(F32)
    label_rows = dot_on(one_hot, table_ref[...], 0, 0, lax.Precision.HIGHEST)
    memory_in = (encoded.astype(F32) + flag * label_rows).astype(BF16)
    cols = key_ref.shape[1] // lax.axis_size("space")
    val_cols = value_ref.shape[1] // lax.axis_size("space")
    key_start = pl.multiple_of(place * cols, LANES)
    val_start = pl.multiple_of(place * val_cols, LANES)
    own_keys = dot(encoded, key_ref[:, pl.ds(key_start, cols)]).astype(BF16)
    own_values = dot(memory_in, value_ref[:, pl.ds(val_start, val_cols)]).astype(BF16)
    key_dim, val_dim = cols // share, val_cols // share
    states = []
    for h in range(share):
        state = dot_on(
            own_keys[:, h * key_dim : (h + 1) * key_dim],
            own_values[:, h * val_dim : (h + 1) * val_dim],
            0,
            0,
        ) * tokens ** (-0.5)
        state_ref[h * key_dim : (h + 1) * key_dim, :] = state
        states.append(state)
    write_payload(pay_ref, states, decay_ref[...], share, key_dim)


def combine_body(bit, share, first, last, recv_ref, total_ref, product_ref, *refs):
    if first:
        rate_ref = product_ref
        outs = refs
    else:
        reach_ref, prefix_ref = refs[:2]
        outs = refs[2:]
    rows = total_ref.shape[0]
    key_dim = rows // share
    upper = (lax.axis_index("tm") >> bit) & 1
    is_upper = jnp.full(product_ref.shape, upper, jnp.int32) == 1
    product = product_ref[...]
    reach = product if first else reach_ref[...]
    tail = recv_ref[rows:, :].astype(F32)
    got = tail[:share] + tail[share : 2 * share] + tail[2 * share : 3 * share]
    ones = jnp.ones_like(product)
    on_got = jnp.where(is_upper, product, ones)
    on_own = jnp.where(is_upper, ones, got)
    on_prefix = jnp.where(is_upper, reach, jnp.zeros_like(product))
    totals = []
    for h in range(share):
        part = slice(h * key_dim, (h + 1) * key_dim)
        arrived = recv_ref[part, :].astype(F32)
        prefix = on_prefix[h : h + 1] * arrived
        if not first:
            prefix = prefix + prefix_ref[part, :]
        if last:
            outs[0][part, :] = prefix.astype(BF16)
        else:
            outs[3][part, :] = prefix
            total = on_got[h : h + 1] * arrived + on_own[h : h + 1] * total_ref[part, :]
            totals.append(total)
            outs[0][part, :] = total
    if not last:
        joined = product * got
        outs[1][...] = joined
        outs[2][...] = jnp.where(is_upper, reach * got, reach)
        write_payload(outs[4], totals, joined, share, key_dim)


def keys_body(window_ref, key_ref, out_ref):
    out_ref[...] = dot(window_ref[...], key_ref[...]).astype(BF16)


def decode_body(
    width, heads, key_ref, window_ref, memory_ref, read_ref, conv_ref, up_ref, spread_ref, out_ref
):
    rows, dim = window_ref.shape
    tile_tok = rows - 2 * width
    key_dim = key_ref.shape[1] // heads
    reads = [
        (
            dot(
                key_ref[:, h * key_dim : (h + 1) * key_dim],
                memory_ref[h * key_dim : (h + 1) * key_dim, :],
            )
            * key_dim ** (-0.5)
        ).astype(BF16)
        for h in range(heads)
    ]
    readout = jnp.concatenate(reads, axis=1)
    joined = (window_ref[...].astype(F32) + dot(readout, read_ref[...])).astype(BF16)
    columns = []
    for b in range(3):
        total = dot(joined[:tile_tok], conv_ref[0, b])
        for a in range(1, 3):
            total = total + dot(joined[a * width : a * width + tile_tok], conv_ref[a, b])
        columns.append(total)
    col = lax.broadcasted_iota(jnp.int32, columns[0].shape, 0) % width
    zero = jnp.zeros_like(columns[0])
    left = jnp.where(col == 0, zero, pltpu.roll(columns[0], 1, 0))
    right = jnp.where(col == width - 1, zero, pltpu.roll(columns[2], tile_tok - 1, 0))
    mapped = jax.nn.gelu(left + columns[1] + right).astype(BF16)
    wide = width * UP
    lane = lax.broadcasted_iota(jnp.int32, (UP, UP, wide), 2)
    sub = lax.broadcasted_iota(jnp.int32, (UP, UP, wide), 1)
    chosen = (lane % UP) == sub
    for i in range(tile_tok // width):
        hidden = dot(spread_ref[...], mapped[i * width : (i + 1) * width]).astype(BF16)
        pixels = dot_on(up_ref[...], hidden, 0, 1).reshape(UP, UP, wide)
        picked = jnp.sum(jnp.where(chosen, pixels, jnp.zeros_like(pixels)), axis=1)
        out_ref[i * UP : (i + 1) * UP, :] = picked


def shards(
    frames_feat,
    prompt_labels,
    label_table,
    enc_qkv,
    enc_out,
    norm_gain,
    key_proj,
    value_proj,
    read_proj,
    decay,
    dec_conv,
    dec_up,
):
    _, tile_rows, width, dim = frames_feat.shape
    tile_tok = tile_rows * width
    bands, frames = lax.axis_size("space"), lax.axis_size("tm")
    tokens = tile_tok * bands
    heads = decay.shape[1]
    share = heads // bands
    key_dim, val_dim = key_proj.shape[1] // heads, value_proj.shape[1] // heads
    rows = share * key_dim
    window_rows = tile_tok + 2 * width
    sds = jax.ShapeDtypeStruct

    flat = frames_feat.reshape(tile_tok, dim)
    frame = lax.all_gather(flat, "space", axis=0, tiled=True)
    labels = lax.all_gather(prompt_labels.reshape(1, tile_tok), "space", axis=1, tiled=True)
    rate = lax.dynamic_slice_in_dim(decay, lax.axis_index("space") * share, share, 1)
    rate = jnp.broadcast_to(rate.reshape(share, 1), (share, val_dim))

    token = np.arange(tokens)
    cell = (token // width // 2) * (width // 2) + token % width // 2
    pool = jnp.asarray((cell[None, :] == np.arange(tokens // 4)[:, None]) * 0.25, BF16)
    wide = np.arange(width * UP)
    spread = jnp.asarray((wide[:, None] // UP) == np.arange(width)[None, :], BF16)

    pay = sds((rows + carry_rows(share), val_dim), BF16)
    state = sds((rows, val_dim), F32)
    small = sds((share, val_dim), F32)
    window, total, payload = call(
        functools.partial(encode_body, width, tile_tok, share),
        (sds((window_rows, dim), BF16), state, pay),
        (pltpu.VMEM((tokens + 2 * width, dim), BF16),),
    )(
        frame,
        labels,
        label_table,
        pool,
        enc_qkv,
        enc_out,
        norm_gain.reshape(1, dim),
        key_proj,
        value_proj,
        rate,
    )
    product, carried = rate, ()
    steps = (frames - 1).bit_length()
    key_rows = None
    for bit in range(steps):
        first, last = bit == 0, bit == steps - 1
        pairs = [(i, i ^ (1 << bit)) for i in range(frames) if i ^ (1 << bit) < frames]
        arrived = lax.ppermute(payload, "tm", pairs)
        if first:
            key_rows = call(keys_body, sds((window_rows, heads * key_dim), BF16))(window, key_proj)
        body = functools.partial(combine_body, bit, share, first, last)
        if last:
            memory = call(body, sds((rows, val_dim), BF16))(arrived, total, product, *carried)
        else:
            total, product, reach, prefix, payload = call(body, (state, small, small, state, pay))(
                arrived, total, product, *carried
            )
            carried = (reach, prefix)
    memory = lax.all_gather(memory, "space", axis=0, tiled=True)
    logits = call(
        functools.partial(decode_body, width, heads),
        sds((tile_rows * UP, width * UP), F32),
    )(key_rows, window, memory, read_proj, dec_conv, dec_up, spread)
    return logits[None]


def solution(mesh):
    return jax.shard_map(
        shards,
        mesh=mesh,
        in_specs=(
            P("tm", "space", None, None),
            P("space", None),
            P(),
            P(),
            P(),
            P(),
            P(),
            P(),
            P(),
            P("tm", None),
            P(),
            P(),
        ),
        out_specs=P("tm", "space", None),
        check_vma=False,
    )
```

time: 145 us -> 53.6 us (0.37)
  blocking collectives: 46.6 us -> 9.14 us
  waiting for transfers between devices: 49.2 us -> 12.5 us
  other arithmetic: 20.6 us -> 0 us
  Pallas kernels: 0 us -> 17.2 us
  between operations: 13.7 us -> 0.02 us
  matrix products: 7.67 us -> 0 us
  starting transfers between devices: 3.42 us -> 8.53 us
  local copies, waits for them, and re-layouts: 2.35 us -> 5.86 us
    all_gather x4 -> x3, blocking collectives: 46.6 us -> 9.14 us  [the longest x1 3.53 us: shards(): frame = lax.all_gather(flat, 'space', axis=0, tiled=True)]
    all_gather x1 -> x0, waiting for transfers between devices: 36.8 us -> none  [entering(): everything = jax.tree.map(lambda part: lax.all_gather(part, axis), x)]
    pallas_call x0 -> x7, Pallas kernels: none -> 17.2 us  [the longest x3 5.89 us: shards(): call(body, (state, small, small, state, pay))]
    select_n x16 -> x0, other arithmetic: 16.8 us -> none  [hop(): return jax.tree.map(lambda a, b: jnp.where(reached, a, b), new, before)]
    ppermute x2 -> x4, waiting for transfers between devices: 1.79 us -> 12.5 us  [shards(): arrived = lax.ppermute(payload, 'tm', pairs)]
    reduce_scatter x1 -> x0, waiting for transfers between devices: 10.5 us -> none  [shards(): lax.psum_scatter(partial_value, 'space', scatter_dimension=1, tiled=True)]
    dot_general x20 -> x0, matrix products: 7.67 us -> none  [the longest x1 1.19 us: shards(): jnp.dot(attended, enc_out, preferred_element_type=jnp.float32)]
    ppermute x2 -> x4, starting transfers between devices: 3.34 us -> 8.53 us  [shards(): arrived = lax.ppermute(payload, 'tm', pairs)]
  transfers between devices with their start and end apart: 4 -> 4, of which waited for: 3 -> 4; matrix products, arithmetic and copies ran while one was open for 0% -> 3% of each run, Pallas kernels for 0% -> 4%
where the time goes in v1:
time: 53.6 us; the launch traced here: 53.3 us
  Pallas kernels  17.2 us (32%)
  waiting for transfers between devices  12.5 us (23%)
  blocking collectives  9.14 us (17%)
  starting transfers between devices  8.53 us (16%)
  local copies, waits for them, and re-layouts  5.86 us (11%)
    ppermute x4, waiting for transfers between devices, shards(): arrived = lax.ppermute(payload, 'tm', pairs)  12.5 us
    ppermute x4, starting transfers between devices, shards(): arrived = lax.ppermute(payload, 'tm', pairs)  8.53 us
    pallas_call x3, Pallas kernels, shards(): call(body, (state, small, small, state, pay))  5.89 us
    unnamed x18, local copies, waits for them, and re-layouts  5.05 us
    pallas_call x1, Pallas kernels, shards(): call(functools.partial(encode_body, width, tile_tok, share), (sds((window...  3.91 us
    all_gather x1, blocking collectives, shards(): frame = lax.all_gather(flat, 'space', axis=0, tiled=True)  3.53 us
    all_gather x1, blocking collectives, shards(): memory = lax.all_gather(memory, 'space', axis=0, tiled=True)  3.53 us
    pallas_call x1, Pallas kernels, shards(): call(functools.partial(decode_body, width, heads), sds((tile_rows * UP, w...  3.4 us
  transfers between devices with their start and end apart: 4, of which 4 were waited for; matrix products, arithmetic and copies ran while one was open for 3% of the time, Pallas kernels for 4%

profile of v1, /device:TPU:0, one launch (start us, length us, event | category | flops | bytes accessed | tf_op | source)
XLA Modules:
  0.0 53.3 jit_solution(12334486814420440765)
XLA Ops:
  0.0 0.7 %copy-done.7 = s32[2,64]{1,0:T(2,128)S(1)} copy-done((s32[2,64]{1,0:T(2,128)S(1)}, s32[2,64]{1,0:T(2,128)}, u32[]{:S(2)}) %copy-start.7) | copy-done | bytes 536
  0.8 2.1 %all_gather.10.label_ref = s32[1,256]{1,0:T(1,128)} all-gather(s32[1,128]{1,0:T(1,128)S(1)} %reshape.12), channel_id=1, replica_groups=mesh['tm'=16,'space'=2] {'space'}, dimensions={1}, use_global_device_ids=true | all-gather | bytes 1536 | tf_op jit(solution)/shard_map/all_gather | solution.py:243
  2.9 3.5 %all_gather.9.x_ref = bf16[256,256]{1,0:T(8,128)(2,1)} all-gather(bf16[128,256]{1,0:T(8,128)(2,1)} %bitcast.5), channel_id=1, replica_groups=mesh['tm'=16,'space'=2] {'space'}, dimensions={0}, use_global_device_ids=true | all-gather | bytes 196608 | tf_op jit(solution)/shard_map/all_gather | solution.py:242
  6.5 0.7 %broadcast_in_dim.11.decay_ref.product_ref = f32[4,128]{1,0:T(4,128)} broadcast(f32[4]{0:T(128)S(1)} %dynamic-slice_bitcast_fusion), dimensions={0} | broadcast | bytes 2064 | tf_op jit(solution)/shard_map/broadcast_in_dim | solution.py:245
  7.1 3.9 %shard_map.136 = (bf16[256,256]{1,0:T(8,128)(2,1)}, f32[512,128]{1,0:T(8,128)}, bf16[528,128]{1,0:T(8,128)(2,1)}) custom-call(bf16[256,256]{1,0:T(8,128)(2,1)} %all_gather.9.x_ref, s32[1,256]{1,0:T(1,128)} %all_gather.10.label_ref, f32[4,256]{1,0:T(4,128)} %table_ref.1, bf16[64,256]{1,0:T(8,128)(2,1)} %constant.14.clone.pool_ref, bf16[256,768]{1,0:T(8,128)(2,1)} %qkv_ref.1, ...), custom_call_target="tpu_custom_call" | custom-call | tf_op jit(solution)/shard_map/pallas_call | solution.py:256
  11.0 2.5 %collective-permute-start = (bf16[528,128]{1,0:T(8,128)(2,1)}, bf16[528,128]{1,0:T(8,128)(2,1)S(1)}, u32[]{:S(2)}, u32[]{:S(2)}) collective-permute-start(bf16[528,128]{1,0:T(8,128)(2,1)} %get-tuple-element.24), channel_id=1, source_target_pairs={{0,2},{2,0},{4,6},{6,4},{8,10},{10,8},{12,14},{14,12},{16,18},{18,... | collective-permute-start | bytes 405512 | tf_op jit(solution)/shard_map/ppermute | solution.py:278
  13.5 4.3 %collective-permute-done.recv_ref = bf16[528,128]{1,0:T(8,128)(2,1)S(1)} collective-permute-done((bf16[528,128]{1,0:T(8,128)(2,1)}, bf16[528,128]{1,0:T(8,128)(2,1)S(1)}, u32[]{:S(2)}, u32[]{:S(2)}) %collective-permute-start) | collective-permute-done | bytes 135200 | tf_op jit(solution)/shard_map/ppermute | solution.py:278
  17.8 0.6 %copy-done.2 = bf16[528,128]{1,0:T(8,128)(2,1)} copy-done((bf16[528,128]{1,0:T(8,128)(2,1)}, bf16[528,128]{1,0:T(8,128)(2,1)S(1)}, u32[]{:S(2)}) %copy-start.2) | copy-done | bytes 135192
  18.5 1.9 %shard_map.138 = (f32[512,128]{1,0:T(8,128)}, f32[4,128]{1,0:T(4,128)}, f32[4,128]{1,0:T(4,128)}, f32[512,128]{1,0:T(8,128)}, bf16[528,128]{1,0:T(8,128)(2,1)}) custom-call(bf16[528,128]{1,0:T(8,128)(2,1)} %copy-done.2, f32[512,128]{1,0:T(8,128)} %get-tuple-element.25.total_ref, f32[4,128]{1,0:T(4,128)} %broadcast_in_dim.11.decay_ref.product_ref), custom_call_target="tpu_custom_call" | custom-call | tf_op jit(solution)/shard_map/pallas_call | solution.py:285
  20.3 1.8 %collective-permute-start.1 = (bf16[528,128]{1,0:T(8,128)(2,1)}, bf16[528,128]{1,0:T(8,128)(2,1)S(1)}, u32[]{:S(2)}, u32[]{:S(2)}) collective-permute-start(bf16[528,128]{1,0:T(8,128)(2,1)} %get-tuple-element.26), channel_id=1, source_target_pairs={{0,4},{2,6},{4,0},{6,2},{8,12},{10,14},{12,8},{14,10},{16,20},{18,... | collective-permute-start | bytes 405512 | tf_op jit(solution)/shard_map/ppermute | solution.py:278
  22.1 3.7 %collective-permute-done.1.recv_ref = bf16[528,128]{1,0:T(8,128)(2,1)S(1)} collective-permute-done((bf16[528,128]{1,0:T(8,128)(2,1)}, bf16[528,128]{1,0:T(8,128)(2,1)S(1)}, u32[]{:S(2)}, u32[]{:S(2)}) %collective-permute-start.1) | collective-permute-done | bytes 135200 | tf_op jit(solution)/shard_map/ppermute | solution.py:278
  26.4 2.0 %shard_map.139 = (f32[512,128]{1,0:T(8,128)}, f32[4,128]{1,0:T(4,128)}, f32[4,128]{1,0:T(4,128)}, f32[512,128]{1,0:T(8,128)}, bf16[528,128]{1,0:T(8,128)(2,1)}) custom-call(bf16[528,128]{1,0:T(8,128)(2,1)} %copy-done.3, f32[512,128]{1,0:T(8,128)} %get-tuple-element.27.total_ref, f32[4,128]{1,0:T(4,128)} %get-tuple-element.28.product_ref, ...), custom_call_target="tpu_custom_call" | custom-call | tf_op jit(solution)/shard_map/pallas_call | solution.py:285
  28.4 1.6 %collective-permute-start.2 = (bf16[528,128]{1,0:T(8,128)(2,1)}, bf16[528,128]{1,0:T(8,128)(2,1)S(1)}, u32[]{:S(2)}, u32[]{:S(2)}) collective-permute-start(bf16[528,128]{1,0:T(8,128)(2,1)} %get-tuple-element.31), channel_id=1, source_target_pairs={{0,8},{2,10},{4,12},{6,14},{8,0},{10,2},{12,4},{14,6},{16,24},{18,... | collective-permute-start | bytes 405512 | tf_op jit(solution)/shard_map/ppermute | solution.py:278
  30.0 3.6 %collective-permute-done.2.recv_ref = bf16[528,128]{1,0:T(8,128)(2,1)S(1)} collective-permute-done((bf16[528,128]{1,0:T(8,128)(2,1)}, bf16[528,128]{1,0:T(8,128)(2,1)S(1)}, u32[]{:S(2)}, u32[]{:S(2)}) %collective-permute-start.2) | collective-permute-done | bytes 135200 | tf_op jit(solution)/shard_map/ppermute | solution.py:278
  33.6 0.7 %copy-done.4 = bf16[528,128]{1,0:T(8,128)(2,1)} copy-done((bf16[528,128]{1,0:T(8,128)(2,1)}, bf16[528,128]{1,0:T(8,128)(2,1)S(1)}, u32[]{:S(2)}) %copy-start.4) | copy-done | bytes 135192
  34.3 2.0 %shard_map.140 = (f32[512,128]{1,0:T(8,128)}, f32[4,128]{1,0:T(4,128)}, f32[4,128]{1,0:T(4,128)}, f32[512,128]{1,0:T(8,128)}, bf16[528,128]{1,0:T(8,128)(2,1)}) custom-call(bf16[528,128]{1,0:T(8,128)(2,1)} %copy-done.4, f32[512,128]{1,0:T(8,128)} %get-tuple-element.32.total_ref, f32[4,128]{1,0:T(4,128)} %get-tuple-element.33.product_ref, ...), custom_call_target="tpu_custom_call" | custom-call | tf_op jit(solution)/shard_map/pallas_call | solution.py:285
  36.3 2.6 %collective-permute-start.3 = (bf16[528,128]{1,0:T(8,128)(2,1)}, bf16[528,128]{1,0:T(8,128)(2,1)S(1)}, u32[]{:S(2)}, u32[]{:S(2)}) collective-permute-start(bf16[528,128]{1,0:T(8,128)(2,1)} %get-tuple-element.36), channel_id=1, source_target_pairs={{0,16},{2,18},{4,20},{6,22},{8,24},{10,26},{12,28},{14,30},{16,0},... | collective-permute-start | bytes 405512 | tf_op jit(solution)/shard_map/ppermute | solution.py:278
  38.9 0.7 %copy.16.up_ref = bf16[64,16]{1,0:T(8,128)(2,1)} copy(bf16[64,16]{0,1:T(8,128)(2,1)S(1)} %copy-done.6) | data formatting | bytes 4096 | tf_op args[11]
  39.6 2.2 %shard_map.137.key_ref = bf16[256,1024]{1,0:T(8,128)(2,1)} custom-call(bf16[256,256]{1,0:T(8,128)(2,1)} %get-tuple-element.23.window_ref, bf16[256,1024]{1,0:T(8,128)(2,1)} %key_ref.3), custom_call_target="tpu_custom_call" | custom-call | tf_op jit(solution)/shard_map/pallas_call | solution.py:280
  41.9 1.1 %copy.15.conv_ref = bf16[3,3,256,64]{3,2,1,0:T(8,128)(2,1)} copy(bf16[3,3,256,64]{2,3,1,0:T(8,128)(2,1)S(1)} %copy-done.1) | data formatting | bytes 589824 | tf_op args[10]
  42.9 0.9 %collective-permute-done.3.recv_ref = bf16[528,128]{1,0:T(8,128)(2,1)S(1)} collective-permute-done((bf16[528,128]{1,0:T(8,128)(2,1)}, bf16[528,128]{1,0:T(8,128)(2,1)S(1)}, u32[]{:S(2)}, u32[]{:S(2)}) %collective-permute-start.3) | collective-permute-done | bytes 135200 | tf_op jit(solution)/shard_map/ppermute | solution.py:278
  44.5 1.8 %shard_map.141 = bf16[512,128]{1,0:T(8,128)(2,1)} custom-call(bf16[528,128]{1,0:T(8,128)(2,1)} %copy-done.5, f32[512,128]{1,0:T(8,128)} %get-tuple-element.37.total_ref, f32[4,128]{1,0:T(4,128)} %get-tuple-element.38.product_ref, f32[4,128]{1,0:T(4,128)} %get-tuple-element.39.refs_0_, f32[512,128]{1,0:T(8,128)} %get-tuple-element.40.refs_1_), custom_call_target="tpu_custom_call" | custom-call | tf_op jit(solution)/shard_map/pallas_call | solution.py:283
  46.3 3.5 %all_gather.11.memory_ref = bf16[1024,128]{1,0:T(8,128)(2,1)} all-gather(bf16[512,128]{1,0:T(8,128)(2,1)} %shard_map.141), channel_id=1, replica_groups=mesh['tm'=16,'space'=2] {'space'}, dimensions={0}, use_global_device_ids=true | all-gather | bytes 393216 | tf_op jit(solution)/shard_map/all_gather | solution.py:289
  49.9 3.4 %shard_map.142 = f32[8,256]{1,0:T(8,128)} custom-call(bf16[256,1024]{1,0:T(8,128)(2,1)} %shard_map.137.key_ref, bf16[256,256]{1,0:T(8,128)(2,1)} %get-tuple-element.23.window_ref, bf16[1024,128]{1,0:T(8,128)(2,1)} %all_gather.11.memory_ref, bf16[1024,256]{1,0:T(8,128)(2,1)} %read_ref.1, bf16[3,3,256,64]{3,2,1,0:T(8,128)(2,1)} %copy.15.conv_ref, ...), custom_call_target="tpu_custom_call" | custom-call | tf_op jit(solution)/shard_map/pallas_call | solution.py:290
  (15 shorter events, 1.5 us)
Async XLA Ops:
  0.0 6.4 %copy-start = (f32[1,8]{1,0:T(1,128)S(1)}, f32[1,8]{1,0:T(1,128)}, u32[]{:S(2)}) copy-start(f32[1,8]{1,0:T(1,128)} %param.23) | copy-start | bytes 100
  0.0 0.7 %copy-start.7 = (s32[2,64]{1,0:T(2,128)S(1)}, s32[2,64]{1,0:T(2,128)}, u32[]{:S(2)}) copy-start(s32[2,64]{1,0:T(2,128)} %param.15) | copy-start | bytes 1540
  11.0 6.8 %collective-permute-start = (bf16[528,128]{1,0:T(8,128)(2,1)}, bf16[528,128]{1,0:T(8,128)(2,1)S(1)}, u32[]{:S(2)}, u32[]{:S(2)}) collective-permute-start(bf16[528,128]{1,0:T(8,128)(2,1)} %get-tuple-element.24), channel_id=1, source_target_pairs={{0,2},{2,0},{4,6},{6,4},{8,10},{10,8},{12,14},{14,12},{16,18},{18,... | collective-permute-start | bytes 405512 | tf_op jit(solution)/shard_map/ppermute | solution.py:278
  17.8 0.7 %copy-start.2 = (bf16[528,128]{1,0:T(8,128)(2,1)}, bf16[528,128]{1,0:T(8,128)(2,1)S(1)}, u32[]{:S(2)}) copy-start(bf16[528,128]{1,0:T(8,128)(2,1)S(1)} %collective-permute-done.recv_ref) | copy-start | bytes 405508
  20.3 5.4 %collective-permute-start.1 = (bf16[528,128]{1,0:T(8,128)(2,1)}, bf16[528,128]{1,0:T(8,128)(2,1)S(1)}, u32[]{:S(2)}, u32[]{:S(2)}) collective-permute-start(bf16[528,128]{1,0:T(8,128)(2,1)} %get-tuple-element.26), channel_id=1, source_target_pairs={{0,4},{2,6},{4,0},{6,2},{8,12},{10,14},{12,8},{14,10},{16,20},{18,... | collective-permute-start | bytes 405512 | tf_op jit(solution)/shard_map/ppermute | solution.py:278
  25.8 0.6 %copy-start.3 = (bf16[528,128]{1,0:T(8,128)(2,1)}, bf16[528,128]{1,0:T(8,128)(2,1)S(1)}, u32[]{:S(2)}) copy-start(bf16[528,128]{1,0:T(8,128)(2,1)S(1)} %collective-permute-done.1.recv_ref) | copy-start | bytes 405508
  28.4 5.2 %collective-permute-start.2 = (bf16[528,128]{1,0:T(8,128)(2,1)}, bf16[528,128]{1,0:T(8,128)(2,1)S(1)}, u32[]{:S(2)}, u32[]{:S(2)}) collective-permute-start(bf16[528,128]{1,0:T(8,128)(2,1)} %get-tuple-element.31), channel_id=1, source_target_pairs={{0,8},{2,10},{4,12},{6,14},{8,0},{10,2},{12,4},{14,6},{16,24},{18,... | collective-permute-start | bytes 405512 | tf_op jit(solution)/shard_map/ppermute | solution.py:278
  33.6 0.7 %copy-start.4 = (bf16[528,128]{1,0:T(8,128)(2,1)}, bf16[528,128]{1,0:T(8,128)(2,1)S(1)}, u32[]{:S(2)}) copy-start(bf16[528,128]{1,0:T(8,128)(2,1)S(1)} %collective-permute-done.2.recv_ref) | copy-start | bytes 405508
  34.3 4.7 %copy-start.6 = (bf16[64,16]{0,1:T(8,128)(2,1)S(1)}, bf16[64,16]{0,1:T(8,128)(2,1)}, u32[]{:S(2)}) copy-start(bf16[64,16]{0,1:T(8,128)(2,1)} %param.25) | copy-start | bytes 6148
  36.3 7.6 %collective-permute-start.3 = (bf16[528,128]{1,0:T(8,128)(2,1)}, bf16[528,128]{1,0:T(8,128)(2,1)S(1)}, u32[]{:S(2)}, u32[]{:S(2)}) collective-permute-start(bf16[528,128]{1,0:T(8,128)(2,1)} %get-tuple-element.36), channel_id=1, source_target_pairs={{0,16},{2,18},{4,20},{6,22},{8,24},{10,26},{12,28},{14,30},{16,0},... | collective-permute-start | bytes 405512 | tf_op jit(solution)/shard_map/ppermute | solution.py:278
  39.6 2.3 %copy-start.1 = (bf16[3,3,256,64]{2,3,1,0:T(8,128)(2,1)S(1)}, bf16[3,3,256,64]{2,3,1,0:T(8,128)(2,1)}, u32[]{:S(2)}) copy-start(bf16[3,3,256,64]{2,3,1,0:T(8,128)(2,1)} %param.24) | copy-start | bytes 884740
  43.9 0.7 %copy-start.5 = (bf16[528,128]{1,0:T(8,128)(2,1)}, bf16[528,128]{1,0:T(8,128)(2,1)S(1)}, u32[]{:S(2)}) copy-start(bf16[528,128]{1,0:T(8,128)(2,1)S(1)} %collective-permute-done.3.recv_ref) | copy-start | bytes 405508

commit v2 on v1

--- a/solution.py
+++ b/solution.py
@@ -27,13 +27,24 @@
     )
 
 
-def call(body, outs, scratch=()):
-    return pl.pallas_call(
-        body,
-        out_shape=outs,
-        out_specs=jax.tree.map(lambda _: VMEM, outs),
-        scratch_shapes=scratch,
-    )
+def call(body, outs, scratch=(), spaces=None):
+    def on_chip(*operands):
+        places = [pltpu.VMEM] * len(operands) if spaces is None else spaces
+        run = pl.pallas_call(
+            body,
+            out_shape=outs,
+            in_specs=[pl.BlockSpec(memory_space=place) for place in places],
+            out_specs=jax.tree.map(lambda _: VMEM, outs),
+            scratch_shapes=scratch,
+        )
+        return run(
+            *[
+                pltpu.with_memory_space_constraint(x, place) if place is pltpu.VMEM else x
+                for x, place in zip(operands, places)
+            ]
+        )
+
+    return on_chip
 
 
 def carry_rows(share):
@@ -55,30 +66,40 @@
     pay_ref[share * key_dim :, :] = jnp.concatenate(parts, axis=0).astype(BF16)
 
 
-def encode_body(
-    width,
-    tile_tok,
-    share,
-    x_ref,
-    label_ref,
-    table_ref,
-    pool_ref,
-    qkv_ref,
-    out_ref,
-    gain_ref,
-    key_ref,
-    value_ref,
-    decay_ref,
-    window_ref,
-    state_ref,
-    pay_ref,
-    padded,
-):
-    tokens, dim = x_ref.shape
+def encode_body(width, share, parts, *refs):
+    tiles, labels = refs[:parts], refs[parts : 2 * parts]
+    table_ref, gain_ref, decay_ref = refs[2 * parts : 2 * parts + 3]
+    pool_hbm, qkv_hbm, out_hbm, key_hbm, value_hbm = refs[2 * parts + 3 : 2 * parts + 8]
+    window_ref, state_ref, product_ref, pay_ref = refs[2 * parts + 8 : 2 * parts + 12]
+    padded, tile_ref, pool_ref, qkv_ref, out_ref, key_ref, value_ref, sems = refs[2 * parts + 12 :]
+    place = lax.axis_index("space")
+    cols, val_cols = key_ref.shape[1], value_ref.shape[1]
+    key_start = pl.multiple_of(place * cols, LANES)
+    val_start = pl.multiple_of(place * val_cols, LANES)
+    loads = [
+        pltpu.make_async_copy(source, target, sems.at[n])
+        for n, (source, target) in enumerate(
+            (
+                (tiles[0], tile_ref),
+                (pool_hbm, pool_ref),
+                (qkv_hbm, qkv_ref),
+                (out_hbm, out_ref),
+                (key_hbm.at[:, pl.ds(key_start, cols)], key_ref),
+                (value_hbm.at[:, pl.ds(val_start, val_cols)], value_ref),
+            )
+        )
+    ]
+    for load in loads:
+        load.start()
+    loads[0].wait()
+    x = jnp.concatenate([tile_ref[...]] + [tile[...] for tile in tiles[1:]], axis=0)
+    tokens, dim = x.shape
     size = dim // ENC_HEADS
-    place = lax.axis_index("space")
-    x = x_ref[...]
+    window_rows = window_ref.shape[0]
+    tile_tok = window_rows - 2 * width
+    loads[1].wait()
     pooled = dot(pool_ref[...], x).astype(BF16)
+    loads[2].wait()
     pair = dot(pooled, qkv_ref[:, dim:]).astype(BF16)
     queries = dot(x, qkv_ref[:, :dim]).astype(BF16)
     count = pooled.shape[0]
@@ -93,28 +114,31 @@
     rounded = weights.astype(BF16).reshape(ENC_HEADS * count, tokens)
     summed = dot_on(values, rounded, 0, 0).reshape(ENC_HEADS, size, tokens)
     attended = (summed / totals).reshape(dim, tokens).astype(BF16)
+    loads[3].wait()
     hidden = x.astype(F32) + dot_on(attended, out_ref[...], 0, 0)
     scale = lax.rsqrt(jnp.mean(hidden * hidden, axis=-1, keepdims=True) + EPSILON)
     encoded = (hidden * scale * gain_ref[...]).astype(BF16)
     edge = jnp.zeros((width, dim), BF16)
     padded[:width, :] = edge
-    padded[width : width + tokens, :] = encoded
     padded[width + tokens :, :] = edge
-    start = pl.multiple_of(place * tile_tok, width)
-    window_ref[...] = padded[pl.ds(start, tile_tok + 2 * width), :]
+    for p in range(parts):
+        spot = place if p == 0 else 1 - place
+        spot = pl.multiple_of(width + spot * tile_tok, width) if parts > 1 else width
+        rows = tokens // parts
+        padded[pl.ds(spot, rows), :] = encoded[p * rows : (p + 1) * rows]
+    window_ref[...] = padded[pl.ds(pl.multiple_of(place * tile_tok, width), window_rows), :]
 
     flag = (lax.axis_index("tm") == 0).astype(F32)
     kinds = table_ref.shape[0]
+    label = jnp.concatenate([ref[...] for ref in labels], axis=1)
     kind = lax.broadcasted_iota(jnp.int32, (kinds, tokens), 0)
-    one_hot = (jnp.broadcast_to(label_ref[...], (kinds, tokens)) == kind).astype(F32)
+    one_hot = (jnp.broadcast_to(label, (kinds, tokens)) == kind).astype(F32)
     label_rows = dot_on(one_hot, table_ref[...], 0, 0, lax.Precision.HIGHEST)
     memory_in = (encoded.astype(F32) + flag * label_rows).astype(BF16)
-    cols = key_ref.shape[1] // lax.axis_size("space")
-    val_cols = value_ref.shape[1] // lax.axis_size("space")
-    key_start = pl.multiple_of(place * cols, LANES)
-    val_start = pl.multiple_of(place * val_cols, LANES)
-    own_keys = dot(encoded, key_ref[:, pl.ds(key_start, cols)]).astype(BF16)
-    own_values = dot(memory_in, value_ref[:, pl.ds(val_start, val_cols)]).astype(BF16)
+    loads[4].wait()
+    own_keys = dot(encoded, key_ref[...]).astype(BF16)
+    loads[5].wait()
+    own_values = dot(memory_in, value_ref[...]).astype(BF16)
     key_dim, val_dim = cols // share, val_cols // share
     states = []
     for h in range(share):
@@ -126,7 +150,11 @@
         ) * tokens ** (-0.5)
         state_ref[h * key_dim : (h + 1) * key_dim, :] = state
         states.append(state)
-    write_payload(pay_ref, states, decay_ref[...], share, key_dim)
+    product = jnp.concatenate(
+        [jnp.full((1, val_dim), decay_ref[0, place * share + h], F32) for h in range(share)], axis=0
+    )
+    product_ref[...] = product
+    write_payload(pay_ref, states, product, share, key_dim)
 
 
 def combine_body(bit, share, first, last, recv_ref, total_ref, product_ref, *refs):
@@ -193,9 +221,11 @@
     joined = (window_ref[...].astype(F32) + dot(readout, read_ref[...])).astype(BF16)
     columns = []
     for b in range(3):
-        total = dot(joined[:tile_tok], conv_ref[0, b])
+        total = dot_on(joined[:tile_tok], conv_ref[0, b], 1, 1)
         for a in range(1, 3):
-            total = total + dot(joined[a * width : a * width + tile_tok], conv_ref[a, b])
+            total = total + dot_on(
+                joined[a * width : a * width + tile_tok], conv_ref[a, b], 1, 1
+            )
         columns.append(total)
     col = lax.broadcasted_iota(jnp.int32, columns[0].shape, 0) % width
     zero = jnp.zeros_like(columns[0])
@@ -208,7 +238,7 @@
     chosen = (lane % UP) == sub
     for i in range(tile_tok // width):
         hidden = dot(spread_ref[...], mapped[i * width : (i + 1) * width]).astype(BF16)
-        pixels = dot_on(up_ref[...], hidden, 0, 1).reshape(UP, UP, wide)
+        pixels = dot_on(up_ref[...], hidden, 1, 1).reshape(UP, UP, wide)
         picked = jnp.sum(jnp.where(chosen, pixels, jnp.zeros_like(pixels)), axis=1)
         out_ref[i * UP : (i + 1) * UP, :] = picked
 
@@ -236,13 +266,17 @@
     key_dim, val_dim = key_proj.shape[1] // heads, value_proj.shape[1] // heads
     rows = share * key_dim
     window_rows = tile_tok + 2 * width
-    sds = jax.ShapeDtypeStruct
+    sds = pltpu.VMEM
 
     flat = frames_feat.reshape(tile_tok, dim)
-    frame = lax.all_gather(flat, "space", axis=0, tiled=True)
-    labels = lax.all_gather(prompt_labels.reshape(1, tile_tok), "space", axis=1, tiled=True)
-    rate = lax.dynamic_slice_in_dim(decay, lax.axis_index("space") * share, share, 1)
-    rate = jnp.broadcast_to(rate.reshape(share, 1), (share, val_dim))
+    labels = prompt_labels.reshape(1, tile_tok)
+    if bands == 2:
+        swap = [(0, 1), (1, 0)]
+        tiles = [flat, lax.ppermute(flat, "space", swap)]
+        marks = [labels, lax.ppermute(labels, "space", swap)]
+    else:
+        tiles = [lax.all_gather(flat, "space", axis=0, tiled=True)]
+        marks = [lax.all_gather(labels, "space", axis=1, tiled=True)]
 
     token = np.arange(tokens)
     cell = (token // width // 2) * (width // 2) + token % width // 2
@@ -253,23 +287,35 @@
     pay = sds((rows + carry_rows(share), val_dim), BF16)
     state = sds((rows, val_dim), F32)
     small = sds((share, val_dim), F32)
-    window, total, payload = call(
-        functools.partial(encode_body, width, tile_tok, share),
-        (sds((window_rows, dim), BF16), state, pay),
-        (pltpu.VMEM((tokens + 2 * width, dim), BF16),),
+    parts = len(tiles)
+    key_cols, val_cols = share * key_dim, share * val_dim
+    window, total, product, payload = call(
+        functools.partial(encode_body, width, share, parts),
+        (sds((window_rows, dim), BF16), state, small, pay),
+        (
+            pltpu.VMEM((tokens + 2 * width, dim), BF16),
+            pltpu.VMEM(tiles[0].shape, BF16),
+            pltpu.VMEM(pool.shape, BF16),
+            pltpu.VMEM(enc_qkv.shape, BF16),
+            pltpu.VMEM(enc_out.shape, BF16),
+            pltpu.VMEM((dim, key_cols), BF16),
+            pltpu.VMEM((dim, val_cols), BF16),
+            pltpu.SemaphoreType.DMA((6,)),
+        ),
+        [pl.ANY] + [pltpu.VMEM] * (2 * parts + 1) + [pltpu.SMEM] + [pl.ANY] * 5,
     )(
-        frame,
-        labels,
+        *tiles,
+        *marks,
         label_table,
+        norm_gain.reshape(1, dim),
+        decay,
         pool,
         enc_qkv,
         enc_out,
-        norm_gain.reshape(1, dim),
         key_proj,
         value_proj,
-        rate,
     )
-    product, carried = rate, ()
+    carried = ()
     steps = (frames - 1).bit_length()
     key_rows = None
     for bit in range(steps):
@@ -289,8 +335,8 @@
     memory = lax.all_gather(memory, "space", axis=0, tiled=True)
     logits = call(
         functools.partial(decode_body, width, heads),
-        sds((tile_rows * UP, width * UP), F32),
-    )(key_rows, window, memory, read_proj, dec_conv, dec_up, spread)
+        jax.ShapeDtypeStruct((tile_rows * UP, width * UP), F32),
+    )(key_rows, window, memory, read_proj, dec_conv.swapaxes(2, 3), dec_up.T, spread)
     return logits[None]
 
 

time: 53.6 us -> 35.5 us (0.66)
  Pallas kernels: 17.2 us -> 6.31 us
  blocking collectives: 9.14 us -> 2.13 us
  local copies, waits for them, and re-layouts: 5.86 us -> 0.79 us
  waiting for transfers between devices: 12.5 us -> 16.5 us
  starting transfers between devices: 8.53 us -> 9.5 us
    pallas_call x7, Pallas kernels: 17.2 us -> 6.31 us  [on_chip(): run(*[pltpu.with_memory_space_constraint(x, place) if place is pltpu.VMEM...]
    all_gather x2 -> x0, blocking collectives: 5.61 us -> none  [the longest x1 3.53 us: shards(): frame = lax.all_gather(flat, 'space', axis=0, tiled=True)]
    unnamed x18 -> x14, local copies, waits for them, and re-layouts: 5.05 us -> 0.03 us
    ppermute x4, waiting for transfers between devices: 12.5 us -> 15.3 us  [shards(): arrived = lax.ppermute(payload, 'tm', pairs)]
    all_gather x1, blocking collectives: 3.53 us -> 2.13 us  [shards(): memory = lax.all_gather(memory, 'space', axis=0, tiled=True)]
    ppermute x0 -> x2, waiting for transfers between devices: none -> 1.15 us  [the longest x1 1.14 us: shards(): marks = [labels, lax.ppermute(labels, 'space', swap)]]
    broadcast_in_dim x2 -> x0, local copies, waits for them, and re-layouts: 0.72 us -> none  [shards(): rate = jnp.broadcast_to(rate.reshape(share, 1), (share, val_dim))]
    reshape x1, local copies, waits for them, and re-layouts: 0.08 us -> 0.76 us  [shards(): labels = prompt_labels.reshape(1, tile_tok)]
  transfers between devices with their start and end apart: 4 -> 6, of which waited for: 4 -> 5; matrix products, arithmetic and copies ran while one was open for 3% -> 2% of each run, Pallas kernels for 4% -> 1%
where the time goes in v2:
time: 35.5 us; the launch traced here: 35.3 us
  waiting for transfers between devices  16.5 us (46%)
  starting transfers between devices  9.5 us (27%)
  Pallas kernels  6.31 us (18%)
  blocking collectives  2.13 us (6%)
  local copies, waits for them, and re-layouts  0.79 us (2%)
    ppermute x4, waiting for transfers between devices, shards(): arrived = lax.ppermute(payload, 'tm', pairs)  15.3 us
    ppermute x4, starting transfers between devices, shards(): arrived = lax.ppermute(payload, 'tm', pairs)  8.99 us
    pallas_call x7, Pallas kernels, on_chip(): run(*[pltpu.with_memory_space_constraint(x, place) if place is pltpu.VMEM...  6.31 us
    all_gather x1, blocking collectives, shards(): memory = lax.all_gather(memory, 'space', axis=0, tiled=True)  2.13 us
    ppermute x1, waiting for transfers between devices, shards(): marks = [labels, lax.ppermute(labels, 'space', swap)]  1.14 us
    reshape x1, local copies, waits for them, and re-layouts, shards(): labels = prompt_labels.reshape(1, tile_tok)  0.76 us
  transfers between devices with their start and end apart: 6, of which 5 were waited for; matrix products, arithmetic and copies ran while one was open for 2% of the time, Pallas kernels for 1%

profile of v2, /device:TPU:0, one launch (start us, length us, event | category | flops | bytes accessed | tf_op | source)
XLA Modules:
  0.0 35.3 jit_solution(7815251166113019555)
XLA Ops:
  0.0 0.5 %collective-permute-start = (bf16[128,256]{1,0:T(8,128)(2,1)}, bf16[128,256]{1,0:T(8,128)(2,1)S(1)}, u32[]{:S(2)}, u32[]{:S(2)}) collective-permute-start(bf16[128,256]{1,0:T(8,128)(2,1)} %bitcast.8), channel_id=1, source_target_pairs={{0,1},{1,0},{2,3},{3,2},{4,5},{5,4},{6,7},{7,6},{8,9},{9,8},{10,11... | collective-permute-start | bytes 196616 | tf_op jit(solution)/shard_map/ppermute | solution.py:275
  0.5 0.8 %reshape.10.refs_2_ = s32[1,128]{1,0:T(1,128)S(1)} reshape(s32[2,64]{1,0:T(2,128)} %param.15) | data formatting | bytes 1024 | tf_op jit(solution)/shard_map/reshape | solution.py:272
  1.3 0.0 collective-permute-start.1
  1.3 1.1 %collective-permute-done.1.refs_3_ = s32[1,128]{1,0:T(1,128)S(1)} collective-permute-done((s32[1,128]{1,0:T(1,128)S(1)}, s32[1,128]{1,0:T(1,128)S(1)}, u32[]{:S(2)}, u32[]{:S(2)}) %collective-permute-start.1) | collective-permute-done | bytes 544 | tf_op jit(solution)/shard_map/ppermute | solution.py:276
  2.4 0.0 collective-permute-done.refs_1_
  2.4 0.0 copy-done.6
  2.4 3.8 %shard_map.136 = (bf16[256,256]{1,0:T(8,128)(2,1)S(1)}, f32[512,128]{1,0:T(8,128)S(1)}, f32[4,128]{1,0:T(4,128)S(1)}, bf16[528,128]{1,0:T(8,128)(2,1)S(1)}) custom-call(bf16[128,256]{1,0:T(8,128)(2,1)} %bitcast.9, bf16[128,256]{1,0:T(8,128)(2,1)S(1)} %collective-permute-done.refs_1_, s32[1,128]{1,0:T(1,128)S(1)} %reshape.10.refs_2_, ...), custom_call_target="tpu_custom_call" | custom-call | tf_op jit(solution)/shard_map/pallas_call | solution.py:40
  6.3 2.7 %collective-permute-start.2 = (bf16[528,128]{1,0:T(8,128)(2,1)S(1)}, bf16[528,128]{1,0:T(8,128)(2,1)S(1)}, u32[]{:S(2)}, u32[]{:S(2)}) collective-permute-start(bf16[528,128]{1,0:T(8,128)(2,1)S(1)} %get-tuple-element.25), channel_id=1, source_target_pairs={{0,2},{2,0},{4,6},{6,4},{8,10},{10,8},{12,14},{14,12},{16,18},{18,... | collective-permute-start | bytes 405512 | tf_op jit(solution)/shard_map/ppermute | solution.py:324
  9.0 4.1 %collective-permute-done.2.recv_ref = bf16[528,128]{1,0:T(8,128)(2,1)S(1)} collective-permute-done((bf16[528,128]{1,0:T(8,128)(2,1)S(1)}, bf16[528,128]{1,0:T(8,128)(2,1)S(1)}, u32[]{:S(2)}, u32[]{:S(2)}) %collective-permute-start.2) | collective-permute-done | bytes 135200 | tf_op jit(solution)/shard_map/ppermute | solution.py:324
  13.1 0.1 shard_map.138
  13.2 1.8 %collective-permute-start.3 = (bf16[528,128]{1,0:T(8,128)(2,1)S(1)}, bf16[528,128]{1,0:T(8,128)(2,1)S(1)}, u32[]{:S(2)}, u32[]{:S(2)}) collective-permute-start(bf16[528,128]{1,0:T(8,128)(2,1)S(1)} %get-tuple-element.28), channel_id=1, source_target_pairs={{0,4},{2,6},{4,0},{6,2},{8,12},{10,14},{12,8},{14,10},{16,20},{18,... | collective-permute-start | bytes 405512 | tf_op jit(solution)/shard_map/ppermute | solution.py:324
  15.0 3.5 %collective-permute-done.3.recv_ref = bf16[528,128]{1,0:T(8,128)(2,1)S(1)} collective-permute-done((bf16[528,128]{1,0:T(8,128)(2,1)S(1)}, bf16[528,128]{1,0:T(8,128)(2,1)S(1)}, u32[]{:S(2)}, u32[]{:S(2)}) %collective-permute-start.3) | collective-permute-done | bytes 135200 | tf_op jit(solution)/shard_map/ppermute | solution.py:324
  18.5 0.1 shard_map.139
  18.6 1.6 %collective-permute-start.4 = (bf16[528,128]{1,0:T(8,128)(2,1)S(1)}, bf16[528,128]{1,0:T(8,128)(2,1)S(1)}, u32[]{:S(2)}, u32[]{:S(2)}) collective-permute-start(bf16[528,128]{1,0:T(8,128)(2,1)S(1)} %get-tuple-element.33), channel_id=1, source_target_pairs={{0,8},{2,10},{4,12},{6,14},{8,0},{10,2},{12,4},{14,6},{16,24},{18,... | collective-permute-start | bytes 405512 | tf_op jit(solution)/shard_map/ppermute | solution.py:324
  20.2 3.4 %collective-permute-done.4.recv_ref = bf16[528,128]{1,0:T(8,128)(2,1)S(1)} collective-permute-done((bf16[528,128]{1,0:T(8,128)(2,1)S(1)}, bf16[528,128]{1,0:T(8,128)(2,1)S(1)}, u32[]{:S(2)}, u32[]{:S(2)}) %collective-permute-start.4) | collective-permute-done | bytes 135200 | tf_op jit(solution)/shard_map/ppermute | solution.py:324
  23.7 0.1 shard_map.140
  23.7 2.8 %collective-permute-start.5 = (bf16[528,128]{1,0:T(8,128)(2,1)S(1)}, bf16[528,128]{1,0:T(8,128)(2,1)S(1)}, u32[]{:S(2)}, u32[]{:S(2)}) collective-permute-start(bf16[528,128]{1,0:T(8,128)(2,1)S(1)} %get-tuple-element.38), channel_id=1, source_target_pairs={{0,16},{2,18},{4,20},{6,22},{8,24},{10,26},{12,28},{14,30},{16,0},... | collective-permute-start | bytes 405512 | tf_op jit(solution)/shard_map/ppermute | solution.py:324
  26.6 0.3 shard_map.137.key_ref
  26.9 4.3 %collective-permute-done.5.recv_ref = bf16[528,128]{1,0:T(8,128)(2,1)S(1)} collective-permute-done((bf16[528,128]{1,0:T(8,128)(2,1)S(1)}, bf16[528,128]{1,0:T(8,128)(2,1)S(1)}, u32[]{:S(2)}, u32[]{:S(2)}) %collective-permute-start.5) | collective-permute-done | bytes 135200 | tf_op jit(solution)/shard_map/ppermute | solution.py:324
  31.2 0.0 copy-start.2
  31.2 0.0 copy-start.3
  31.2 0.0 copy-start.5
  31.3 2.1 %all_gather.3.memory_ref = bf16[1024,128]{1,0:T(8,128)(2,1)S(1)} all-gather(bf16[512,128]{1,0:T(8,128)(2,1)S(1)} %shard_map.141), channel_id=1, replica_groups=mesh['tm'=16,'space'=2] {'space'}, dimensions={0}, use_global_device_ids=true | all-gather | bytes 393216 | tf_op jit(solution)/shard_map/all_gather | solution.py:335
  33.4 1.9 %shard_map.142 = f32[8,256]{1,0:T(8,128)} custom-call(bf16[256,1024]{1,0:T(8,128)(2,1)S(1)} %shard_map.137.key_ref, bf16[256,256]{1,0:T(8,128)(2,1)S(1)} %get-tuple-element.24.window_ref, bf16[1024,128]{1,0:T(8,128)(2,1)S(1)} %all_gather.3.memory_ref, bf16[1024,256]{1,0:T(8,128)(2,1)S(1)} %copy-done.1, bf16[3,3,64,256]{3,2,1,0:T(8,128)(2,1)S(1)} %bitcast.5, ...), custom_call_target="tpu_custom_call" | custom-call | tf_op jit(solution)/shard_map/pallas_call | solution.py:40
  (11 shorter events, 0.1 us)
Async XLA Ops:
  0.0 2.4 %copy-start.4 = (f32[4,256]{1,0:T(4,128)S(1)}, f32[4,256]{1,0:T(4,128)}, u32[]{:S(2)}) copy-start(f32[4,256]{1,0:T(4,128)} %refs_4_.1) | copy-start | bytes 12292
  0.0 2.4 %collective-permute-start = (bf16[128,256]{1,0:T(8,128)(2,1)}, bf16[128,256]{1,0:T(8,128)(2,1)S(1)}, u32[]{:S(2)}, u32[]{:S(2)}) collective-permute-start(bf16[128,256]{1,0:T(8,128)(2,1)} %bitcast.8), channel_id=1, source_target_pairs={{0,1},{1,0},{2,3},{3,2},{4,5},{5,4},{6,7},{7,6},{8,9},{9,8},{10,11... | collective-permute-start | bytes 196616 | tf_op jit(solution)/shard_map/ppermute | solution.py:275
  1.3 1.2 %copy-start.6 = (f32[256]{0:T(256)S(1)}, f32[256]{0:T(256)}, u32[]{:S(2)}) copy-start(f32[256]{0:T(256)} %param.19) | copy-start | bytes 3076
  1.3 1.2 %collective-permute-start.1 = (s32[1,128]{1,0:T(1,128)S(1)}, s32[1,128]{1,0:T(1,128)S(1)}, u32[]{:S(2)}, u32[]{:S(2)}) collective-permute-start(s32[1,128]{1,0:T(1,128)S(1)} %reshape.10.refs_2_), channel_id=1, source_target_pairs={{0,1},{1,0},{2,3},{3,2},{4,5},{5,4},{6,7},{7,6},{8,9},{9,8},{10,11... | collective-permute-start | bytes 1544 | tf_op jit(solution)/shard_map/ppermute | solution.py:276
  6.3 6.8 %collective-permute-start.2 = (bf16[528,128]{1,0:T(8,128)(2,1)S(1)}, bf16[528,128]{1,0:T(8,128)(2,1)S(1)}, u32[]{:S(2)}, u32[]{:S(2)}) collective-permute-start(bf16[528,128]{1,0:T(8,128)(2,1)S(1)} %get-tuple-element.25), channel_id=1, source_target_pairs={{0,2},{2,0},{4,6},{6,4},{8,10},{10,8},{12,14},{14,12},{16,18},{18,... | collective-permute-start | bytes 405512 | tf_op jit(solution)/shard_map/ppermute | solution.py:324
  13.2 5.3 %collective-permute-start.3 = (bf16[528,128]{1,0:T(8,128)(2,1)S(1)}, bf16[528,128]{1,0:T(8,128)(2,1)S(1)}, u32[]{:S(2)}, u32[]{:S(2)}) collective-permute-start(bf16[528,128]{1,0:T(8,128)(2,1)S(1)} %get-tuple-element.28), channel_id=1, source_target_pairs={{0,4},{2,6},{4,0},{6,2},{8,12},{10,14},{12,8},{14,10},{16,20},{18,... | collective-permute-start | bytes 405512 | tf_op jit(solution)/shard_map/ppermute | solution.py:324
  18.5 8.1 %copy-start = (bf16[256,1024]{1,0:T(8,128)(2,1)S(1)}, bf16[256,1024]{1,0:T(8,128)(2,1)}, u32[]{:S(2)}) copy-start(bf16[256,1024]{1,0:T(8,128)(2,1)} %key_ref.1) | copy-start | bytes 1572868
  18.6 5.1 %collective-permute-start.4 = (bf16[528,128]{1,0:T(8,128)(2,1)S(1)}, bf16[528,128]{1,0:T(8,128)(2,1)S(1)}, u32[]{:S(2)}, u32[]{:S(2)}) collective-permute-start(bf16[528,128]{1,0:T(8,128)(2,1)S(1)} %get-tuple-element.33), channel_id=1, source_target_pairs={{0,8},{2,10},{4,12},{6,14},{8,0},{10,2},{12,4},{14,6},{16,24},{18,... | collective-permute-start | bytes 405512 | tf_op jit(solution)/shard_map/ppermute | solution.py:324
  23.7 7.4 %collective-permute-start.5 = (bf16[528,128]{1,0:T(8,128)(2,1)S(1)}, bf16[528,128]{1,0:T(8,128)(2,1)S(1)}, u32[]{:S(2)}, u32[]{:S(2)}) collective-permute-start(bf16[528,128]{1,0:T(8,128)(2,1)S(1)} %get-tuple-element.38), channel_id=1, source_target_pairs={{0,16},{2,18},{4,20},{6,22},{8,24},{10,26},{12,28},{14,30},{16,0},... | collective-permute-start | bytes 405512 | tf_op jit(solution)/shard_map/ppermute | solution.py:324
  31.2 2.2 %copy-start.1 = (bf16[1024,256]{1,0:T(8,128)(2,1)S(1)}, bf16[1024,256]{1,0:T(8,128)(2,1)}, u32[]{:S(2)}) copy-start(bf16[1024,256]{1,0:T(8,128)(2,1)} %read_ref.1) | copy-start | bytes 1572868
  31.2 2.2 %copy-start.2 = (bf16[3,3,256,64]{2,3,1,0:T(8,128)(2,1)S(1)}, bf16[3,3,256,64]{2,3,1,0:T(8,128)(2,1)}, u32[]{:S(2)}) copy-start(bf16[3,3,256,64]{2,3,1,0:T(8,128)(2,1)} %param.24) | copy-start | bytes 884740
  31.2 2.2 %copy-start.3 = (bf16[256,64]{1,0:T(8,128)(2,1)S(1)}, bf16[256,64]{1,0:T(8,128)(2,1)}, u32[]{:S(2)}) copy-start(bf16[256,64]{1,0:T(8,128)(2,1)} %constant.5.clone.spread_ref) | copy-start | bytes 98308
  31.2 2.2 %copy-start.5 = (bf16[64,16]{0,1:T(8,128)(2,1)S(1)}, bf16[64,16]{0,1:T(8,128)(2,1)}, u32[]{:S(2)}) copy-start(bf16[64,16]{0,1:T(8,128)(2,1)} %param.25) | copy-start | bytes 6148

commit v3 on v2

--- a/solution.py
+++ b/solution.py
@@ -66,12 +66,12 @@
     pay_ref[share * key_dim :, :] = jnp.concatenate(parts, axis=0).astype(BF16)
 
 
-def encode_body(width, share, parts, *refs):
+def encode_body(width, parts, *refs):
     tiles, labels = refs[:parts], refs[parts : 2 * parts]
-    table_ref, gain_ref, decay_ref = refs[2 * parts : 2 * parts + 3]
-    pool_hbm, qkv_hbm, out_hbm, key_hbm, value_hbm = refs[2 * parts + 3 : 2 * parts + 8]
-    window_ref, state_ref, product_ref, pay_ref = refs[2 * parts + 8 : 2 * parts + 12]
-    padded, tile_ref, pool_ref, qkv_ref, out_ref, key_ref, value_ref, sems = refs[2 * parts + 12 :]
+    rest = refs[2 * parts :]
+    table_ref, gain_ref, pool_hbm, qkv_hbm, out_hbm, key_hbm, value_hbm = rest[:7]
+    window_ref, encoded_ref, memory_ref, key_ref, value_ref = rest[7:12]
+    padded, tile_ref, pool_ref, qkv_ref, out_ref, sems = rest[12:]
     place = lax.axis_index("space")
     cols, val_cols = key_ref.shape[1], value_ref.shape[1]
     key_start = pl.multiple_of(place * cols, LANES)
@@ -134,27 +134,39 @@
     kind = lax.broadcasted_iota(jnp.int32, (kinds, tokens), 0)
     one_hot = (jnp.broadcast_to(label, (kinds, tokens)) == kind).astype(F32)
     label_rows = dot_on(one_hot, table_ref[...], 0, 0, lax.Precision.HIGHEST)
-    memory_in = (encoded.astype(F32) + flag * label_rows).astype(BF16)
+    memory_ref[...] = (encoded.astype(F32) + flag * label_rows).astype(BF16)
+    encoded_ref[...] = encoded
     loads[4].wait()
-    own_keys = dot(encoded, key_ref[...]).astype(BF16)
     loads[5].wait()
-    own_values = dot(memory_in, value_ref[...]).astype(BF16)
-    key_dim, val_dim = cols // share, val_cols // share
+
+
+def state_body(
+    share, first_head, encoded_ref, memory_ref, key_ref, value_ref, decay_ref, *out_refs
+):
+    state_ref, product_ref, pay_ref = out_refs
+    heads = product_ref.shape[0]
+    key_dim, val_dim = key_ref.shape[1] // share, value_ref.shape[1] // share
+    tokens = encoded_ref.shape[0]
+    cols = slice(first_head * key_dim, (first_head + heads) * key_dim)
+    val_cols = slice(first_head * val_dim, (first_head + heads) * val_dim)
+    keys = dot(encoded_ref[...], key_ref[:, cols]).astype(BF16)
+    values = dot(memory_ref[...], value_ref[:, val_cols]).astype(BF16)
     states = []
-    for h in range(share):
+    for h in range(heads):
         state = dot_on(
-            own_keys[:, h * key_dim : (h + 1) * key_dim],
-            own_values[:, h * val_dim : (h + 1) * val_dim],
+            keys[:, h * key_dim : (h + 1) * key_dim],
+            values[:, h * val_dim : (h + 1) * val_dim],
             0,
             0,
         ) * tokens ** (-0.5)
         state_ref[h * key_dim : (h + 1) * key_dim, :] = state
         states.append(state)
+    start = lax.axis_index("space") * share + first_head
     product = jnp.concatenate(
-        [jnp.full((1, val_dim), decay_ref[0, place * share + h], F32) for h in range(share)], axis=0
+        [jnp.full((1, val_dim), decay_ref[0, start + h], F32) for h in range(heads)], axis=0
     )
     product_ref[...] = product
-    write_payload(pay_ref, states, product, share, key_dim)
+    write_payload(pay_ref, states, product, heads, key_dim)
 
 
 def combine_body(bit, share, first, last, recv_ref, total_ref, product_ref, *refs):
@@ -264,7 +276,6 @@
     heads = decay.shape[1]
     share = heads // bands
     key_dim, val_dim = key_proj.shape[1] // heads, value_proj.shape[1] // heads
-    rows = share * key_dim
     window_rows = tile_tok + 2 * width
     sds = pltpu.VMEM
 
@@ -284,54 +295,71 @@
     wide = np.arange(width * UP)
     spread = jnp.asarray((wide[:, None] // UP) == np.arange(width)[None, :], BF16)
 
-    pay = sds((rows + carry_rows(share), val_dim), BF16)
-    state = sds((rows, val_dim), F32)
-    small = sds((share, val_dim), F32)
     parts = len(tiles)
-    key_cols, val_cols = share * key_dim, share * val_dim
-    window, total, product, payload = call(
-        functools.partial(encode_body, width, share, parts),
-        (sds((window_rows, dim), BF16), state, small, pay),
+    window, encoded, memory_in, own_keys, own_values = call(
+        functools.partial(encode_body, width, parts),
+        (
+            sds((window_rows, dim), BF16),
+            sds((tokens, dim), BF16),
+            sds((tokens, dim), BF16),
+            sds((dim, share * key_dim), BF16),
+            sds((dim, share * val_dim), BF16),
+        ),
         (
             pltpu.VMEM((tokens + 2 * width, dim), BF16),
             pltpu.VMEM(tiles[0].shape, BF16),
             pltpu.VMEM(pool.shape, BF16),
             pltpu.VMEM(enc_qkv.shape, BF16),
             pltpu.VMEM(enc_out.shape, BF16),
-            pltpu.VMEM((dim, key_cols), BF16),
-            pltpu.VMEM((dim, val_cols), BF16),
             pltpu.SemaphoreType.DMA((6,)),
         ),
-        [pl.ANY] + [pltpu.VMEM] * (2 * parts + 1) + [pltpu.SMEM] + [pl.ANY] * 5,
+        [pl.ANY] + [pltpu.VMEM] * (2 * parts + 1) + [pl.ANY] * 5,
     )(
         *tiles,
         *marks,
         label_table,
         norm_gain.reshape(1, dim),
-        decay,
         pool,
         enc_qkv,
         enc_out,
         key_proj,
         value_proj,
     )
-    carried = ()
+    chains = 2 if share % 2 == 0 else 1
+    group = share // chains
+    rows = group * key_dim
+    pay = sds((rows + carry_rows(group), val_dim), BF16)
+    state = sds((rows, val_dim), F32)
+    small = sds((group, val_dim), F32)
+    held = [
+        call(
+            functools.partial(state_body, share, chain * group),
+            (state, small, pay),
+            (),
+            [pltpu.VMEM] * 4 + [pltpu.SMEM],
+        )(encoded, memory_in, own_keys, own_values, decay)
+        for chain in range(chains)
+    ]
+    key_rows = call(keys_body, sds((window_rows, heads * key_dim), BF16))(window, key_proj)
+    held = [(total, product, (), payload) for total, product, payload in held]
     steps = (frames - 1).bit_length()
-    key_rows = None
+    memories = []
     for bit in range(steps):
         first, last = bit == 0, bit == steps - 1
         pairs = [(i, i ^ (1 << bit)) for i in range(frames) if i ^ (1 << bit) < frames]
-        arrived = lax.ppermute(payload, "tm", pairs)
-        if first:
-            key_rows = call(keys_body, sds((window_rows, heads * key_dim), BF16))(window, key_proj)
-        body = functools.partial(combine_body, bit, share, first, last)
-        if last:
-            memory = call(body, sds((rows, val_dim), BF16))(arrived, total, product, *carried)
-        else:
-            total, product, reach, prefix, payload = call(body, (state, small, small, state, pay))(
-                arrived, total, product, *carried
-            )
-            carried = (reach, prefix)
+        body = functools.partial(combine_body, bit, group, first, last)
+        for chain, (total, product, carried, payload) in enumerate(held):
+            arrived = lax.ppermute(payload, "tm", pairs)
+            if last:
+                memories.append(
+                    call(body, sds((rows, val_dim), BF16))(arrived, total, product, *carried)
+                )
+            else:
+                total, product, reach, prefix, payload = call(
+                    body, (state, small, small, state, pay)
+                )(arrived, total, product, *carried)
+                held[chain] = (total, product, (reach, prefix), payload)
+    memory = memories[0] if chains == 1 else jnp.concatenate(memories, axis=0)
     memory = lax.all_gather(memory, "space", axis=0, tiled=True)
     logits = call(
         functools.partial(decode_body, width, heads),

time: 35.5 us -> 33.7 us (0.949)
  waiting for transfers between devices: 16.5 us -> 7.48 us
  starting transfers between devices: 9.5 us -> 15.5 us
  Pallas kernels: 6.31 us -> 7.17 us
    ppermute x4 -> x8, waiting for transfers between devices: 15.3 us -> 6.34 us  [shards(): arrived = lax.ppermute(payload, 'tm', pairs)]
    ppermute x4 -> x8, starting transfers between devices: 8.99 us -> 15 us  [shards(): arrived = lax.ppermute(payload, 'tm', pairs)]
    pallas_call x7 -> x13, Pallas kernels: 6.31 us -> 7.17 us  [on_chip(): run(*[pltpu.with_memory_space_constraint(x, place) if place is pltpu.VMEM...]
  transfers between devices with their start and end apart: 6 -> 10, of which waited for: 5 -> 7; matrix products, arithmetic and copies ran while one was open for 2% -> 2% of each run, Pallas kernels for 1% -> 5%
where the time goes in v3:
time: 33.7 us; the launch traced here: 33.2 us
  starting transfers between devices  15.5 us (46%)
  waiting for transfers between devices  7.48 us (22%)
  Pallas kernels  7.17 us (21%)
  blocking collectives  2.13 us (6%)
  local copies, waits for them, and re-layouts  0.8 us (2%)
    ppermute x8, starting transfers between devices, shards(): arrived = lax.ppermute(payload, 'tm', pairs)  15 us
    pallas_call x13, Pallas kernels, on_chip(): run(*[pltpu.with_memory_space_constraint(x, place) if place is pltpu.VMEM...  7.17 us
    ppermute x8, waiting for transfers between devices, shards(): arrived = lax.ppermute(payload, 'tm', pairs)  6.34 us
    all_gather x1, blocking collectives, shards(): memory = lax.all_gather(memory, 'space', axis=0, tiled=True)  2.13 us
    ppermute x1, waiting for transfers between devices, shards(): marks = [labels, lax.ppermute(labels, 'space', swap)]  1.14 us
    reshape x1, local copies, waits for them, and re-layouts, shards(): labels = prompt_labels.reshape(1, tile_tok)  0.76 us
  transfers between devices with their start and end apart: 10, of which 7 were waited for; matrix products, arithmetic and copies ran while one was open for 2% of the time, Pallas kernels for 5%

profile of v3, /device:TPU:0, one launch (start us, length us, event | category | flops | bytes accessed | tf_op | source)
XLA Modules:
  0.0 33.2 jit_solution(7202974943702837575)
XLA Ops:
  0.0 0.5 %collective-permute-start = (bf16[128,256]{1,0:T(8,128)(2,1)}, bf16[128,256]{1,0:T(8,128)(2,1)S(1)}, u32[]{:S(2)}, u32[]{:S(2)}) collective-permute-start(bf16[128,256]{1,0:T(8,128)(2,1)} %bitcast.8), channel_id=1, source_target_pairs={{0,1},{1,0},{2,3},{3,2},{4,5},{5,4},{6,7},{7,6},{8,9},{9,8},{10,11... | collective-permute-start | bytes 196616 | tf_op jit(solution)/shard_map/ppermute | solution.py:286
  0.5 0.8 %reshape.10.refs_2_ = s32[1,128]{1,0:T(1,128)S(1)} reshape(s32[2,64]{1,0:T(2,128)} %param.15) | data formatting | bytes 1024 | tf_op jit(solution)/shard_map/reshape | solution.py:283
  1.3 1.1 %collective-permute-done.1.refs_3_ = s32[1,128]{1,0:T(1,128)S(1)} collective-permute-done((s32[1,128]{1,0:T(1,128)S(1)}, s32[1,128]{1,0:T(1,128)S(1)}, u32[]{:S(2)}, u32[]{:S(2)}) %collective-permute-start.1) | collective-permute-done | bytes 544 | tf_op jit(solution)/shard_map/ppermute | solution.py:287
  2.4 2.5 %shard_map.136 = (bf16[256,256]{1,0:T(8,128)(2,1)S(1)}, bf16[256,256]{1,0:T(8,128)(2,1)S(1)}, bf16[256,256]{1,0:T(8,128)(2,1)S(1)}, bf16[256,512]{1,0:T(8,128)(2,1)S(1)}, bf16[256,512]{1,0:T(8,128)(2,1)S(1)}) custom-call(bf16[128,256]{1,0:T(8,128)(2,1)} %bitcast.9, bf16[128,256]{1,0:T(8,128)(2,1)S(1)} %collective-permute-done.refs_1_, ...), custom_call_target="tpu_custom_call" | custom-call | tf_op jit(solution)/shard_map/pallas_call | solution.py:40
  4.9 1.1 %shard_map.138 = (f32[256,128]{1,0:T(8,128)S(1)}, f32[2,128]{1,0:T(2,128)S(1)}, bf16[272,128]{1,0:T(8,128)(2,1)S(1)}) custom-call(bf16[256,256]{1,0:T(8,128)(2,1)S(1)} %get-tuple-element.47.encoded_ref, bf16[256,256]{1,0:T(8,128)(2,1)S(1)} %get-tuple-element.48.memory_ref, bf16[256,512]{1,0:T(8,128)(2,1)S(1)} %get-tuple-element.49.key_ref, ...), custom_call_target="tpu_custom_call" | custom-call | tf_op jit(solution)/shard_map/pallas_call | solution.py:40
  6.0 2.7 %collective-permute-start.2 = (bf16[272,128]{1,0:T(8,128)(2,1)S(1)}, bf16[272,128]{1,0:T(8,128)(2,1)S(1)}, u32[]{:S(2)}, u32[]{:S(2)}) collective-permute-start(bf16[272,128]{1,0:T(8,128)(2,1)S(1)} %get-tuple-element.51), channel_id=1, source_target_pairs={{0,2},{2,0},{4,6},{6,4},{8,10},{10,8},{12,14},{14,12},{16,18},{18,... | collective-permute-start | bytes 208904 | tf_op jit(solution)/shard_map/ppermute | solution.py:352
  8.7 1.1 %shard_map.143 = (f32[256,128]{1,0:T(8,128)S(1)}, f32[2,128]{1,0:T(2,128)S(1)}, bf16[272,128]{1,0:T(8,128)(2,1)S(1)}) custom-call(bf16[256,256]{1,0:T(8,128)(2,1)S(1)} %get-tuple-element.47.encoded_ref, bf16[256,256]{1,0:T(8,128)(2,1)S(1)} %get-tuple-element.48.memory_ref, bf16[256,512]{1,0:T(8,128)(2,1)S(1)} %get-tuple-element.49.key_ref, ...), custom_call_target="tpu_custom_call" | custom-call | tf_op jit(solution)/shard_map/pallas_call | solution.py:40
  9.8 0.1 collective-permute-start.6
  9.9 1.5 %collective-permute-done.2.recv_ref = bf16[272,128]{1,0:T(8,128)(2,1)S(1)} collective-permute-done((bf16[272,128]{1,0:T(8,128)(2,1)S(1)}, bf16[272,128]{1,0:T(8,128)(2,1)S(1)}, u32[]{:S(2)}, u32[]{:S(2)}) %collective-permute-start.2) | collective-permute-done | bytes 69664 | tf_op jit(solution)/shard_map/ppermute | solution.py:352
  11.4 1.8 %collective-permute-start.3 = (bf16[272,128]{1,0:T(8,128)(2,1)S(1)}, bf16[272,128]{1,0:T(8,128)(2,1)S(1)}, u32[]{:S(2)}, u32[]{:S(2)}) collective-permute-start(bf16[272,128]{1,0:T(8,128)(2,1)S(1)} %get-tuple-element.54), channel_id=1, source_target_pairs={{0,4},{2,6},{4,0},{6,2},{8,12},{10,14},{12,8},{14,10},{16,20},{18,... | collective-permute-start | bytes 208904 | tf_op jit(solution)/shard_map/ppermute | solution.py:352
  13.3 0.9 %collective-permute-done.6.recv_ref = bf16[272,128]{1,0:T(8,128)(2,1)S(1)} collective-permute-done((bf16[272,128]{1,0:T(8,128)(2,1)S(1)}, bf16[272,128]{1,0:T(8,128)(2,1)S(1)}, u32[]{:S(2)}, u32[]{:S(2)}) %collective-permute-start.6) | collective-permute-done | bytes 69664 | tf_op jit(solution)/shard_map/ppermute | solution.py:352
  14.2 1.6 %collective-permute-start.7 = (bf16[272,128]{1,0:T(8,128)(2,1)S(1)}, bf16[272,128]{1,0:T(8,128)(2,1)S(1)}, u32[]{:S(2)}, u32[]{:S(2)}) collective-permute-start(bf16[272,128]{1,0:T(8,128)(2,1)S(1)} %get-tuple-element.72), channel_id=1, source_target_pairs={{0,4},{2,6},{4,0},{6,2},{8,12},{10,14},{12,8},{14,10},{16,20},{18,... | collective-permute-start | bytes 208904 | tf_op jit(solution)/shard_map/ppermute | solution.py:352
  15.9 2.2 %collective-permute-start.4 = (bf16[272,128]{1,0:T(8,128)(2,1)S(1)}, bf16[272,128]{1,0:T(8,128)(2,1)S(1)}, u32[]{:S(2)}, u32[]{:S(2)}) collective-permute-start(bf16[272,128]{1,0:T(8,128)(2,1)S(1)} %get-tuple-element.59), channel_id=1, source_target_pairs={{0,8},{2,10},{4,12},{6,14},{8,0},{10,2},{12,4},{14,6},{16,24},{18,... | collective-permute-start | bytes 208904 | tf_op jit(solution)/shard_map/ppermute | solution.py:352
  18.0 0.6 %collective-permute-done.7.recv_ref = bf16[272,128]{1,0:T(8,128)(2,1)S(1)} collective-permute-done((bf16[272,128]{1,0:T(8,128)(2,1)S(1)}, bf16[272,128]{1,0:T(8,128)(2,1)S(1)}, u32[]{:S(2)}, u32[]{:S(2)}) %collective-permute-start.7) | collective-permute-done | bytes 69664 | tf_op jit(solution)/shard_map/ppermute | solution.py:352
  18.7 1.6 %collective-permute-start.8 = (bf16[272,128]{1,0:T(8,128)(2,1)S(1)}, bf16[272,128]{1,0:T(8,128)(2,1)S(1)}, u32[]{:S(2)}, u32[]{:S(2)}) collective-permute-start(bf16[272,128]{1,0:T(8,128)(2,1)S(1)} %get-tuple-element.77), channel_id=1, source_target_pairs={{0,8},{2,10},{4,12},{6,14},{8,0},{10,2},{12,4},{14,6},{16,24},{18,... | collective-permute-start | bytes 208904 | tf_op jit(solution)/shard_map/ppermute | solution.py:352
  20.3 0.4 %collective-permute-done.4.recv_ref = bf16[272,128]{1,0:T(8,128)(2,1)S(1)} collective-permute-done((bf16[272,128]{1,0:T(8,128)(2,1)S(1)}, bf16[272,128]{1,0:T(8,128)(2,1)S(1)}, u32[]{:S(2)}, u32[]{:S(2)}) %collective-permute-start.4) | collective-permute-done | bytes 69664 | tf_op jit(solution)/shard_map/ppermute | solution.py:352
  20.7 3.0 %collective-permute-start.5 = (bf16[272,128]{1,0:T(8,128)(2,1)S(1)}, bf16[272,128]{1,0:T(8,128)(2,1)S(1)}, u32[]{:S(2)}, u32[]{:S(2)}) collective-permute-start(bf16[272,128]{1,0:T(8,128)(2,1)S(1)} %get-tuple-element.64), channel_id=1, source_target_pairs={{0,16},{2,18},{4,20},{6,22},{8,24},{10,26},{12,28},{14,30},{16,0},... | collective-permute-start | bytes 208904 | tf_op jit(solution)/shard_map/ppermute | solution.py:352
  23.7 0.1 shard_map.146
  23.8 2.0 %collective-permute-start.9 = (bf16[272,128]{1,0:T(8,128)(2,1)S(1)}, bf16[272,128]{1,0:T(8,128)(2,1)S(1)}, u32[]{:S(2)}, u32[]{:S(2)}) collective-permute-start(bf16[272,128]{1,0:T(8,128)(2,1)S(1)} %get-tuple-element.82), channel_id=1, source_target_pairs={{0,16},{2,18},{4,20},{6,22},{8,24},{10,26},{12,28},{14,30},{16,0},... | collective-permute-start | bytes 208904 | tf_op jit(solution)/shard_map/ppermute | solution.py:352
  25.7 0.3 shard_map.137.key_ref
  26.1 1.3 %collective-permute-done.5.recv_ref = bf16[272,128]{1,0:T(8,128)(2,1)S(1)} collective-permute-done((bf16[272,128]{1,0:T(8,128)(2,1)S(1)}, bf16[272,128]{1,0:T(8,128)(2,1)S(1)}, u32[]{:S(2)}, u32[]{:S(2)}) %collective-permute-start.5) | collective-permute-done | bytes 69664 | tf_op jit(solution)/shard_map/ppermute | solution.py:352
  27.4 1.7 %collective-permute-done.9.recv_ref = bf16[272,128]{1,0:T(8,128)(2,1)S(1)} collective-permute-done((bf16[272,128]{1,0:T(8,128)(2,1)S(1)}, bf16[272,128]{1,0:T(8,128)(2,1)S(1)}, u32[]{:S(2)}, u32[]{:S(2)}) %collective-permute-start.9) | collective-permute-done | bytes 69664 | tf_op jit(solution)/shard_map/ppermute | solution.py:352
  29.1 2.1 %all_gather.3.memory_ref = bf16[1024,128]{1,0:T(8,128)(2,1)S(1)} all-gather(bf16[512,128]{1,0:T(8,128)(2,1)S(1)} %pad_maximum_fusion), channel_id=1, replica_groups=mesh['tm'=16,'space'=2] {'space'}, dimensions={0}, use_global_device_ids=true | all-gather | bytes 393216 | tf_op jit(solution)/shard_map/all_gather | solution.py:363
  31.3 1.9 %shard_map.148 = f32[8,256]{1,0:T(8,128)} custom-call(bf16[256,1024]{1,0:T(8,128)(2,1)S(1)} %shard_map.137.key_ref, bf16[256,256]{1,0:T(8,128)(2,1)S(1)} %get-tuple-element.46.window_ref, bf16[1024,128]{1,0:T(8,128)(2,1)S(1)} %all_gather.3.memory_ref, bf16[1024,256]{1,0:T(8,128)(2,1)S(1)} %copy-done.1, bf16[3,3,64,256]{3,2,1,0:T(8,128)(2,1)S(1)} %bitcast.5, ...), custom_call_target="tpu_custom_call" | custom-call | tf_op jit(solution)/shard_map/pallas_call | solution.py:40
  (26 shorter events, 0.4 us)
Async XLA Ops:
  0.0 2.4 %copy-start.4 = (f32[4,256]{1,0:T(4,128)S(1)}, f32[4,256]{1,0:T(4,128)}, u32[]{:S(2)}) copy-start(f32[4,256]{1,0:T(4,128)} %refs_4_.1) | copy-start | bytes 12292
  0.0 2.4 %collective-permute-start = (bf16[128,256]{1,0:T(8,128)(2,1)}, bf16[128,256]{1,0:T(8,128)(2,1)S(1)}, u32[]{:S(2)}, u32[]{:S(2)}) collective-permute-start(bf16[128,256]{1,0:T(8,128)(2,1)} %bitcast.8), channel_id=1, source_target_pairs={{0,1},{1,0},{2,3},{3,2},{4,5},{5,4},{6,7},{7,6},{8,9},{9,8},{10,11... | collective-permute-start | bytes 196616 | tf_op jit(solution)/shard_map/ppermute | solution.py:286
  1.3 1.2 %copy-start.6 = (f32[256]{0:T(256)S(1)}, f32[256]{0:T(256)}, u32[]{:S(2)}) copy-start(f32[256]{0:T(256)} %param.19) | copy-start | bytes 3076
  1.3 1.2 %collective-permute-start.1 = (s32[1,128]{1,0:T(1,128)S(1)}, s32[1,128]{1,0:T(1,128)S(1)}, u32[]{:S(2)}, u32[]{:S(2)}) collective-permute-start(s32[1,128]{1,0:T(1,128)S(1)} %reshape.10.refs_2_), channel_id=1, source_target_pairs={{0,1},{1,0},{2,3},{3,2},{4,5},{5,4},{6,7},{7,6},{8,9},{9,8},{10,11... | collective-permute-start | bytes 1544 | tf_op jit(solution)/shard_map/ppermute | solution.py:287
  6.0 5.4 %collective-permute-start.2 = (bf16[272,128]{1,0:T(8,128)(2,1)S(1)}, bf16[272,128]{1,0:T(8,128)(2,1)S(1)}, u32[]{:S(2)}, u32[]{:S(2)}) collective-permute-start(bf16[272,128]{1,0:T(8,128)(2,1)S(1)} %get-tuple-element.51), channel_id=1, source_target_pairs={{0,2},{2,0},{4,6},{6,4},{8,10},{10,8},{12,14},{14,12},{16,18},{18,... | collective-permute-start | bytes 208904 | tf_op jit(solution)/shard_map/ppermute | solution.py:352
  9.8 4.4 %collective-permute-start.6 = (bf16[272,128]{1,0:T(8,128)(2,1)S(1)}, bf16[272,128]{1,0:T(8,128)(2,1)S(1)}, u32[]{:S(2)}, u32[]{:S(2)}) collective-permute-start(bf16[272,128]{1,0:T(8,128)(2,1)S(1)} %get-tuple-element.69), channel_id=1, source_target_pairs={{0,2},{2,0},{4,6},{6,4},{8,10},{10,8},{12,14},{14,12},{16,18},{18,... | collective-permute-start | bytes 208904 | tf_op jit(solution)/shard_map/ppermute | solution.py:352
  11.4 4.4 %collective-permute-start.3 = (bf16[272,128]{1,0:T(8,128)(2,1)S(1)}, bf16[272,128]{1,0:T(8,128)(2,1)S(1)}, u32[]{:S(2)}, u32[]{:S(2)}) collective-permute-start(bf16[272,128]{1,0:T(8,128)(2,1)S(1)} %get-tuple-element.54), channel_id=1, source_target_pairs={{0,4},{2,6},{4,0},{6,2},{8,12},{10,14},{12,8},{14,10},{16,20},{18,... | collective-permute-start | bytes 208904 | tf_op jit(solution)/shard_map/ppermute | solution.py:352
  14.2 4.4 %collective-permute-start.7 = (bf16[272,128]{1,0:T(8,128)(2,1)S(1)}, bf16[272,128]{1,0:T(8,128)(2,1)S(1)}, u32[]{:S(2)}, u32[]{:S(2)}) collective-permute-start(bf16[272,128]{1,0:T(8,128)(2,1)S(1)} %get-tuple-element.72), channel_id=1, source_target_pairs={{0,4},{2,6},{4,0},{6,2},{8,12},{10,14},{12,8},{14,10},{16,20},{18,... | collective-permute-start | bytes 208904 | tf_op jit(solution)/shard_map/ppermute | solution.py:352
  15.9 9.9 %copy-start = (bf16[256,1024]{1,0:T(8,128)(2,1)S(1)}, bf16[256,1024]{1,0:T(8,128)(2,1)}, u32[]{:S(2)}) copy-start(bf16[256,1024]{1,0:T(8,128)(2,1)} %key_ref.1) | copy-start | bytes 1572868
  15.9 4.8 %collective-permute-start.4 = (bf16[272,128]{1,0:T(8,128)(2,1)S(1)}, bf16[272,128]{1,0:T(8,128)(2,1)S(1)}, u32[]{:S(2)}, u32[]{:S(2)}) collective-permute-start(bf16[272,128]{1,0:T(8,128)(2,1)S(1)} %get-tuple-element.59), channel_id=1, source_target_pairs={{0,8},{2,10},{4,12},{6,14},{8,0},{10,2},{12,4},{14,6},{16,24},{18,... | collective-permute-start | bytes 208904 | tf_op jit(solution)/shard_map/ppermute | solution.py:352
  18.7 5.1 %collective-permute-start.8 = (bf16[272,128]{1,0:T(8,128)(2,1)S(1)}, bf16[272,128]{1,0:T(8,128)(2,1)S(1)}, u32[]{:S(2)}, u32[]{:S(2)}) collective-permute-start(bf16[272,128]{1,0:T(8,128)(2,1)S(1)} %get-tuple-element.77), channel_id=1, source_target_pairs={{0,8},{2,10},{4,12},{6,14},{8,0},{10,2},{12,4},{14,6},{16,24},{18,... | collective-permute-start | bytes 208904 | tf_op jit(solution)/shard_map/ppermute | solution.py:352
  20.7 6.6 %collective-permute-start.5 = (bf16[272,128]{1,0:T(8,128)(2,1)S(1)}, bf16[272,128]{1,0:T(8,128)(2,1)S(1)}, u32[]{:S(2)}, u32[]{:S(2)}) collective-permute-start(bf16[272,128]{1,0:T(8,128)(2,1)S(1)} %get-tuple-element.64), channel_id=1, source_target_pairs={{0,16},{2,18},{4,20},{6,22},{8,24},{10,26},{12,28},{14,30},{16,0},... | collective-permute-start | bytes 208904 | tf_op jit(solution)/shard_map/ppermute | solution.py:352
  23.8 5.3 %collective-permute-start.9 = (bf16[272,128]{1,0:T(8,128)(2,1)S(1)}, bf16[272,128]{1,0:T(8,128)(2,1)S(1)}, u32[]{:S(2)}, u32[]{:S(2)}) collective-permute-start(bf16[272,128]{1,0:T(8,128)(2,1)S(1)} %get-tuple-element.82), channel_id=1, source_target_pairs={{0,16},{2,18},{4,20},{6,22},{8,24},{10,26},{12,28},{14,30},{16,0},... | collective-permute-start | bytes 208904 | tf_op jit(solution)/shard_map/ppermute | solution.py:352
  29.1 2.2 %copy-start.1 = (bf16[1024,256]{1,0:T(8,128)(2,1)S(1)}, bf16[1024,256]{1,0:T(8,128)(2,1)}, u32[]{:S(2)}) copy-start(bf16[1024,256]{1,0:T(8,128)(2,1)} %read_ref.1) | copy-start | bytes 1572868
  29.1 2.2 %copy-start.2 = (bf16[3,3,256,64]{2,3,1,0:T(8,128)(2,1)S(1)}, bf16[3,3,256,64]{2,3,1,0:T(8,128)(2,1)}, u32[]{:S(2)}) copy-start(bf16[3,3,256,64]{2,3,1,0:T(8,128)(2,1)} %param.24) | copy-start | bytes 884740
  29.1 2.2 %copy-start.3 = (bf16[256,64]{1,0:T(8,128)(2,1)S(1)}, bf16[256,64]{1,0:T(8,128)(2,1)}, u32[]{:S(2)}) copy-start(bf16[256,64]{1,0:T(8,128)(2,1)} %constant.5.clone.spread_ref) | copy-start | bytes 98308
  29.1 2.2 %copy-start.5 = (bf16[64,16]{0,1:T(8,128)(2,1)S(1)}, bf16[64,16]{0,1:T(8,128)(2,1)}, u32[]{:S(2)}) copy-start(bf16[64,16]{0,1:T(8,128)(2,1)} %param.25) | copy-start | bytes 6148

commit v4 on v3

v4 whole, which is shorter than its diff:
```python
import functools

import jax
import jax.numpy as jnp
import numpy as np
from jax import lax
from jax.experimental import pallas as pl
from jax.experimental.pallas import tpu as pltpu
from jax.sharding import PartitionSpec as P

ENC_HEADS = 8
UP = 4
LANES = 128
ON_CHIP = 1 << 18
EPSILON = 1e-06
F32 = jnp.float32
BF16 = jnp.bfloat16
VMEM = pl.BlockSpec(memory_space=pltpu.VMEM)


def dot(a, b):
    return jnp.dot(a, b, preferred_element_type=F32)


def dot_on(a, b, dim_a, dim_b, precision=None):
    return lax.dot_general(
        a, b, (((dim_a,), (dim_b,)), ((), ())), precision=precision, preferred_element_type=F32
    )


def call_in(chip, body, outs, scratch=(), spaces=None, micros=0):
    def result(x):
        shaped = jax.ShapeDtypeStruct(x.shape, x.dtype)
        return x if chip or isinstance(x, jax.ShapeDtypeStruct) else shaped

    outs = jax.tree.map(result, outs)

    def run(*operands):
        places = [pltpu.VMEM] * len(operands) if spaces is None else spaces
        kernel = pl.pallas_call(
            body,
            out_shape=outs,
            in_specs=[pl.BlockSpec(memory_space=place) for place in places],
            out_specs=jax.tree.map(lambda _: VMEM, outs),
            scratch_shapes=scratch,
            cost_estimate=pl.CostEstimate(
                flops=int(micros * 1e9), transcendentals=0, bytes_accessed=0
            ),
        )
        held = chip and pltpu.VMEM
        return kernel(
            *[
                pltpu.with_memory_space_constraint(x, place) if place is held else x
                for x, place in zip(operands, places)
            ]
        )

    return run


def carry_rows(share):
    return -(-3 * share // 16) * 16


def split(x):
    high = x.astype(BF16).astype(F32)
    mid = (x - high).astype(BF16).astype(F32)
    low = (x - high - mid).astype(BF16).astype(F32)
    return [high, mid, low]


def write_payload(pay_ref, totals, product, share, key_dim):
    for h in range(share):
        rows = slice(h * key_dim, (h + 1) * key_dim)
        pay_ref[rows, :] = totals[h].astype(BF16)
    parts = split(product)
    tail = carry_rows(share)
    if tail > 3 * share:
        parts.append(jnp.zeros((tail - 3 * share, product.shape[1]), F32))
    pay_ref[share * key_dim :, :] = jnp.concatenate(parts, axis=0).astype(BF16)


def project_body(loaded, *refs):
    sources, targets = refs[:loaded], refs[loaded : 2 * loaded]
    query_ref, pair_ref, sems = refs[2 * loaded :]
    tile_ref, pool_ref, qkv_ref = targets[:3]
    dim = tile_ref.shape[1]
    loads = [
        pltpu.make_async_copy(source, target, sems.at[n])
        for n, (source, target) in enumerate(zip(sources, targets))
    ]
    for load in loads:
        load.start()
    loads[0].wait()
    loads[1].wait()
    pooled = dot(pool_ref[...], tile_ref[...]).astype(BF16)
    loads[2].wait()
    pair_ref[...] = dot(pooled, qkv_ref[:, dim:]).astype(BF16)
    query_ref[...] = dot(tile_ref[...], qkv_ref[:, :dim]).astype(BF16)
    for load in loads[3:]:
        load.wait()


def encode_body(width, parts, *refs):
    tiles, labels = refs[:parts], refs[parts : 2 * parts]
    rest = refs[2 * parts :]
    query_ref, pair_ref, pool_ref, qkv_ref, table_ref, gain_ref, out_ref, key_ref = rest[:8]
    window_ref, encoded_ref, memory_ref, turned_ref, padded = rest[8:]
    place = lax.axis_index("space")
    dim = query_ref.shape[1]
    size = dim // ENC_HEADS
    window_rows = window_ref.shape[0]
    tile_tok = window_rows - 2 * width
    queries, pairs = [query_ref[...]], [pair_ref[...]]
    for tile in tiles[1:]:
        queries.append(dot(tile[...], qkv_ref[:, :dim]).astype(BF16))
        pooled = dot(pool_ref[...], tile[...]).astype(BF16)
        pairs.append(dot(pooled, qkv_ref[:, dim:]).astype(BF16))
    x = jnp.concatenate([tile[...] for tile in tiles], axis=0)
    queries = jnp.concatenate(queries, axis=0)
    pair = jnp.concatenate(pairs, axis=0)
    tokens = x.shape[0]
    count = pair.shape[0]
    lane = lax.broadcasted_iota(jnp.int32, (count, dim), 1)
    masks = [(lane >= h * size) & (lane < (h + 1) * size) for h in range(ENC_HEADS)]
    zero = jnp.zeros((count, dim), BF16)
    keys = jnp.concatenate([jnp.where(m, pair[:, :dim], zero) for m in masks], axis=0)
    values = jnp.concatenate([jnp.where(m, pair[:, dim:], zero) for m in masks], axis=0)
    scores = (dot_on(keys, queries, 1, 1) * size ** (-0.5)).reshape(ENC_HEADS, count, tokens)
    weights = jnp.exp(scores - jnp.max(scores, axis=1, keepdims=True))
    totals = jnp.sum(weights, axis=1, keepdims=True)
    rounded = weights.astype(BF16).reshape(ENC_HEADS * count, tokens)
    summed = dot_on(values, rounded, 0, 0).reshape(ENC_HEADS, size, tokens)
    attended = (summed / totals).reshape(dim, tokens).astype(BF16)
    hidden = x.astype(F32) + dot_on(attended, out_ref[...], 0, 0)
    scale = lax.rsqrt(jnp.mean(hidden * hidden, axis=-1, keepdims=True) + EPSILON)
    encoded = (hidden * scale * gain_ref[...]).astype(BF16)
    encoded_ref[...] = encoded

    flag = (lax.axis_index("tm") == 0).astype(F32)
    kinds = table_ref.shape[0]
    label = jnp.concatenate(
        [ref[r : r + 1, :] for ref in labels for r in range(ref.shape[0])], axis=1
    )
    kind = lax.broadcasted_iota(jnp.int32, (kinds, tokens), 0)
    one_hot = (jnp.broadcast_to(label, (kinds, tokens)) == kind).astype(F32)
    one_hot = jnp.concatenate([one_hot] * 3, axis=0).astype(BF16)
    label_rows = dot_on(one_hot, jnp.concatenate(split(table_ref[...]), axis=0).astype(BF16), 0, 0)
    memory_ref[...] = (encoded.astype(F32) + flag * label_rows).astype(BF16)

    edge = jnp.zeros((width, dim), BF16)
    padded[:width, :] = edge
    padded[width + tokens :, :] = edge
    for p in range(parts):
        spot = place if p == 0 else 1 - place
        spot = pl.multiple_of(width + spot * tile_tok, width) if parts > 1 else width
        rows = tokens // parts
        padded[pl.ds(spot, rows), :] = encoded[p * rows : (p + 1) * rows]
    window_ref[...] = padded[pl.ds(pl.multiple_of(place * tile_tok, width), window_rows), :]
    cols = turned_ref.shape[0]
    turned_ref[...] = key_ref[:, pl.ds(pl.multiple_of(place * cols, LANES), cols)].T


def state_body(
    share, first_head, encoded_ref, memory_ref, turned_ref, value_ref, decay_ref, *out_refs
):
    state_ref, product_ref, pay_ref = out_refs
    heads = product_ref.shape[0]
    key_dim = turned_ref.shape[0] // share
    val_dim = state_ref.shape[1]
    tokens = encoded_ref.shape[0]
    cols = slice(first_head * key_dim, (first_head + heads) * key_dim)
    start = lax.axis_index("space") * share + first_head
    val_cols = pl.ds(pl.multiple_of(start * val_dim, val_dim), heads * val_dim)
    keys = dot_on(turned_ref[cols, :], encoded_ref[...], 1, 1).astype(BF16)
    values = dot(memory_ref[...], value_ref[:, val_cols]).astype(BF16)
    states = []
    for h in range(heads):
        state = dot(
            keys[h * key_dim : (h + 1) * key_dim], values[:, h * val_dim : (h + 1) * val_dim]
        ) * tokens ** (-0.5)
        state_ref[h * key_dim : (h + 1) * key_dim, :] = state
        states.append(state)
    rates = jnp.broadcast_to(decay_ref[...], (heads, decay_ref.shape[1]))
    head = lax.broadcasted_iota(jnp.int32, rates.shape, 0) + start
    picked = lax.broadcasted_iota(jnp.int32, rates.shape, 1) == head
    rate = jnp.sum(jnp.where(picked, rates, jnp.zeros_like(rates)), axis=1, keepdims=True)
    product = jnp.broadcast_to(rate, (heads, val_dim))
    product_ref[...] = product
    write_payload(pay_ref, states, product, heads, key_dim)


def combine_body(bit, share, first, last, recv_ref, total_ref, product_ref, *refs):
    if not first:
        reach_ref, prefix_ref = refs[:2]
    outs = refs[-1:] if last else refs[-5:]
    rows = total_ref.shape[0]
    key_dim = rows // share
    upper = (lax.axis_index("tm") >> bit) & 1
    is_upper = jnp.full(product_ref.shape, upper, jnp.int32) == 1
    product = product_ref[...]
    reach = product if first else reach_ref[...]
    tail = recv_ref[rows:, :].astype(F32)
    got = tail[:share] + tail[share : 2 * share] + tail[2 * share : 3 * share]
    ones = jnp.ones_like(product)
    on_got = jnp.where(is_upper, product, ones)
    on_own = jnp.where(is_upper, ones, got)
    on_prefix = jnp.where(is_upper, reach, jnp.zeros_like(product))
    totals = []
    for h in range(share):
        part = slice(h * key_dim, (h + 1) * key_dim)
        arrived = recv_ref[part, :].astype(F32)
        prefix = on_prefix[h : h + 1] * arrived
        if not first:
            prefix = prefix + prefix_ref[part, :]
        if last:
            outs[0][part, :] = prefix.astype(BF16)
        else:
            outs[3][part, :] = prefix
            total = on_got[h : h + 1] * arrived + on_own[h : h + 1] * total_ref[part, :]
            totals.append(total)
            outs[0][part, :] = total
    if not last:
        joined = product * got
        outs[1][...] = joined
        outs[2][...] = jnp.where(is_upper, reach * got, reach)
        write_payload(outs[4], totals, joined, share, key_dim)


def keys_body(window_ref, after, key_hbm, *refs):
    count = (len(refs) - 3) // 2
    sources, out_ref, targets, (key_ref, sems) = (
        refs[:count],
        refs[count],
        refs[count + 1 : -2],
        refs[-2:],
    )
    loads = [
        pltpu.make_async_copy(source, target, sems.at[n])
        for n, (source, target) in enumerate(zip((key_hbm, *sources), (key_ref, *targets)))
    ]
    for load in loads:
        load.start()
    loads[0].wait()
    out_ref[...] = dot(window_ref[...], key_ref[...]).astype(BF16)
    for load in loads[1:]:
        load.wait()


def read_rows(heads, firsts, key_ref, read_ref, memories):
    key_dim = key_ref.shape[1] // heads
    total = None
    for first, memory_ref in zip(firsts, memories):
        count = memory_ref.shape[0] // key_dim
        start = first * key_dim
        start = start if isinstance(start, int) else pl.multiple_of(start, key_dim)
        keys = key_ref[:, pl.ds(start, count * key_dim)]
        reads = [
            dot(
                keys[:, h * key_dim : (h + 1) * key_dim],
                memory_ref[h * key_dim : (h + 1) * key_dim, :],
            )
            * key_dim ** (-0.5)
            for h in range(count)
        ]
        val_dim = memory_ref.shape[1]
        start = first * val_dim
        start = start if isinstance(start, int) else pl.multiple_of(start, val_dim)
        readout = jnp.concatenate(reads, axis=1).astype(BF16)
        piece = dot(readout, read_ref[pl.ds(start, count * val_dim), :])
        total = piece if total is None else total + piece
    return total


def own_first(share, offset, flip):
    place = lax.axis_index("space")
    return [(1 - place if flip else place) * share + offset]


def read_body(heads, firsts, begun, *refs):
    out_ref = refs[-1]
    key_ref, read_ref = refs[:2]
    memories = refs[2 + begun : -1]
    total = read_rows(heads, firsts(), key_ref, read_ref, memories)
    out_ref[...] = refs[2][...] + total if begun else total


def decode_body(width, heads, firsts, key_ref, read_ref, begun_ref, *refs):
    memories = refs[:-5]
    window_ref, conv_ref, up_ref, spread_ref, out_ref = refs[-5:]
    rows = window_ref.shape[0]
    tile_tok = rows - 2 * width
    total = read_rows(heads, firsts(), key_ref, read_ref, memories) + begun_ref[...]
    joined = (window_ref[...].astype(F32) + total).astype(BF16)
    summed = dot_on(joined[:tile_tok], conv_ref[0], 1, 1)
    for a in range(1, 3):
        summed = summed + dot_on(joined[a * width : a * width + tile_tok], conv_ref[a], 1, 1)
    chans = summed.shape[1] // 3
    columns = [summed[:, b * chans : (b + 1) * chans] for b in range(3)]
    col = lax.broadcasted_iota(jnp.int32, columns[0].shape, 0) % width
    zero = jnp.zeros_like(columns[0])
    left = jnp.where(col == 0, zero, pltpu.roll(columns[0], 1, 0))
    right = jnp.where(col == width - 1, zero, pltpu.roll(columns[2], tile_tok - 1, 0))
    mapped = jax.nn.gelu(left + columns[1] + right).astype(BF16)
    wide = tile_tok * UP
    lane = lax.broadcasted_iota(jnp.int32, (UP, UP, wide), 2)
    sub = lax.broadcasted_iota(jnp.int32, (UP, UP, wide), 1)
    hidden = dot(spread_ref[...], mapped).astype(BF16)
    pixels = dot_on(up_ref[...], hidden, 1, 1).reshape(UP, UP, wide)
    picked = jnp.sum(jnp.where((lane % UP) == sub, pixels, jnp.zeros_like(pixels)), axis=1)
    line = width * UP
    for i in range(tile_tok // width):
        out_ref[i * UP : (i + 1) * UP, :] = picked[:, i * line : (i + 1) * line]


def shards(
    frames_feat,
    prompt_labels,
    label_table,
    enc_qkv,
    enc_out,
    norm_gain,
    key_proj,
    value_proj,
    read_proj,
    decay,
    dec_conv,
    dec_up,
):
    _, tile_rows, width, dim = frames_feat.shape
    tile_tok = tile_rows * width
    bands, frames = lax.axis_size("space"), lax.axis_size("tm")
    tokens = tile_tok * bands
    heads = decay.shape[1]
    share = heads // bands
    key_dim, val_dim = key_proj.shape[1] // heads, value_proj.shape[1] // heads
    window_rows = tile_tok + 2 * width
    sds = pltpu.VMEM
    call = functools.partial(call_in, 2 * tokens * dim <= ON_CHIP)

    flat = frames_feat.reshape(tile_tok, dim)
    swap = [(0, 1), (1, 0)]
    if bands == 2:
        tiles = [flat, lax.ppermute(flat, "space", swap)]
        marks = [prompt_labels, lax.ppermute(prompt_labels, "space", swap)]
    else:
        tiles = [lax.all_gather(flat, "space", axis=0, tiled=True)]
        marks = [lax.all_gather(prompt_labels, "space", axis=0, tiled=True)]
    parts = len(tiles)
    tile = tiles[0].shape

    token = np.arange(tile[0])
    cell = (token // width // 2) * (width // 2) + token % width // 2
    pool = jnp.asarray((cell[None, :] == np.arange(tile[0] // 4)[:, None]) * 0.25, BF16)
    wide = np.arange(tile_tok * UP)
    row = wide // (width * UP) * width + wide % (width * UP) // UP
    spread = jnp.asarray(row[:, None] == np.arange(tile_tok)[None, :], BF16)

    gain = norm_gain.reshape(1, dim)
    loaded = [tiles[0], pool, enc_qkv, marks[0], label_table, gain, decay]
    tiles[0], pool, qkv, marks[0], table, gain, rates, queries, pairs = call(
        functools.partial(project_body, len(loaded)),
        (
            *[sds(x.shape, x.dtype) for x in loaded],
            sds(tile, BF16),
            sds((tile[0] // 4, 2 * dim), BF16),
        ),
        (pltpu.SemaphoreType.DMA((len(loaded),)),),
        [pl.ANY] * len(loaded),
        micros=1,
    )(*loaded)
    window, encoded, memory_in, turned = call(
        functools.partial(encode_body, width, parts),
        (
            sds((window_rows, dim), BF16),
            sds((tokens, dim), BF16),
            sds((tokens, dim), BF16),
            sds((share * key_dim, dim), BF16),
        ),
        (pltpu.VMEM((tokens + 2 * width, dim), BF16),),
        micros=2,
    )(
        *tiles,
        *marks,
        queries,
        pairs,
        pool,
        qkv,
        table,
        gain,
        enc_out,
        key_proj,
    )
    chains = 2 if share % 2 == 0 else 1
    group = share // chains
    rows = group * key_dim
    pay = sds((rows + carry_rows(group), val_dim), BF16)
    state = sds((rows, val_dim), F32)
    small = sds((group, val_dim), F32)
    held = [
        call(
            functools.partial(state_body, share, chain * group),
            (state, small, pay),
        )(encoded, memory_in, turned, value_proj, rates)
        for chain in range(chains)
    ]
    conv = dec_conv.swapaxes(2, 3)
    late = [read_proj, conv.reshape(conv.shape[0], -1, conv.shape[3]), dec_up.T, spread]
    held = [(total, product, (), payload) for total, product, payload in held]
    steps = (frames - 1).bit_length()
    for bit in range(steps):
        first, last = bit == 0, bit == steps - 1
        pairs = [(i, i ^ (1 << bit)) for i in range(frames) if i ^ (1 << bit) < frames]
        body = functools.partial(combine_body, bit, group, first, last)
        for chain, (total, product, carried, payload) in enumerate(held):
            arrived = lax.ppermute(payload, "tm", pairs)
            if last:
                held[chain] = (arrived, total, product, *carried)
                ahead = payload
            else:
                total, product, reach, prefix, payload = call(
                    body, (state, small, small, state, pay)
                )(arrived, total, product, *carried)
                held[chain] = (total, product, (reach, prefix), payload)

    key_rows, *late = call(
        keys_body,
        (sds((window_rows, heads * key_dim), BF16), *[sds(x.shape, BF16) for x in late]),
        (pltpu.VMEM(key_proj.shape, BF16), pltpu.SemaphoreType.DMA((5,))),
        [pltpu.VMEM] * 2 + [pl.ANY] * (1 + len(late)),
    )(window, ahead, key_proj, *late)
    read_out, *late = late

    def read(firsts, arrays, begun):
        body = functools.partial(read_body, heads, firsts, len(begun))
        return [call(body, sds((window_rows, dim), F32))(key_rows, read_out, *begun, *arrays)]

    order, begun, pieces = key_rows, [], []
    for chain, operands in enumerate(held):
        memory = call(body, sds((rows, val_dim), BF16))(*operands, order)
        offset = chain * group
        if bands == 2:
            pieces.append((functools.partial(own_first, share, offset, False), [memory]))
            other = lax.ppermute(memory, "space", swap)
            pieces.append((functools.partial(own_first, share, offset, True), [other]))
        else:
            every = lax.all_gather(memory, "space", axis=0)
            firsts = [band * share + offset for band in range(bands)]
            pieces.append((lambda firsts=firsts: firsts, [every[band] for band in range(bands)]))
        if chain < chains - 1:
            begun = read(*pieces.pop(0), begun)
            order = begun[0]
    for piece in pieces[:-1]:
        begun = read(*piece, begun)
    if not begun:
        begun = [jnp.zeros((window_rows, dim), F32)]
    firsts, arrays = pieces[-1]
    logits = call(
        functools.partial(decode_body, width, heads, firsts),
        jax.ShapeDtypeStruct((tile_rows * UP, width * UP), F32),
    )(key_rows, read_out, *begun, *arrays, window, *late)
    return logits[None]


def solution(mesh):
    return jax.shard_map(
        shards,
        mesh=mesh,
        in_specs=(
            P("tm", "space", None, None),
            P("space", None),
            P(),
            P(),
            P(),
            P(),
            P(),
            P(),
            P(),
            P("tm", None),
            P(),
            P(),
        ),
        out_specs=P("tm", "space", None),
        check_vma=False,
    )
```

time: 33.7 us -> 30 us (0.89)
  blocking collectives: 2.13 us -> 0 us
  waiting for transfers between devices: 7.48 us -> 6.62 us
  local copies, waits for them, and re-layouts: 0.8 us -> 0.02 us
    all_gather x1 -> x0, blocking collectives: 2.13 us -> none  [shards(): memory = lax.all_gather(memory, 'space', axis=0, tiled=True)]
    reshape x1 -> x0, local copies, waits for them, and re-layouts: 0.76 us -> none  [shards(): labels = prompt_labels.reshape(1, tile_tok)]
    ppermute x1 -> x3, starting transfers between devices: 0.02 us -> 0.63 us  [the longest x1 0.49 us: shards(): marks = [prompt_labels, lax.ppermute(prompt_labels, 'space', swap)]]
    ppermute x1 -> x3, waiting for transfers between devices: 1.14 us -> 0.58 us  [the longest x2 0.58 us: shards(): other = lax.ppermute(memory, 'space', swap)]
    ppermute x1, starting transfers between devices: 0.49 us -> 0.02 us  [shards(): tiles = [flat, lax.ppermute(flat, 'space', swap)]]
    ppermute x8, waiting for transfers between devices: 6.34 us -> 5.99 us  [shards(): arrived = lax.ppermute(payload, 'tm', pairs)]
    pallas_call x13 -> x17, Pallas kernels: 7.17 us -> 7.48 us  [run(): kernel(*[pltpu.with_memory_space_constraint(x, place) if place is held el...]
  transfers between devices with their start and end apart: 10 -> 12, of which waited for: 7 -> 6; matrix products, arithmetic and copies ran while one was open for 2% -> 0% of each run, Pallas kernels for 5% -> 15%
where the time goes in v4:
time: 30 us; the launch traced here: 29.8 us
  starting transfers between devices  15.5 us (52%)
  Pallas kernels  7.48 us (25%)
  waiting for transfers between devices  6.62 us (22%)
    ppermute x8, starting transfers between devices, shards(): arrived = lax.ppermute(payload, 'tm', pairs)  14.8 us
    pallas_call x17, Pallas kernels, run(): kernel(*[pltpu.with_memory_space_constraint(x, place) if place is held el...  7.48 us
    ppermute x8, waiting for transfers between devices, shards(): arrived = lax.ppermute(payload, 'tm', pairs)  5.99 us
  transfers between devices with their start and end apart: 12, of which 6 were waited for; matrix products, arithmetic and copies ran while one was open for 0% of the time, Pallas kernels for 15%

profile of v4, /device:TPU:0, one launch (start us, length us, event | category | flops | bytes accessed | tf_op | source)
XLA Modules:
  0.0 29.8 jit_solution(5767691213373789775)
XLA Ops:
  0.0 0.5 %collective-permute-start.1 = (s32[2,64]{1,0:T(2,128)}, s32[2,64]{1,0:T(2,128)S(1)}, u32[]{:S(2)}, u32[]{:S(2)}) collective-permute-start(s32[2,64]{1,0:T(2,128)} %refs_3_.2), channel_id=1, source_target_pairs={{0,1},{1,0},{2,3},{3,2},{4,5},{5,4},{6,7},{7,6},{8,9},{9,8},{10,11... | collective-permute-start | bytes 1544 | tf_op jit(solution)/shard_map/ppermute | solution.py:345
  0.5 1.4 %shard_map.136 = (bf16[128,256]{1,0:T(8,128)(2,1)S(1)}, bf16[32,128]{1,0:T(8,128)(2,1)S(1)}, bf16[256,768]{1,0:T(8,128)(2,1)S(1)}, s32[2,64]{1,0:T(2,128)S(1)}, ...) custom-call(bf16[128,256]{1,0:T(8,128)(2,1)} %bitcast.10, ...), custom_call_target="tpu_custom_call" | custom-call | flops 1000000000 | tf_op jit(solution)/shard_map/pallas_call | solution.py:51
  2.0 1.1 %shard_map.137 = (bf16[256,256]{1,0:T(8,128)(2,1)S(1)}, bf16[256,256]{1,0:T(8,128)(2,1)S(1)}, bf16[256,256]{1,0:T(8,128)(2,1)S(1)}, bf16[512,256]{1,0:T(8,128)(2,1)S(1)}) custom-call(bf16[128,256]{1,0:T(8,128)(2,1)S(1)} %get-tuple-element.59.refs_0_, bf16[128,256]{1,0:T(8,128)(2,1)S(1)} %collective-permute-done.refs_1_, ...), custom_call_target="tpu_custom_call" | custom-call | flops 2000000000 | tf_op jit(solution)/shard_map/pallas_call | solution.py:51
  3.1 0.4 %shard_map.143 = (f32[256,128]{1,0:T(8,128)S(1)}, f32[2,128]{1,0:T(2,128)S(1)}, bf16[272,128]{1,0:T(8,128)(2,1)S(1)}) custom-call(bf16[256,256]{1,0:T(8,128)(2,1)S(1)} %get-tuple-element.68.encoded_ref, bf16[256,256]{1,0:T(8,128)(2,1)S(1)} %get-tuple-element.69.memory_ref, bf16[512,256]{1,0:T(8,128)(2,1)S(1)} %get-tuple-element.70.turned_ref, ...), custom_call_target="tpu_custom_call" | custom-call | tf_op jit(solution)/shard_map/pallas_call | solution.py:51
  3.5 3.0 %collective-permute-start.5 = (bf16[272,128]{1,0:T(8,128)(2,1)S(1)}, bf16[272,128]{1,0:T(8,128)(2,1)S(1)}, u32[]{:S(2)}, u32[]{:S(2)}) collective-permute-start(bf16[272,128]{1,0:T(8,128)(2,1)S(1)} %get-tuple-element.88), channel_id=1, source_target_pairs={{0,2},{2,0},{4,6},{6,4},{8,10},{10,8},{12,14},{14,12},{16,18},{18,... | collective-permute-start | bytes 208904 | tf_op jit(solution)/shard_map/ppermute | solution.py:416
  6.5 0.4 %shard_map.138 = (f32[256,128]{1,0:T(8,128)S(1)}, f32[2,128]{1,0:T(2,128)S(1)}, bf16[272,128]{1,0:T(8,128)(2,1)S(1)}) custom-call(bf16[256,256]{1,0:T(8,128)(2,1)S(1)} %get-tuple-element.68.encoded_ref, bf16[256,256]{1,0:T(8,128)(2,1)S(1)} %get-tuple-element.69.memory_ref, bf16[512,256]{1,0:T(8,128)(2,1)S(1)} %get-tuple-element.70.turned_ref, ...), custom_call_target="tpu_custom_call" | custom-call | tf_op jit(solution)/shard_map/pallas_call | solution.py:51
  6.9 0.1 collective-permute-start.2
  7.0 1.9 %collective-permute-done.5.recv_ref = bf16[272,128]{1,0:T(8,128)(2,1)S(1)} collective-permute-done((bf16[272,128]{1,0:T(8,128)(2,1)S(1)}, bf16[272,128]{1,0:T(8,128)(2,1)S(1)}, u32[]{:S(2)}, u32[]{:S(2)}) %collective-permute-start.5) | collective-permute-done | bytes 69664 | tf_op jit(solution)/shard_map/ppermute | solution.py:416
  8.9 2.0 %collective-permute-start.6 = (bf16[272,128]{1,0:T(8,128)(2,1)S(1)}, bf16[272,128]{1,0:T(8,128)(2,1)S(1)}, u32[]{:S(2)}, u32[]{:S(2)}) collective-permute-start(bf16[272,128]{1,0:T(8,128)(2,1)S(1)} %get-tuple-element.91), channel_id=1, source_target_pairs={{0,4},{2,6},{4,0},{6,2},{8,12},{10,14},{12,8},{14,10},{16,20},{18,... | collective-permute-start | bytes 208904 | tf_op jit(solution)/shard_map/ppermute | solution.py:416
  10.9 0.3 %collective-permute-done.2.recv_ref = bf16[272,128]{1,0:T(8,128)(2,1)S(1)} collective-permute-done((bf16[272,128]{1,0:T(8,128)(2,1)S(1)}, bf16[272,128]{1,0:T(8,128)(2,1)S(1)}, u32[]{:S(2)}, u32[]{:S(2)}) %collective-permute-start.2) | collective-permute-done | bytes 69664 | tf_op jit(solution)/shard_map/ppermute | solution.py:416
  11.3 1.6 %collective-permute-start.3 = (bf16[272,128]{1,0:T(8,128)(2,1)S(1)}, bf16[272,128]{1,0:T(8,128)(2,1)S(1)}, u32[]{:S(2)}, u32[]{:S(2)}) collective-permute-start(bf16[272,128]{1,0:T(8,128)(2,1)S(1)} %get-tuple-element.75), channel_id=1, source_target_pairs={{0,4},{2,6},{4,0},{6,2},{8,12},{10,14},{12,8},{14,10},{16,20},{18,... | collective-permute-start | bytes 208904 | tf_op jit(solution)/shard_map/ppermute | solution.py:416
  12.9 1.1 %collective-permute-done.6.recv_ref = bf16[272,128]{1,0:T(8,128)(2,1)S(1)} collective-permute-done((bf16[272,128]{1,0:T(8,128)(2,1)S(1)}, bf16[272,128]{1,0:T(8,128)(2,1)S(1)}, u32[]{:S(2)}, u32[]{:S(2)}) %collective-permute-start.6) | collective-permute-done | bytes 69664 | tf_op jit(solution)/shard_map/ppermute | solution.py:416
  14.0 1.7 %collective-permute-start.7 = (bf16[272,128]{1,0:T(8,128)(2,1)S(1)}, bf16[272,128]{1,0:T(8,128)(2,1)S(1)}, u32[]{:S(2)}, u32[]{:S(2)}) collective-permute-start(bf16[272,128]{1,0:T(8,128)(2,1)S(1)} %get-tuple-element.96), channel_id=1, source_target_pairs={{0,8},{2,10},{4,12},{6,14},{8,0},{10,2},{12,4},{14,6},{16,24},{18,... | collective-permute-start | bytes 208904 | tf_op jit(solution)/shard_map/ppermute | solution.py:416
  15.8 1.6 %collective-permute-start.4 = (bf16[272,128]{1,0:T(8,128)(2,1)S(1)}, bf16[272,128]{1,0:T(8,128)(2,1)S(1)}, u32[]{:S(2)}, u32[]{:S(2)}) collective-permute-start(bf16[272,128]{1,0:T(8,128)(2,1)S(1)} %get-tuple-element.80), channel_id=1, source_target_pairs={{0,8},{2,10},{4,12},{6,14},{8,0},{10,2},{12,4},{14,6},{16,24},{18,... | collective-permute-start | bytes 208904 | tf_op jit(solution)/shard_map/ppermute | solution.py:416
  17.4 1.0 %collective-permute-done.7.recv_ref = bf16[272,128]{1,0:T(8,128)(2,1)S(1)} collective-permute-done((bf16[272,128]{1,0:T(8,128)(2,1)S(1)}, bf16[272,128]{1,0:T(8,128)(2,1)S(1)}, u32[]{:S(2)}, u32[]{:S(2)}) %collective-permute-start.7) | collective-permute-done | bytes 69664 | tf_op jit(solution)/shard_map/ppermute | solution.py:416
  18.5 3.1 %collective-permute-start.8 = (bf16[272,128]{1,0:T(8,128)(2,1)S(1)}, bf16[272,128]{1,0:T(8,128)(2,1)S(1)}, u32[]{:S(2)}, u32[]{:S(2)}) collective-permute-start(bf16[272,128]{1,0:T(8,128)(2,1)S(1)} %get-tuple-element.101), channel_id=1, source_target_pairs={{0,16},{2,18},{4,20},{6,22},{8,24},{10,26},{12,28},{14,30},{16,0},... | collective-permute-start | bytes 208904 | tf_op jit(solution)/shard_map/ppermute | solution.py:416
  21.6 1.8 %collective-permute-start.10 = (bf16[272,128]{1,0:T(8,128)(2,1)S(1)}, bf16[272,128]{1,0:T(8,128)(2,1)S(1)}, u32[]{:S(2)}, u32[]{:S(2)}) collective-permute-start(bf16[272,128]{1,0:T(8,128)(2,1)S(1)} %get-tuple-element.85.after), channel_id=1, source_target_pairs={{0,16},{2,18},{4,20},{6,22},{8,24},{10,26},{12,28},{14,30},{16,0},... | collective-permute-start | bytes 208904 | tf_op jit(solution)/shard_map/ppermute | solution.py:416
  23.4 1.4 %shard_map.142 = (bf16[256,1024]{1,0:T(8,128)(2,1)S(1)}, bf16[1024,256]{1,0:T(8,128)(2,1)S(1)}, bf16[3,192,256]{2,1,0:T(8,128)(2,1)S(1)}, bf16[16,64]{1,0:T(8,128)(2,1)S(1)}, bf16[512,128]{1,0:T(8,128)(2,1)S(1)}) custom-call(bf16[256,256]{1,0:T(8,128)(2,1)S(1)} %get-tuple-element.67.window_ref.refs_1_, bf16[272,128]{1,0:T(8,128)(2,1)S(1)} %get-tuple-element.85.after, ...), custom_call_target="tpu_custom_call" | custom-call | tf_op jit(solution)/shard_map/pallas_call | solution.py:51
  24.9 0.3 %shard_map.148.refs_2_ = f32[256,256]{1,0:T(8,128)S(1)} custom-call(bf16[256,1024]{1,0:T(8,128)(2,1)S(1)} %get-tuple-element.86.refs_2_.refs_0_.key_ref, bf16[1024,256]{1,0:T(8,128)(2,1)S(1)} %get-tuple-element.87.refs_1_.read_ref, bf16[256,128]{1,0:T(8,128)(2,1)S(1)} %shard_map.147.refs_2_), custom_call_target="tpu_custom_call" | custom-call | tf_op jit(solution)/shard_map/pallas_call | solution.py:51
  25.2 1.7 %collective-permute-done.10.recv_ref = bf16[272,128]{1,0:T(8,128)(2,1)S(1)} collective-permute-done((bf16[272,128]{1,0:T(8,128)(2,1)S(1)}, bf16[272,128]{1,0:T(8,128)(2,1)S(1)}, u32[]{:S(2)}, u32[]{:S(2)}) %collective-permute-start.10) | collective-permute-done | bytes 69664 | tf_op jit(solution)/shard_map/ppermute | solution.py:416
  27.0 0.3 %shard_map.149.refs_2_ = f32[256,256]{1,0:T(8,128)S(1)} custom-call(bf16[256,1024]{1,0:T(8,128)(2,1)S(1)} %get-tuple-element.86.refs_2_.refs_0_.key_ref, bf16[1024,256]{1,0:T(8,128)(2,1)S(1)} %get-tuple-element.87.refs_1_.read_ref, f32[256,256]{1,0:T(8,128)S(1)} %shard_map.148.refs_2_, bf16[256,128]{1,0:T(8,128)(2,1)S(1)} %collective-permute-done.9.refs_3_), custom_call_target="tpu_custom_call" | custom-call | tf_op jit(solution)/shard_map/pallas_call | solution.py:51
  27.3 0.3 %shard_map.151.begun_ref = f32[256,256]{1,0:T(8,128)S(1)} custom-call(bf16[256,1024]{1,0:T(8,128)(2,1)S(1)} %get-tuple-element.86.refs_2_.refs_0_.key_ref, bf16[1024,256]{1,0:T(8,128)(2,1)S(1)} %get-tuple-element.87.refs_1_.read_ref, f32[256,256]{1,0:T(8,128)S(1)} %shard_map.149.refs_2_, bf16[256,128]{1,0:T(8,128)(2,1)S(1)} %shard_map.150.refs_3_), custom_call_target="tpu_custom_call" | custom-call | tf_op jit(solution)/shard_map/pallas_call | solution.py:51
  27.6 0.6 %collective-permute-done.11.refs_0_ = bf16[256,128]{1,0:T(8,128)(2,1)S(1)} collective-permute-done((bf16[256,128]{1,0:T(8,128)(2,1)S(1)}, bf16[256,128]{1,0:T(8,128)(2,1)S(1)}, u32[]{:S(2)}, u32[]{:S(2)}) %collective-permute-start.11) | collective-permute-done | bytes 65568 | tf_op jit(solution)/shard_map/ppermute | solution.py:444
  28.2 1.6 %shard_map.152 = f32[8,256]{1,0:T(8,128)} custom-call(bf16[256,1024]{1,0:T(8,128)(2,1)S(1)} %get-tuple-element.86.refs_2_.refs_0_.key_ref, bf16[1024,256]{1,0:T(8,128)(2,1)S(1)} %get-tuple-element.87.refs_1_.read_ref, f32[256,256]{1,0:T(8,128)S(1)} %shard_map.151.begun_ref, bf16[256,128]{1,0:T(8,128)(2,1)S(1)} %collective-permute-done.11.refs_0_, ...), custom_call_target="tpu_custom_call" | custom-call | tf_op jit(solution)/shard_map/pallas_call | solution.py:51
  (27 shorter events, 0.6 us)
Async XLA Ops:
  0.0 1.9 %collective-permute-start.1 = (s32[2,64]{1,0:T(2,128)}, s32[2,64]{1,0:T(2,128)S(1)}, u32[]{:S(2)}, u32[]{:S(2)}) collective-permute-start(s32[2,64]{1,0:T(2,128)} %refs_3_.2), channel_id=1, source_target_pairs={{0,1},{1,0},{2,3},{3,2},{4,5},{5,4},{6,7},{7,6},{8,9},{9,8},{10,11... | collective-permute-start | bytes 1544 | tf_op jit(solution)/shard_map/ppermute | solution.py:345
  0.5 1.5 %collective-permute-start = (bf16[128,256]{1,0:T(8,128)(2,1)}, bf16[128,256]{1,0:T(8,128)(2,1)S(1)}, u32[]{:S(2)}, u32[]{:S(2)}) collective-permute-start(bf16[128,256]{1,0:T(8,128)(2,1)} %bitcast.9), channel_id=1, source_target_pairs={{0,1},{1,0},{2,3},{3,2},{4,5},{5,4},{6,7},{7,6},{8,9},{9,8},{10,11... | collective-permute-start | bytes 196616 | tf_op jit(solution)/shard_map/ppermute | solution.py:344
  0.5 1.4 %copy-start.1 = (bf16[256,1024]{1,0:T(8,128)(2,1)S(1)}, bf16[256,1024]{1,0:T(8,128)(2,1)}, u32[]{:S(2)}) copy-start(bf16[256,1024]{1,0:T(8,128)(2,1)} %key_hbm.1) | copy-start | bytes 1572868
  0.5 1.5 %copy-start.4 = (bf16[256,256]{1,0:T(8,128)(2,1)S(1)}, bf16[256,256]{1,0:T(8,128)(2,1)}, u32[]{:S(2)}) copy-start(bf16[256,256]{1,0:T(8,128)(2,1)} %refs_10_.1) | copy-start | bytes 393220
  2.0 1.1 %copy-start = (bf16[256,1024]{1,0:T(8,128)(2,1)S(1)}, bf16[256,1024]{1,0:T(8,128)(2,1)}, u32[]{:S(2)}) copy-start(bf16[256,1024]{1,0:T(8,128)(2,1)} %value_ref.3) | copy-start | bytes 1572868
  3.0 20.3 %copy-start.2 = (bf16[256,256]{1,0:T(8,128)(2,1)}, bf16[256,256]{1,0:T(8,128)(2,1)S(1)}, u32[]{:S(2)}) copy-start(bf16[256,256]{1,0:T(8,128)(2,1)S(1)} %get-tuple-element.67.window_ref.refs_1_) | copy-start | bytes 393220
  3.5 5.4 %collective-permute-start.5 = (bf16[272,128]{1,0:T(8,128)(2,1)S(1)}, bf16[272,128]{1,0:T(8,128)(2,1)S(1)}, u32[]{:S(2)}, u32[]{:S(2)}) collective-permute-start(bf16[272,128]{1,0:T(8,128)(2,1)S(1)} %get-tuple-element.88), channel_id=1, source_target_pairs={{0,2},{2,0},{4,6},{6,4},{8,10},{10,8},{12,14},{14,12},{16,18},{18,... | collective-permute-start | bytes 208904 | tf_op jit(solution)/shard_map/ppermute | solution.py:416
  6.9 4.4 %collective-permute-start.2 = (bf16[272,128]{1,0:T(8,128)(2,1)S(1)}, bf16[272,128]{1,0:T(8,128)(2,1)S(1)}, u32[]{:S(2)}, u32[]{:S(2)}) collective-permute-start(bf16[272,128]{1,0:T(8,128)(2,1)S(1)} %get-tuple-element.72), channel_id=1, source_target_pairs={{0,2},{2,0},{4,6},{6,4},{8,10},{10,8},{12,14},{14,12},{16,18},{18,... | collective-permute-start | bytes 208904 | tf_op jit(solution)/shard_map/ppermute | solution.py:416
  8.9 5.1 %collective-permute-start.6 = (bf16[272,128]{1,0:T(8,128)(2,1)S(1)}, bf16[272,128]{1,0:T(8,128)(2,1)S(1)}, u32[]{:S(2)}, u32[]{:S(2)}) collective-permute-start(bf16[272,128]{1,0:T(8,128)(2,1)S(1)} %get-tuple-element.91), channel_id=1, source_target_pairs={{0,4},{2,6},{4,0},{6,2},{8,12},{10,14},{12,8},{14,10},{16,20},{18,... | collective-permute-start | bytes 208904 | tf_op jit(solution)/shard_map/ppermute | solution.py:416
  11.3 4.5 %collective-permute-start.3 = (bf16[272,128]{1,0:T(8,128)(2,1)S(1)}, bf16[272,128]{1,0:T(8,128)(2,1)S(1)}, u32[]{:S(2)}, u32[]{:S(2)}) collective-permute-start(bf16[272,128]{1,0:T(8,128)(2,1)S(1)} %get-tuple-element.75), channel_id=1, source_target_pairs={{0,4},{2,6},{4,0},{6,2},{8,12},{10,14},{12,8},{14,10},{16,20},{18,... | collective-permute-start | bytes 208904 | tf_op jit(solution)/shard_map/ppermute | solution.py:416
  14.0 4.4 %collective-permute-start.7 = (bf16[272,128]{1,0:T(8,128)(2,1)S(1)}, bf16[272,128]{1,0:T(8,128)(2,1)S(1)}, u32[]{:S(2)}, u32[]{:S(2)}) collective-permute-start(bf16[272,128]{1,0:T(8,128)(2,1)S(1)} %get-tuple-element.96), channel_id=1, source_target_pairs={{0,8},{2,10},{4,12},{6,14},{8,0},{10,2},{12,4},{14,6},{16,24},{18,... | collective-permute-start | bytes 208904 | tf_op jit(solution)/shard_map/ppermute | solution.py:416
  15.8 5.7 %collective-permute-start.4 = (bf16[272,128]{1,0:T(8,128)(2,1)S(1)}, bf16[272,128]{1,0:T(8,128)(2,1)S(1)}, u32[]{:S(2)}, u32[]{:S(2)}) collective-permute-start(bf16[272,128]{1,0:T(8,128)(2,1)S(1)} %get-tuple-element.80), channel_id=1, source_target_pairs={{0,8},{2,10},{4,12},{6,14},{8,0},{10,2},{12,4},{14,6},{16,24},{18,... | collective-permute-start | bytes 208904 | tf_op jit(solution)/shard_map/ppermute | solution.py:416
  18.5 6.3 %collective-permute-start.8 = (bf16[272,128]{1,0:T(8,128)(2,1)S(1)}, bf16[272,128]{1,0:T(8,128)(2,1)S(1)}, u32[]{:S(2)}, u32[]{:S(2)}) collective-permute-start(bf16[272,128]{1,0:T(8,128)(2,1)S(1)} %get-tuple-element.101), channel_id=1, source_target_pairs={{0,16},{2,18},{4,20},{6,22},{8,24},{10,26},{12,28},{14,30},{16,0},... | collective-permute-start | bytes 208904 | tf_op jit(solution)/shard_map/ppermute | solution.py:416
  21.6 5.3 %collective-permute-start.10 = (bf16[272,128]{1,0:T(8,128)(2,1)S(1)}, bf16[272,128]{1,0:T(8,128)(2,1)S(1)}, u32[]{:S(2)}, u32[]{:S(2)}) collective-permute-start(bf16[272,128]{1,0:T(8,128)(2,1)S(1)} %get-tuple-element.85.after), channel_id=1, source_target_pairs={{0,16},{2,18},{4,20},{6,22},{8,24},{10,26},{12,28},{14,30},{16,0},... | collective-permute-start | bytes 208904 | tf_op jit(solution)/shard_map/ppermute | solution.py:416
  24.8 2.2 %collective-permute-start.9 = (bf16[256,128]{1,0:T(8,128)(2,1)S(1)}, bf16[256,128]{1,0:T(8,128)(2,1)S(1)}, u32[]{:S(2)}, u32[]{:S(2)}) collective-permute-start(bf16[256,128]{1,0:T(8,128)(2,1)S(1)} %shard_map.147.refs_2_), channel_id=1, source_target_pairs={{0,1},{1,0},{2,3},{3,2},{4,5},{5,4},{6,7},{7,6},{8,9},{9,8},{10,11... | collective-permute-start | bytes 196616 | tf_op jit(solution)/shard_map/ppermute | solution.py:444
  26.9 1.3 %collective-permute-start.11 = (bf16[256,128]{1,0:T(8,128)(2,1)S(1)}, bf16[256,128]{1,0:T(8,128)(2,1)S(1)}, u32[]{:S(2)}, u32[]{:S(2)}) collective-permute-start(bf16[256,128]{1,0:T(8,128)(2,1)S(1)} %shard_map.150.refs_3_), channel_id=1, source_target_pairs={{0,1},{1,0},{2,3},{3,2},{4,5},{5,4},{6,7},{7,6},{8,9},{9,8},{10,11... | collective-permute-start | bytes 196616 | tf_op jit(solution)/shard_map/ppermute | solution.py:444
  27.3 0.9 %copy-start.3 = (bf16[256,256]{1,0:T(8,128)(2,1)S(1)}, bf16[256,256]{1,0:T(8,128)(2,1)}, u32[]{:S(2)}) copy-start(bf16[256,256]{1,0:T(8,128)(2,1)} %copy-done.2) | copy-start | bytes 393220

commit v5 on v4

--- a/solution.py
+++ b/solution.py
@@ -12,6 +12,8 @@
 UP = 4
 LANES = 128
 ON_CHIP = 1 << 18
+SIZES = [2, 2]
+CROSSED_BITS = 1
 EPSILON = 1e-06
 F32 = jnp.float32
 BF16 = jnp.bfloat16
@@ -58,6 +60,18 @@
     return run
 
 
+def own_band(crossed):
+    band = lax.axis_index("space")
+    if crossed:
+        bits = lax.axis_index("tm") & CROSSED_BITS
+        shift = 16
+        while shift:
+            bits = bits ^ (bits >> shift)
+            shift //= 2
+        band = (band + bits) & 1
+    return band
+
+
 def carry_rows(share):
     return -(-3 * share // 16) * 16
 
@@ -73,8 +87,10 @@
     for h in range(share):
         rows = slice(h * key_dim, (h + 1) * key_dim)
         pay_ref[rows, :] = totals[h].astype(BF16)
+    tail = pay_ref.shape[0] - share * key_dim
+    if tail == 0:
+        return
     parts = split(product)
-    tail = carry_rows(share)
     if tail > 3 * share:
         parts.append(jnp.zeros((tail - 3 * share, product.shape[1]), F32))
     pay_ref[share * key_dim :, :] = jnp.concatenate(parts, axis=0).astype(BF16)
@@ -158,11 +174,12 @@
         padded[pl.ds(spot, rows), :] = encoded[p * rows : (p + 1) * rows]
     window_ref[...] = padded[pl.ds(pl.multiple_of(place * tile_tok, width), window_rows), :]
     cols = turned_ref.shape[0]
-    turned_ref[...] = key_ref[:, pl.ds(pl.multiple_of(place * cols, LANES), cols)].T
+    start = pl.multiple_of(own_band(parts == 2) * cols, LANES)
+    turned_ref[...] = key_ref[:, pl.ds(start, cols)].T
 
 
 def state_body(
-    share, first_head, encoded_ref, memory_ref, turned_ref, value_ref, decay_ref, *out_refs
+    share, crossed, first_head, encoded_ref, memory_ref, turned_ref, value_ref, decay_ref, *out_refs
 ):
     state_ref, product_ref, pay_ref = out_refs
     heads = product_ref.shape[0]
@@ -170,7 +187,7 @@
     val_dim = state_ref.shape[1]
     tokens = encoded_ref.shape[0]
     cols = slice(first_head * key_dim, (first_head + heads) * key_dim)
-    start = lax.axis_index("space") * share + first_head
+    start = own_band(crossed) * share + first_head
     val_cols = pl.ds(pl.multiple_of(start * val_dim, val_dim), heads * val_dim)
     keys = dot_on(turned_ref[cols, :], encoded_ref[...], 1, 1).astype(BF16)
     values = dot(memory_ref[...], value_ref[:, val_cols]).astype(BF16)
@@ -200,11 +217,12 @@
     is_upper = jnp.full(product_ref.shape, upper, jnp.int32) == 1
     product = product_ref[...]
     reach = product if first else reach_ref[...]
-    tail = recv_ref[rows:, :].astype(F32)
-    got = tail[:share] + tail[share : 2 * share] + tail[2 * share : 3 * share]
-    ones = jnp.ones_like(product)
-    on_got = jnp.where(is_upper, product, ones)
-    on_own = jnp.where(is_upper, ones, got)
+    if not last:
+        tail = recv_ref[rows:, :].astype(F32)
+        got = tail[:share] + tail[share : 2 * share] + tail[2 * share : 3 * share]
+        ones = jnp.ones_like(product)
+        on_got = jnp.where(is_upper, product, ones)
+        on_own = jnp.where(is_upper, ones, got)
     on_prefix = jnp.where(is_upper, reach, jnp.zeros_like(product))
     totals = []
     for h in range(share):
@@ -273,7 +291,7 @@
 
 
 def own_first(share, offset, flip):
-    place = lax.axis_index("space")
+    place = own_band(True)
     return [(1 - place if flip else place) * share + offset]
 
 
@@ -305,8 +323,9 @@
     wide = tile_tok * UP
     lane = lax.broadcasted_iota(jnp.int32, (UP, UP, wide), 2)
     sub = lax.broadcasted_iota(jnp.int32, (UP, UP, wide), 1)
-    hidden = dot(spread_ref[...], mapped).astype(BF16)
-    pixels = dot_on(up_ref[...], hidden, 1, 1).reshape(UP, UP, wide)
+    small = jnp.concatenate(split(dot_on(up_ref[...], mapped, 1, 1)), axis=0).astype(BF16)
+    parts = dot(small, spread_ref[...]).reshape(3, UP, UP, wide)
+    pixels = parts[0] + parts[1] + parts[2]
     picked = jnp.sum(jnp.where((lane % UP) == sub, pixels, jnp.zeros_like(pixels)), axis=1)
     line = width * UP
     for i in range(tile_tok // width):
@@ -354,7 +373,7 @@
     pool = jnp.asarray((cell[None, :] == np.arange(tile[0] // 4)[:, None]) * 0.25, BF16)
     wide = np.arange(tile_tok * UP)
     row = wide // (width * UP) * width + wide % (width * UP) // UP
-    spread = jnp.asarray(row[:, None] == np.arange(tile_tok)[None, :], BF16)
+    spread = jnp.asarray(row[None, :] == np.arange(tile_tok)[:, None], BF16)
 
     gain = norm_gain.reshape(1, dim)
     loaded = [tiles[0], pool, enc_qkv, marks[0], label_table, gain, decay]
@@ -391,33 +410,43 @@
         enc_out,
         key_proj,
     )
-    chains = 2 if share % 2 == 0 else 1
-    group = share // chains
-    rows = group * key_dim
-    pay = sds((rows + carry_rows(group), val_dim), BF16)
-    state = sds((rows, val_dim), F32)
-    small = sds((group, val_dim), F32)
-    held = [
-        call(
-            functools.partial(state_body, share, chain * group),
-            (state, small, pay),
+    crossed = bands == 2
+    sizes = SIZES if sum(SIZES) == share else [share]
+    chains = len(sizes)
+    offsets = [sum(sizes[:chain]) for chain in range(chains)]
+
+    def kinds(group, carry=True):
+        rows = group * key_dim
+        pay = sds((rows + carry * carry_rows(group), val_dim), BF16)
+        return sds((rows, val_dim), F32), sds((group, val_dim), F32), pay
+
+    held = []
+    for offset, group in zip(offsets, sizes):
+        total, product, payload = call(
+            functools.partial(state_body, share, crossed, offset), kinds(group)
         )(encoded, memory_in, turned, value_proj, rates)
-        for chain in range(chains)
-    ]
+        held.append((total, product, (), payload))
     conv = dec_conv.swapaxes(2, 3)
     late = [read_proj, conv.reshape(conv.shape[0], -1, conv.shape[3]), dec_up.T, spread]
-    held = [(total, product, (), payload) for total, product, payload in held]
     steps = (frames - 1).bit_length()
     for bit in range(steps):
         first, last = bit == 0, bit == steps - 1
-        pairs = [(i, i ^ (1 << bit)) for i in range(frames) if i ^ (1 << bit) < frames]
-        body = functools.partial(combine_body, bit, group, first, last)
+        mask = 1 << bit
+        turn = crossed and (mask & CROSSED_BITS).bit_count() % 2
+        pairs = [
+            (i * bands + c, (i ^ mask) * bands + (1 - c if turn else c))
+            for i in range(frames)
+            for c in range(bands)
+            if i ^ mask < frames
+        ]
         for chain, (total, product, carried, payload) in enumerate(held):
-            arrived = lax.ppermute(payload, "tm", pairs)
+            arrived = lax.ppermute(payload, ("tm", "space"), pairs)
             if last:
                 held[chain] = (arrived, total, product, *carried)
                 ahead = payload
             else:
+                state, small, pay = kinds(sizes[chain], bit < steps - 2)
+                body = functools.partial(combine_body, bit, sizes[chain], first, False)
                 total, product, reach, prefix, payload = call(
                     body, (state, small, small, state, pay)
                 )(arrived, total, product, *carried)
@@ -437,8 +466,9 @@
 
     order, begun, pieces = key_rows, [], []
     for chain, operands in enumerate(held):
-        memory = call(body, sds((rows, val_dim), BF16))(*operands, order)
-        offset = chain * group
+        body = functools.partial(combine_body, steps - 1, sizes[chain], steps == 1, True)
+        memory = call(body, sds((sizes[chain] * key_dim, val_dim), BF16))(*operands, order)
+        offset = offsets[chain]
         if bands == 2:
             pieces.append((functools.partial(own_first, share, offset, False), [memory]))
             other = lax.ppermute(memory, "space", swap)

time: 30 us -> 29.6 us (0.987)
  starting transfers between devices: 15.5 us -> 14.4 us
  waiting for transfers between devices: 6.62 us -> 7.3 us
    ppermute x8, starting transfers between devices: 14.8 us -> 13.7 us  [shards(): arrived = lax.ppermute(payload, ('tm', 'space'), pairs)]
    ppermute x8, waiting for transfers between devices: 5.99 us -> 6.68 us  [shards(): arrived = lax.ppermute(payload, ('tm', 'space'), pairs)]
where the time goes in v5:
time: 29.6 us; the launch traced here: 29.3 us
  starting transfers between devices  14.4 us (49%)
  Pallas kernels  7.46 us (25%)
  waiting for transfers between devices  7.3 us (25%)
    ppermute x8, starting transfers between devices, shards(): arrived = lax.ppermute(payload, ('tm', 'space'), pairs)  13.7 us
    pallas_call x17, Pallas kernels, run(): kernel(*[pltpu.with_memory_space_constraint(x, place) if place is held el...  7.46 us
    ppermute x8, waiting for transfers between devices, shards(): arrived = lax.ppermute(payload, ('tm', 'space'), pairs)  6.68 us
  transfers between devices with their start and end apart: 12, of which 6 were waited for; matrix products, arithmetic and copies ran while one was open for 0% of the time, Pallas kernels for 15%

profile of v5, /device:TPU:0, one launch (start us, length us, event | category | flops | bytes accessed | tf_op | source)
XLA Modules:
  0.0 29.3 jit_solution(10541919306018814820)
XLA Ops:
  0.0 0.5 %collective-permute-start.1 = (s32[2,64]{1,0:T(2,128)}, s32[2,64]{1,0:T(2,128)S(1)}, u32[]{:S(2)}, u32[]{:S(2)}) collective-permute-start(s32[2,64]{1,0:T(2,128)} %refs_3_.2), channel_id=1, source_target_pairs={{0,1},{1,0},{2,3},{3,2},{4,5},{5,4},{6,7},{7,6},{8,9},{9,8},{10,11... | collective-permute-start | bytes 1544 | tf_op jit(solution)/shard_map/ppermute | solution.py:364
  0.5 1.4 %shard_map.136 = (bf16[128,256]{1,0:T(8,128)(2,1)S(1)}, bf16[32,128]{1,0:T(8,128)(2,1)S(1)}, bf16[256,768]{1,0:T(8,128)(2,1)S(1)}, s32[2,64]{1,0:T(2,128)S(1)}, ...) custom-call(bf16[128,256]{1,0:T(8,128)(2,1)} %bitcast.10, ...), custom_call_target="tpu_custom_call" | custom-call | flops 1000000000 | tf_op jit(solution)/shard_map/pallas_call | solution.py:53
  2.0 1.1 %shard_map.137 = (bf16[256,256]{1,0:T(8,128)(2,1)S(1)}, bf16[256,256]{1,0:T(8,128)(2,1)S(1)}, bf16[256,256]{1,0:T(8,128)(2,1)S(1)}, bf16[512,256]{1,0:T(8,128)(2,1)S(1)}) custom-call(bf16[128,256]{1,0:T(8,128)(2,1)S(1)} %get-tuple-element.59.refs_0_, bf16[128,256]{1,0:T(8,128)(2,1)S(1)} %collective-permute-done.refs_1_, ...), custom_call_target="tpu_custom_call" | custom-call | flops 2000000000 | tf_op jit(solution)/shard_map/pallas_call | solution.py:53
  3.1 0.4 %shard_map.143 = (f32[256,128]{1,0:T(8,128)S(1)}, f32[2,128]{1,0:T(2,128)S(1)}, bf16[272,128]{1,0:T(8,128)(2,1)S(1)}) custom-call(bf16[256,256]{1,0:T(8,128)(2,1)S(1)} %get-tuple-element.68.encoded_ref, bf16[256,256]{1,0:T(8,128)(2,1)S(1)} %get-tuple-element.69.memory_ref, bf16[512,256]{1,0:T(8,128)(2,1)S(1)} %get-tuple-element.70.turned_ref, ...), custom_call_target="tpu_custom_call" | custom-call | tf_op jit(solution)/shard_map/pallas_call | solution.py:53
  3.5 2.7 %collective-permute-start.5 = (bf16[272,128]{1,0:T(8,128)(2,1)S(1)}, bf16[272,128]{1,0:T(8,128)(2,1)S(1)}, u32[]{:S(2)}, u32[]{:S(2)}) collective-permute-start(bf16[272,128]{1,0:T(8,128)(2,1)S(1)} %get-tuple-element.88), channel_id=1, source_target_pairs={{0,3},{1,2},{2,1},{3,0},{4,7},{5,6},{6,5},{7,4},{8,11},{9,10},{10,... | collective-permute-start | bytes 208904 | tf_op jit(solution)/shard_map/ppermute | solution.py:443
  6.1 0.4 %shard_map.138 = (f32[256,128]{1,0:T(8,128)S(1)}, f32[2,128]{1,0:T(2,128)S(1)}, bf16[272,128]{1,0:T(8,128)(2,1)S(1)}) custom-call(bf16[256,256]{1,0:T(8,128)(2,1)S(1)} %get-tuple-element.68.encoded_ref, bf16[256,256]{1,0:T(8,128)(2,1)S(1)} %get-tuple-element.69.memory_ref, bf16[512,256]{1,0:T(8,128)(2,1)S(1)} %get-tuple-element.70.turned_ref, ...), custom_call_target="tpu_custom_call" | custom-call | tf_op jit(solution)/shard_map/pallas_call | solution.py:53
  6.6 0.1 collective-permute-start.2
  6.6 2.1 %collective-permute-done.5.recv_ref = bf16[272,128]{1,0:T(8,128)(2,1)S(1)} collective-permute-done((bf16[272,128]{1,0:T(8,128)(2,1)S(1)}, bf16[272,128]{1,0:T(8,128)(2,1)S(1)}, u32[]{:S(2)}, u32[]{:S(2)}) %collective-permute-start.5) | collective-permute-done | bytes 69664 | tf_op jit(solution)/shard_map/ppermute | solution.py:443
  8.8 2.2 %collective-permute-start.6 = (bf16[272,128]{1,0:T(8,128)(2,1)S(1)}, bf16[272,128]{1,0:T(8,128)(2,1)S(1)}, u32[]{:S(2)}, u32[]{:S(2)}) collective-permute-start(bf16[272,128]{1,0:T(8,128)(2,1)S(1)} %get-tuple-element.91), channel_id=1, source_target_pairs={{0,4},{1,5},{2,6},{3,7},{4,0},{5,1},{6,2},{7,3},{8,12},{9,13},{10,... | collective-permute-start | bytes 208904 | tf_op jit(solution)/shard_map/ppermute | solution.py:443
  11.0 1.1 %collective-permute-start.3 = (bf16[272,128]{1,0:T(8,128)(2,1)S(1)}, bf16[272,128]{1,0:T(8,128)(2,1)S(1)}, u32[]{:S(2)}, u32[]{:S(2)}) collective-permute-start(bf16[272,128]{1,0:T(8,128)(2,1)S(1)} %get-tuple-element.75), channel_id=1, source_target_pairs={{0,4},{1,5},{2,6},{3,7},{4,0},{5,1},{6,2},{7,3},{8,12},{9,13},{10,... | collective-permute-start | bytes 208904 | tf_op jit(solution)/shard_map/ppermute | solution.py:443
  12.1 1.3 %collective-permute-done.6.recv_ref = bf16[272,128]{1,0:T(8,128)(2,1)S(1)} collective-permute-done((bf16[272,128]{1,0:T(8,128)(2,1)S(1)}, bf16[272,128]{1,0:T(8,128)(2,1)S(1)}, u32[]{:S(2)}, u32[]{:S(2)}) %collective-permute-start.6) | collective-permute-done | bytes 69664 | tf_op jit(solution)/shard_map/ppermute | solution.py:443
  13.4 2.0 %collective-permute-start.7 = (bf16[272,128]{1,0:T(8,128)(2,1)S(1)}, bf16[272,128]{1,0:T(8,128)(2,1)S(1)}, u32[]{:S(2)}, u32[]{:S(2)}) collective-permute-start(bf16[272,128]{1,0:T(8,128)(2,1)S(1)} %get-tuple-element.96), channel_id=1, source_target_pairs={{0,8},{1,9},{2,10},{3,11},{4,12},{5,13},{6,14},{7,15},{8,0},{9,1},... | collective-permute-start | bytes 208904 | tf_op jit(solution)/shard_map/ppermute | solution.py:443
  15.5 1.5 %collective-permute-start.4 = (bf16[272,128]{1,0:T(8,128)(2,1)S(1)}, bf16[272,128]{1,0:T(8,128)(2,1)S(1)}, u32[]{:S(2)}, u32[]{:S(2)}) collective-permute-start(bf16[272,128]{1,0:T(8,128)(2,1)S(1)} %get-tuple-element.80), channel_id=1, source_target_pairs={{0,8},{1,9},{2,10},{3,11},{4,12},{5,13},{6,14},{7,15},{8,0},{9,1},... | collective-permute-start | bytes 208904 | tf_op jit(solution)/shard_map/ppermute | solution.py:443
  17.0 1.4 %collective-permute-done.7.recv_ref = bf16[272,128]{1,0:T(8,128)(2,1)S(1)} collective-permute-done((bf16[272,128]{1,0:T(8,128)(2,1)S(1)}, bf16[272,128]{1,0:T(8,128)(2,1)S(1)}, u32[]{:S(2)}, u32[]{:S(2)}) %collective-permute-start.7) | collective-permute-done | bytes 69664 | tf_op jit(solution)/shard_map/ppermute | solution.py:443
  18.5 2.7 %collective-permute-start.8 = (bf16[256,128]{1,0:T(8,128)(2,1)S(1)}, bf16[256,128]{1,0:T(8,128)(2,1)S(1)}, u32[]{:S(2)}, u32[]{:S(2)}) collective-permute-start(bf16[256,128]{1,0:T(8,128)(2,1)S(1)} %get-tuple-element.101), channel_id=1, source_target_pairs={{0,16},{1,17},{2,18},{3,19},{4,20},{5,21},{6,22},{7,23},{8,24},{9,... | collective-permute-start | bytes 196616 | tf_op jit(solution)/shard_map/ppermute | solution.py:443
  21.2 1.5 %collective-permute-start.10 = (bf16[256,128]{1,0:T(8,128)(2,1)S(1)}, bf16[256,128]{1,0:T(8,128)(2,1)S(1)}, u32[]{:S(2)}, u32[]{:S(2)}) collective-permute-start(bf16[256,128]{1,0:T(8,128)(2,1)S(1)} %get-tuple-element.85.after), channel_id=1, source_target_pairs={{0,16},{1,17},{2,18},{3,19},{4,20},{5,21},{6,22},{7,23},{8,24},{9,... | collective-permute-start | bytes 196616 | tf_op jit(solution)/shard_map/ppermute | solution.py:443
  22.7 1.4 %shard_map.142 = (bf16[256,1024]{1,0:T(8,128)(2,1)S(1)}, bf16[1024,256]{1,0:T(8,128)(2,1)S(1)}, bf16[3,192,256]{2,1,0:T(8,128)(2,1)S(1)}, bf16[16,64]{1,0:T(8,128)(2,1)S(1)}, bf16[128,512]{1,0:T(8,128)(2,1)S(1)}) custom-call(bf16[256,256]{1,0:T(8,128)(2,1)S(1)} %get-tuple-element.67.window_ref.refs_1_, bf16[256,128]{1,0:T(8,128)(2,1)S(1)} %get-tuple-element.85.after, ...), custom_call_target="tpu_custom_call" | custom-call | tf_op jit(solution)/shard_map/pallas_call | solution.py:53
  24.1 1.0 %collective-permute-done.8.recv_ref = bf16[256,128]{1,0:T(8,128)(2,1)S(1)} collective-permute-done((bf16[256,128]{1,0:T(8,128)(2,1)S(1)}, bf16[256,128]{1,0:T(8,128)(2,1)S(1)}, u32[]{:S(2)}, u32[]{:S(2)}) %collective-permute-start.8) | collective-permute-done | bytes 65568 | tf_op jit(solution)/shard_map/ppermute | solution.py:443
  25.2 0.3 %shard_map.148.refs_2_ = f32[256,256]{1,0:T(8,128)S(1)} custom-call(bf16[256,1024]{1,0:T(8,128)(2,1)S(1)} %get-tuple-element.86.refs_2_.refs_0_.key_ref, bf16[1024,256]{1,0:T(8,128)(2,1)S(1)} %get-tuple-element.87.refs_1_.read_ref, bf16[256,128]{1,0:T(8,128)(2,1)S(1)} %shard_map.147.refs_2_), custom_call_target="tpu_custom_call" | custom-call | tf_op jit(solution)/shard_map/pallas_call | solution.py:53
  25.5 0.9 %collective-permute-done.10.recv_ref = bf16[256,128]{1,0:T(8,128)(2,1)S(1)} collective-permute-done((bf16[256,128]{1,0:T(8,128)(2,1)S(1)}, bf16[256,128]{1,0:T(8,128)(2,1)S(1)}, u32[]{:S(2)}, u32[]{:S(2)}) %collective-permute-start.10) | collective-permute-done | bytes 65568 | tf_op jit(solution)/shard_map/ppermute | solution.py:443
  26.6 0.3 %shard_map.149.refs_2_ = f32[256,256]{1,0:T(8,128)S(1)} custom-call(bf16[256,1024]{1,0:T(8,128)(2,1)S(1)} %get-tuple-element.86.refs_2_.refs_0_.key_ref, bf16[1024,256]{1,0:T(8,128)(2,1)S(1)} %get-tuple-element.87.refs_1_.read_ref, f32[256,256]{1,0:T(8,128)S(1)} %shard_map.148.refs_2_, bf16[256,128]{1,0:T(8,128)(2,1)S(1)} %collective-permute-done.9.refs_3_), custom_call_target="tpu_custom_call" | custom-call | tf_op jit(solution)/shard_map/pallas_call | solution.py:53
  26.9 0.3 %shard_map.151.begun_ref = f32[256,256]{1,0:T(8,128)S(1)} custom-call(bf16[256,1024]{1,0:T(8,128)(2,1)S(1)} %get-tuple-element.86.refs_2_.refs_0_.key_ref, bf16[1024,256]{1,0:T(8,128)(2,1)S(1)} %get-tuple-element.87.refs_1_.read_ref, f32[256,256]{1,0:T(8,128)S(1)} %shard_map.149.refs_2_, bf16[256,128]{1,0:T(8,128)(2,1)S(1)} %shard_map.150.refs_3_), custom_call_target="tpu_custom_call" | custom-call | tf_op jit(solution)/shard_map/pallas_call | solution.py:53
  27.2 0.6 %collective-permute-done.11.refs_0_ = bf16[256,128]{1,0:T(8,128)(2,1)S(1)} collective-permute-done((bf16[256,128]{1,0:T(8,128)(2,1)S(1)}, bf16[256,128]{1,0:T(8,128)(2,1)S(1)}, u32[]{:S(2)}, u32[]{:S(2)}) %collective-permute-start.11) | collective-permute-done | bytes 65568 | tf_op jit(solution)/shard_map/ppermute | solution.py:474
  27.8 1.5 %shard_map.152 = f32[8,256]{1,0:T(8,128)} custom-call(bf16[256,1024]{1,0:T(8,128)(2,1)S(1)} %get-tuple-element.86.refs_2_.refs_0_.key_ref, bf16[1024,256]{1,0:T(8,128)(2,1)S(1)} %get-tuple-element.87.refs_1_.read_ref, f32[256,256]{1,0:T(8,128)S(1)} %shard_map.151.begun_ref, bf16[256,128]{1,0:T(8,128)(2,1)S(1)} %collective-permute-done.11.refs_0_, ...), custom_call_target="tpu_custom_call" | custom-call | tf_op jit(solution)/shard_map/pallas_call | solution.py:53
  (27 shorter events, 0.6 us)
Async XLA Ops:
  0.0 1.9 %collective-permute-start.1 = (s32[2,64]{1,0:T(2,128)}, s32[2,64]{1,0:T(2,128)S(1)}, u32[]{:S(2)}, u32[]{:S(2)}) collective-permute-start(s32[2,64]{1,0:T(2,128)} %refs_3_.2), channel_id=1, source_target_pairs={{0,1},{1,0},{2,3},{3,2},{4,5},{5,4},{6,7},{7,6},{8,9},{9,8},{10,11... | collective-permute-start | bytes 1544 | tf_op jit(solution)/shard_map/ppermute | solution.py:364
  0.5 1.5 %collective-permute-start = (bf16[128,256]{1,0:T(8,128)(2,1)}, bf16[128,256]{1,0:T(8,128)(2,1)S(1)}, u32[]{:S(2)}, u32[]{:S(2)}) collective-permute-start(bf16[128,256]{1,0:T(8,128)(2,1)} %bitcast.9), channel_id=1, source_target_pairs={{0,1},{1,0},{2,3},{3,2},{4,5},{5,4},{6,7},{7,6},{8,9},{9,8},{10,11... | collective-permute-start | bytes 196616 | tf_op jit(solution)/shard_map/ppermute | solution.py:363
  0.5 1.4 %copy-start.1 = (bf16[256,1024]{1,0:T(8,128)(2,1)S(1)}, bf16[256,1024]{1,0:T(8,128)(2,1)}, u32[]{:S(2)}) copy-start(bf16[256,1024]{1,0:T(8,128)(2,1)} %key_hbm.1) | copy-start | bytes 1572868
  0.5 1.5 %copy-start.4 = (bf16[256,256]{1,0:T(8,128)(2,1)S(1)}, bf16[256,256]{1,0:T(8,128)(2,1)}, u32[]{:S(2)}) copy-start(bf16[256,256]{1,0:T(8,128)(2,1)} %refs_10_.1) | copy-start | bytes 393220
  2.0 1.1 %copy-start = (bf16[256,1024]{1,0:T(8,128)(2,1)S(1)}, bf16[256,1024]{1,0:T(8,128)(2,1)}, u32[]{:S(2)}) copy-start(bf16[256,1024]{1,0:T(8,128)(2,1)} %value_ref.3) | copy-start | bytes 1572868
  3.0 19.7 %copy-start.2 = (bf16[256,256]{1,0:T(8,128)(2,1)}, bf16[256,256]{1,0:T(8,128)(2,1)S(1)}, u32[]{:S(2)}) copy-start(bf16[256,256]{1,0:T(8,128)(2,1)S(1)} %get-tuple-element.67.window_ref.refs_1_) | copy-start | bytes 393220
  3.5 5.2 %collective-permute-start.5 = (bf16[272,128]{1,0:T(8,128)(2,1)S(1)}, bf16[272,128]{1,0:T(8,128)(2,1)S(1)}, u32[]{:S(2)}, u32[]{:S(2)}) collective-permute-start(bf16[272,128]{1,0:T(8,128)(2,1)S(1)} %get-tuple-element.88), channel_id=1, source_target_pairs={{0,3},{1,2},{2,1},{3,0},{4,7},{5,6},{6,5},{7,4},{8,11},{9,10},{10,... | collective-permute-start | bytes 208904 | tf_op jit(solution)/shard_map/ppermute | solution.py:443
  6.6 4.3 %collective-permute-start.2 = (bf16[272,128]{1,0:T(8,128)(2,1)S(1)}, bf16[272,128]{1,0:T(8,128)(2,1)S(1)}, u32[]{:S(2)}, u32[]{:S(2)}) collective-permute-start(bf16[272,128]{1,0:T(8,128)(2,1)S(1)} %get-tuple-element.72), channel_id=1, source_target_pairs={{0,3},{1,2},{2,1},{3,0},{4,7},{5,6},{6,5},{7,4},{8,11},{9,10},{10,... | collective-permute-start | bytes 208904 | tf_op jit(solution)/shard_map/ppermute | solution.py:443
  8.8 4.6 %collective-permute-start.6 = (bf16[272,128]{1,0:T(8,128)(2,1)S(1)}, bf16[272,128]{1,0:T(8,128)(2,1)S(1)}, u32[]{:S(2)}, u32[]{:S(2)}) collective-permute-start(bf16[272,128]{1,0:T(8,128)(2,1)S(1)} %get-tuple-element.91), channel_id=1, source_target_pairs={{0,4},{1,5},{2,6},{3,7},{4,0},{5,1},{6,2},{7,3},{8,12},{9,13},{10,... | collective-permute-start | bytes 208904 | tf_op jit(solution)/shard_map/ppermute | solution.py:443
  11.0 4.5 %collective-permute-start.3 = (bf16[272,128]{1,0:T(8,128)(2,1)S(1)}, bf16[272,128]{1,0:T(8,128)(2,1)S(1)}, u32[]{:S(2)}, u32[]{:S(2)}) collective-permute-start(bf16[272,128]{1,0:T(8,128)(2,1)S(1)} %get-tuple-element.75), channel_id=1, source_target_pairs={{0,4},{1,5},{2,6},{3,7},{4,0},{5,1},{6,2},{7,3},{8,12},{9,13},{10,... | collective-permute-start | bytes 208904 | tf_op jit(solution)/shard_map/ppermute | solution.py:443
  13.4 5.0 %collective-permute-start.7 = (bf16[272,128]{1,0:T(8,128)(2,1)S(1)}, bf16[272,128]{1,0:T(8,128)(2,1)S(1)}, u32[]{:S(2)}, u32[]{:S(2)}) collective-permute-start(bf16[272,128]{1,0:T(8,128)(2,1)S(1)} %get-tuple-element.96), channel_id=1, source_target_pairs={{0,8},{1,9},{2,10},{3,11},{4,12},{5,13},{6,14},{7,15},{8,0},{9,1},... | collective-permute-start | bytes 208904 | tf_op jit(solution)/shard_map/ppermute | solution.py:443
  15.5 5.6 %collective-permute-start.4 = (bf16[272,128]{1,0:T(8,128)(2,1)S(1)}, bf16[272,128]{1,0:T(8,128)(2,1)S(1)}, u32[]{:S(2)}, u32[]{:S(2)}) collective-permute-start(bf16[272,128]{1,0:T(8,128)(2,1)S(1)} %get-tuple-element.80), channel_id=1, source_target_pairs={{0,8},{1,9},{2,10},{3,11},{4,12},{5,13},{6,14},{7,15},{8,0},{9,1},... | collective-permute-start | bytes 208904 | tf_op jit(solution)/shard_map/ppermute | solution.py:443
  18.5 6.6 %collective-permute-start.8 = (bf16[256,128]{1,0:T(8,128)(2,1)S(1)}, bf16[256,128]{1,0:T(8,128)(2,1)S(1)}, u32[]{:S(2)}, u32[]{:S(2)}) collective-permute-start(bf16[256,128]{1,0:T(8,128)(2,1)S(1)} %get-tuple-element.101), channel_id=1, source_target_pairs={{0,16},{1,17},{2,18},{3,19},{4,20},{5,21},{6,22},{7,23},{8,24},{9,... | collective-permute-start | bytes 196616 | tf_op jit(solution)/shard_map/ppermute | solution.py:443
  21.2 5.2 %collective-permute-start.10 = (bf16[256,128]{1,0:T(8,128)(2,1)S(1)}, bf16[256,128]{1,0:T(8,128)(2,1)S(1)}, u32[]{:S(2)}, u32[]{:S(2)}) collective-permute-start(bf16[256,128]{1,0:T(8,128)(2,1)S(1)} %get-tuple-element.85.after), channel_id=1, source_target_pairs={{0,16},{1,17},{2,18},{3,19},{4,20},{5,21},{6,22},{7,23},{8,24},{9,... | collective-permute-start | bytes 196616 | tf_op jit(solution)/shard_map/ppermute | solution.py:443
  25.1 1.5 %collective-permute-start.9 = (bf16[256,128]{1,0:T(8,128)(2,1)S(1)}, bf16[256,128]{1,0:T(8,128)(2,1)S(1)}, u32[]{:S(2)}, u32[]{:S(2)}) collective-permute-start(bf16[256,128]{1,0:T(8,128)(2,1)S(1)} %shard_map.147.refs_2_), channel_id=1, source_target_pairs={{0,1},{1,0},{2,3},{3,2},{4,5},{5,4},{6,7},{7,6},{8,9},{9,8},{10,11... | collective-permute-start | bytes 196616 | tf_op jit(solution)/shard_map/ppermute | solution.py:474
  26.5 1.3 %collective-permute-start.11 = (bf16[256,128]{1,0:T(8,128)(2,1)S(1)}, bf16[256,128]{1,0:T(8,128)(2,1)S(1)}, u32[]{:S(2)}, u32[]{:S(2)}) collective-permute-start(bf16[256,128]{1,0:T(8,128)(2,1)S(1)} %shard_map.150.refs_3_), channel_id=1, source_target_pairs={{0,1},{1,0},{2,3},{3,2},{4,5},{5,4},{6,7},{7,6},{8,9},{9,8},{10,11... | collective-permute-start | bytes 196616 | tf_op jit(solution)/shard_map/ppermute | solution.py:474
  26.9 0.9 %copy-start.3 = (bf16[256,256]{1,0:T(8,128)(2,1)S(1)}, bf16[256,256]{1,0:T(8,128)(2,1)}, u32[]{:S(2)}) copy-start(bf16[256,256]{1,0:T(8,128)(2,1)} %copy-done.2) | copy-start | bytes 393220

commit v6 on v5

--- a/solution.py
+++ b/solution.py
@@ -117,11 +117,13 @@
         load.wait()
 
 
-def encode_body(width, parts, *refs):
+def encode_body(width, parts, share, crossed, *refs):
     tiles, labels = refs[:parts], refs[parts : 2 * parts]
     rest = refs[2 * parts :]
     query_ref, pair_ref, pool_ref, qkv_ref, table_ref, gain_ref, out_ref, key_ref = rest[:8]
-    window_ref, encoded_ref, memory_ref, turned_ref, padded = rest[8:]
+    value_ref, decay_ref = rest[8:10]
+    window_ref, encoded_ref, memory_ref, turned_ref = rest[10:14]
+    state_refs, padded = rest[14:-1], rest[-1]
     place = lax.axis_index("space")
     dim = query_ref.shape[1]
     size = dim // ENC_HEADS
@@ -176,6 +178,9 @@
     cols = turned_ref.shape[0]
     start = pl.multiple_of(own_band(parts == 2) * cols, LANES)
     turned_ref[...] = key_ref[:, pl.ds(start, cols)].T
+    state_body(
+        share, crossed, 0, encoded_ref, memory_ref, turned_ref, value_ref, decay_ref, *state_refs
+    )
 
 
 def state_body(
@@ -388,13 +393,24 @@
         [pl.ANY] * len(loaded),
         micros=1,
     )(*loaded)
-    window, encoded, memory_in, turned = call(
-        functools.partial(encode_body, width, parts),
+    crossed = bands == 2
+    sizes = SIZES if sum(SIZES) == share else [share]
+    chains = len(sizes)
+    offsets = [sum(sizes[:chain]) for chain in range(chains)]
+
+    def kinds(group, carry=True):
+        rows = group * key_dim
+        pay = sds((rows + carry * carry_rows(group), val_dim), BF16)
+        return sds((rows, val_dim), F32), sds((group, val_dim), F32), pay
+
+    window, encoded, memory_in, turned, *opening = call(
+        functools.partial(encode_body, width, parts, share, crossed),
         (
             sds((window_rows, dim), BF16),
             sds((tokens, dim), BF16),
             sds((tokens, dim), BF16),
             sds((share * key_dim, dim), BF16),
+            *kinds(sizes[0]),
         ),
         (pltpu.VMEM((tokens + 2 * width, dim), BF16),),
         micros=2,
@@ -409,19 +425,11 @@
         gain,
         enc_out,
         key_proj,
+        value_proj,
+        rates,
     )
-    crossed = bands == 2
-    sizes = SIZES if sum(SIZES) == share else [share]
-    chains = len(sizes)
-    offsets = [sum(sizes[:chain]) for chain in range(chains)]
-
-    def kinds(group, carry=True):
-        rows = group * key_dim
-        pay = sds((rows + carry * carry_rows(group), val_dim), BF16)
-        return sds((rows, val_dim), F32), sds((group, val_dim), F32), pay
-
-    held = []
-    for offset, group in zip(offsets, sizes):
+    held = [(opening[0], opening[1], (), opening[2])]
+    for offset, group in zip(offsets[1:], sizes[1:]):
         total, product, payload = call(
             functools.partial(state_body, share, crossed, offset), kinds(group)
         )(encoded, memory_in, turned, value_proj, rates)
@@ -457,6 +465,7 @@
         (sds((window_rows, heads * key_dim), BF16), *[sds(x.shape, BF16) for x in late]),
         (pltpu.VMEM(key_proj.shape, BF16), pltpu.SemaphoreType.DMA((5,))),
         [pltpu.VMEM] * 2 + [pl.ANY] * (1 + len(late)),
+        micros=1,
     )(window, ahead, key_proj, *late)
     read_out, *late = late
 

time: 29.6 us -> 29.4 us (level)
    pallas_call x17 -> x16, Pallas kernels: 7.46 us -> 7.4 us  [run(): kernel(*[pltpu.with_memory_space_constraint(x, place) if place is held el...]
where the time goes in v6:
time: 29.4 us; the launch traced here: 29.3 us
  starting transfers between devices  14.4 us (49%)
  Pallas kernels  7.4 us (25%)
  waiting for transfers between devices  7.32 us (25%)
    ppermute x8, starting transfers between devices, shards(): arrived = lax.ppermute(payload, ('tm', 'space'), pairs)  13.7 us
    pallas_call x16, Pallas kernels, run(): kernel(*[pltpu.with_memory_space_constraint(x, place) if place is held el...  7.4 us
    ppermute x8, waiting for transfers between devices, shards(): arrived = lax.ppermute(payload, ('tm', 'space'), pairs)  6.72 us
  transfers between devices with their start and end apart: 12, of which 6 were waited for; matrix products, arithmetic and copies ran while one was open for 0% of the time, Pallas kernels for 15%

profile of v6, /device:TPU:0, one launch (start us, length us, event | category | flops | bytes accessed | tf_op | source)
XLA Modules:
  0.0 29.3 jit_solution(2186670903754863224)
XLA Ops:
  0.0 0.5 %collective-permute-start.1 = (s32[2,64]{1,0:T(2,128)}, s32[2,64]{1,0:T(2,128)S(1)}, u32[]{:S(2)}, u32[]{:S(2)}) collective-permute-start(s32[2,64]{1,0:T(2,128)} %refs_3_.2), channel_id=1, source_target_pairs={{0,1},{1,0},{2,3},{3,2},{4,5},{5,4},{6,7},{7,6},{8,9},{9,8},{10,11... | collective-permute-start | bytes 1544 | tf_op jit(solution)/shard_map/ppermute | solution.py:369
  0.5 1.4 %shard_map.136 = (bf16[128,256]{1,0:T(8,128)(2,1)S(1)}, bf16[32,128]{1,0:T(8,128)(2,1)S(1)}, bf16[256,768]{1,0:T(8,128)(2,1)S(1)}, s32[2,64]{1,0:T(2,128)S(1)}, ...) custom-call(bf16[128,256]{1,0:T(8,128)(2,1)} %bitcast.9, ...), custom_call_target="tpu_custom_call" | custom-call | flops 1000000000 | tf_op jit(solution)/shard_map/pallas_call | solution.py:53
  2.0 1.4 %shard_map.137 = (bf16[256,256]{1,0:T(8,128)(2,1)S(1)}, bf16[256,256]{1,0:T(8,128)(2,1)S(1)}, bf16[256,256]{1,0:T(8,128)(2,1)S(1)}, bf16[512,256]{1,0:T(8,128)(2...) custom-call(bf16[128,256]{1,0:T(8,128)(2,1)S(1)} %get-tuple-element.59.refs_0_, ...), custom_call_target="tpu_custom_call" | custom-call | flops 2000000000 | tf_op jit(solution)/shard_map/pallas_call | solution.py:53
  3.4 2.6 %collective-permute-start.5 = (bf16[272,128]{1,0:T(8,128)(2,1)S(1)}, bf16[272,128]{1,0:T(8,128)(2,1)S(1)}, u32[]{:S(2)}, u32[]{:S(2)}) collective-permute-start(bf16[272,128]{1,0:T(8,128)(2,1)S(1)} %get-tuple-element.88), channel_id=1, source_target_pairs={{0,3},{1,2},{2,1},{3,0},{4,7},{5,6},{6,5},{7,4},{8,11},{9,10},{10,... | collective-permute-start | bytes 208904 | tf_op jit(solution)/shard_map/ppermute | solution.py:451
  6.0 0.4 %shard_map.138 = (f32[256,128]{1,0:T(8,128)S(1)}, f32[2,128]{1,0:T(2,128)S(1)}, bf16[272,128]{1,0:T(8,128)(2,1)S(1)}) custom-call(bf16[256,256]{1,0:T(8,128)(2,1)S(1)} %get-tuple-element.69.encoded_ref, bf16[256,256]{1,0:T(8,128)(2,1)S(1)} %get-tuple-element.70.memory_ref, bf16[512,256]{1,0:T(8,128)(2,1)S(1)} %get-tuple-element.71.turned_ref, ...), custom_call_target="tpu_custom_call" | custom-call | tf_op jit(solution)/shard_map/pallas_call | solution.py:53
  6.4 0.1 collective-permute-start.2
  6.5 2.1 %collective-permute-done.5.recv_ref = bf16[272,128]{1,0:T(8,128)(2,1)S(1)} collective-permute-done((bf16[272,128]{1,0:T(8,128)(2,1)S(1)}, bf16[272,128]{1,0:T(8,128)(2,1)S(1)}, u32[]{:S(2)}, u32[]{:S(2)}) %collective-permute-start.5) | collective-permute-done | bytes 69664 | tf_op jit(solution)/shard_map/ppermute | solution.py:451
  8.6 2.2 %collective-permute-start.6 = (bf16[272,128]{1,0:T(8,128)(2,1)S(1)}, bf16[272,128]{1,0:T(8,128)(2,1)S(1)}, u32[]{:S(2)}, u32[]{:S(2)}) collective-permute-start(bf16[272,128]{1,0:T(8,128)(2,1)S(1)} %get-tuple-element.91), channel_id=1, source_target_pairs={{0,4},{1,5},{2,6},{3,7},{4,0},{5,1},{6,2},{7,3},{8,12},{9,13},{10,... | collective-permute-start | bytes 208904 | tf_op jit(solution)/shard_map/ppermute | solution.py:451
  10.9 1.0 %collective-permute-start.3 = (bf16[272,128]{1,0:T(8,128)(2,1)S(1)}, bf16[272,128]{1,0:T(8,128)(2,1)S(1)}, u32[]{:S(2)}, u32[]{:S(2)}) collective-permute-start(bf16[272,128]{1,0:T(8,128)(2,1)S(1)} %get-tuple-element.75), channel_id=1, source_target_pairs={{0,4},{1,5},{2,6},{3,7},{4,0},{5,1},{6,2},{7,3},{8,12},{9,13},{10,... | collective-permute-start | bytes 208904 | tf_op jit(solution)/shard_map/ppermute | solution.py:451
  11.9 1.4 %collective-permute-done.6.recv_ref = bf16[272,128]{1,0:T(8,128)(2,1)S(1)} collective-permute-done((bf16[272,128]{1,0:T(8,128)(2,1)S(1)}, bf16[272,128]{1,0:T(8,128)(2,1)S(1)}, u32[]{:S(2)}, u32[]{:S(2)}) %collective-permute-start.6) | collective-permute-done | bytes 69664 | tf_op jit(solution)/shard_map/ppermute | solution.py:451
  13.4 2.1 %collective-permute-start.7 = (bf16[272,128]{1,0:T(8,128)(2,1)S(1)}, bf16[272,128]{1,0:T(8,128)(2,1)S(1)}, u32[]{:S(2)}, u32[]{:S(2)}) collective-permute-start(bf16[272,128]{1,0:T(8,128)(2,1)S(1)} %get-tuple-element.96), channel_id=1, source_target_pairs={{0,8},{1,9},{2,10},{3,11},{4,12},{5,13},{6,14},{7,15},{8,0},{9,1},... | collective-permute-start | bytes 208904 | tf_op jit(solution)/shard_map/ppermute | solution.py:451
  15.5 1.5 %collective-permute-start.4 = (bf16[272,128]{1,0:T(8,128)(2,1)S(1)}, bf16[272,128]{1,0:T(8,128)(2,1)S(1)}, u32[]{:S(2)}, u32[]{:S(2)}) collective-permute-start(bf16[272,128]{1,0:T(8,128)(2,1)S(1)} %get-tuple-element.80), channel_id=1, source_target_pairs={{0,8},{1,9},{2,10},{3,11},{4,12},{5,13},{6,14},{7,15},{8,0},{9,1},... | collective-permute-start | bytes 208904 | tf_op jit(solution)/shard_map/ppermute | solution.py:451
  17.0 1.3 %collective-permute-done.7.recv_ref = bf16[272,128]{1,0:T(8,128)(2,1)S(1)} collective-permute-done((bf16[272,128]{1,0:T(8,128)(2,1)S(1)}, bf16[272,128]{1,0:T(8,128)(2,1)S(1)}, u32[]{:S(2)}, u32[]{:S(2)}) %collective-permute-start.7) | collective-permute-done | bytes 69664 | tf_op jit(solution)/shard_map/ppermute | solution.py:451
  18.3 2.8 %collective-permute-start.8 = (bf16[256,128]{1,0:T(8,128)(2,1)S(1)}, bf16[256,128]{1,0:T(8,128)(2,1)S(1)}, u32[]{:S(2)}, u32[]{:S(2)}) collective-permute-start(bf16[256,128]{1,0:T(8,128)(2,1)S(1)} %get-tuple-element.101), channel_id=1, source_target_pairs={{0,16},{1,17},{2,18},{3,19},{4,20},{5,21},{6,22},{7,23},{8,24},{9,... | collective-permute-start | bytes 196616 | tf_op jit(solution)/shard_map/ppermute | solution.py:451
  21.2 1.5 %collective-permute-start.10 = (bf16[256,128]{1,0:T(8,128)(2,1)S(1)}, bf16[256,128]{1,0:T(8,128)(2,1)S(1)}, u32[]{:S(2)}, u32[]{:S(2)}) collective-permute-start(bf16[256,128]{1,0:T(8,128)(2,1)S(1)} %get-tuple-element.85.after), channel_id=1, source_target_pairs={{0,16},{1,17},{2,18},{3,19},{4,20},{5,21},{6,22},{7,23},{8,24},{9,... | collective-permute-start | bytes 196616 | tf_op jit(solution)/shard_map/ppermute | solution.py:451
  22.6 1.4 %shard_map.142 = (bf16[256,1024]{1,0:T(8,128)(2,1)S(1)}, bf16[1024,256]{1,0:T(8,128)(2,1)S(1)}, bf16[3,192,256]{2,1,0:T(8,128)(2,1)S(1)}, bf16[16,64]{1,0:T(8,128)(2,1)S(1)}, bf16[128,512]{1,0:T(8,128)(2,1)S(1)}) custom-call(bf16[256,256]{1,0:T(8,128)(2,1)S(1)} %get-tuple-element.68.window_ref.refs_1_, bf16[256,128]{1,0:T(8,128)(2,1)S(1)} %get-tuple-element.85.after, ...), custom_call_target="tpu_custom_call" | custom-call | flops 1000000000 | tf_op jit(solution)/shard_map/pallas_call | solution.py:53
  24.0 0.9 %collective-permute-done.8.recv_ref = bf16[256,128]{1,0:T(8,128)(2,1)S(1)} collective-permute-done((bf16[256,128]{1,0:T(8,128)(2,1)S(1)}, bf16[256,128]{1,0:T(8,128)(2,1)S(1)}, u32[]{:S(2)}, u32[]{:S(2)}) %collective-permute-start.8) | collective-permute-done | bytes 65568 | tf_op jit(solution)/shard_map/ppermute | solution.py:451
  25.0 0.1 collective-permute-start.9
  25.1 0.3 %shard_map.147.refs_2_ = f32[256,256]{1,0:T(8,128)S(1)} custom-call(bf16[256,1024]{1,0:T(8,128)(2,1)S(1)} %get-tuple-element.86.refs_2_.refs_0_.key_ref, bf16[1024,256]{1,0:T(8,128)(2,1)S(1)} %get-tuple-element.87.refs_1_.read_ref, bf16[256,128]{1,0:T(8,128)(2,1)S(1)} %shard_map.146.refs_2_), custom_call_target="tpu_custom_call" | custom-call | tf_op jit(solution)/shard_map/pallas_call | solution.py:53
  25.4 1.0 %collective-permute-done.10.recv_ref = bf16[256,128]{1,0:T(8,128)(2,1)S(1)} collective-permute-done((bf16[256,128]{1,0:T(8,128)(2,1)S(1)}, bf16[256,128]{1,0:T(8,128)(2,1)S(1)}, u32[]{:S(2)}, u32[]{:S(2)}) %collective-permute-start.10) | collective-permute-done | bytes 65568 | tf_op jit(solution)/shard_map/ppermute | solution.py:451
  26.5 0.3 %shard_map.148.refs_2_ = f32[256,256]{1,0:T(8,128)S(1)} custom-call(bf16[256,1024]{1,0:T(8,128)(2,1)S(1)} %get-tuple-element.86.refs_2_.refs_0_.key_ref, bf16[1024,256]{1,0:T(8,128)(2,1)S(1)} %get-tuple-element.87.refs_1_.read_ref, f32[256,256]{1,0:T(8,128)S(1)} %shard_map.147.refs_2_, bf16[256,128]{1,0:T(8,128)(2,1)S(1)} %collective-permute-done.9.refs_3_), custom_call_target="tpu_custom_call" | custom-call | tf_op jit(solution)/shard_map/pallas_call | solution.py:53
  26.8 0.3 %shard_map.150.begun_ref = f32[256,256]{1,0:T(8,128)S(1)} custom-call(bf16[256,1024]{1,0:T(8,128)(2,1)S(1)} %get-tuple-element.86.refs_2_.refs_0_.key_ref, bf16[1024,256]{1,0:T(8,128)(2,1)S(1)} %get-tuple-element.87.refs_1_.read_ref, f32[256,256]{1,0:T(8,128)S(1)} %shard_map.148.refs_2_, bf16[256,128]{1,0:T(8,128)(2,1)S(1)} %shard_map.149.refs_3_), custom_call_target="tpu_custom_call" | custom-call | tf_op jit(solution)/shard_map/pallas_call | solution.py:53
  27.2 0.6 %collective-permute-done.11.refs_0_ = bf16[256,128]{1,0:T(8,128)(2,1)S(1)} collective-permute-done((bf16[256,128]{1,0:T(8,128)(2,1)S(1)}, bf16[256,128]{1,0:T(8,128)(2,1)S(1)}, u32[]{:S(2)}, u32[]{:S(2)}) %collective-permute-start.11) | collective-permute-done | bytes 65568 | tf_op jit(solution)/shard_map/ppermute | solution.py:483
  27.7 1.5 %shard_map.151 = f32[8,256]{1,0:T(8,128)} custom-call(bf16[256,1024]{1,0:T(8,128)(2,1)S(1)} %get-tuple-element.86.refs_2_.refs_0_.key_ref, bf16[1024,256]{1,0:T(8,128)(2,1)S(1)} %get-tuple-element.87.refs_1_.read_ref, f32[256,256]{1,0:T(8,128)S(1)} %shard_map.150.begun_ref, bf16[256,128]{1,0:T(8,128)(2,1)S(1)} %collective-permute-done.11.refs_0_, ...), custom_call_target="tpu_custom_call" | custom-call | tf_op jit(solution)/shard_map/pallas_call | solution.py:53
  (22 shorter events, 0.4 us)
Async XLA Ops:
  0.0 1.9 %collective-permute-start.1 = (s32[2,64]{1,0:T(2,128)}, s32[2,64]{1,0:T(2,128)S(1)}, u32[]{:S(2)}, u32[]{:S(2)}) collective-permute-start(s32[2,64]{1,0:T(2,128)} %refs_3_.2), channel_id=1, source_target_pairs={{0,1},{1,0},{2,3},{3,2},{4,5},{5,4},{6,7},{7,6},{8,9},{9,8},{10,11... | collective-permute-start | bytes 1544 | tf_op jit(solution)/shard_map/ppermute | solution.py:369
  0.5 1.5 %collective-permute-start = (bf16[128,256]{1,0:T(8,128)(2,1)}, bf16[128,256]{1,0:T(8,128)(2,1)S(1)}, u32[]{:S(2)}, u32[]{:S(2)}) collective-permute-start(bf16[128,256]{1,0:T(8,128)(2,1)} %bitcast.8), channel_id=1, source_target_pairs={{0,1},{1,0},{2,3},{3,2},{4,5},{5,4},{6,7},{7,6},{8,9},{9,8},{10,11... | collective-permute-start | bytes 196616 | tf_op jit(solution)/shard_map/ppermute | solution.py:368
  0.5 1.4 %copy-start = (bf16[256,1024]{1,0:T(8,128)(2,1)S(1)}, bf16[256,1024]{1,0:T(8,128)(2,1)}, u32[]{:S(2)}) copy-start(bf16[256,1024]{1,0:T(8,128)(2,1)} %value_ref.1) | copy-start | bytes 1572868
  0.5 1.5 %copy-start.1 = (bf16[256,1024]{1,0:T(8,128)(2,1)S(1)}, bf16[256,1024]{1,0:T(8,128)(2,1)}, u32[]{:S(2)}) copy-start(bf16[256,1024]{1,0:T(8,128)(2,1)} %key_hbm.1) | copy-start | bytes 1572868
  0.5 1.5 %copy-start.2 = (bf16[256,256]{1,0:T(8,128)(2,1)S(1)}, bf16[256,256]{1,0:T(8,128)(2,1)}, u32[]{:S(2)}) copy-start(bf16[256,256]{1,0:T(8,128)(2,1)} %refs_10_.1) | copy-start | bytes 393220
  3.4 5.2 %collective-permute-start.5 = (bf16[272,128]{1,0:T(8,128)(2,1)S(1)}, bf16[272,128]{1,0:T(8,128)(2,1)S(1)}, u32[]{:S(2)}, u32[]{:S(2)}) collective-permute-start(bf16[272,128]{1,0:T(8,128)(2,1)S(1)} %get-tuple-element.88), channel_id=1, source_target_pairs={{0,3},{1,2},{2,1},{3,0},{4,7},{5,6},{6,5},{7,4},{8,11},{9,10},{10,... | collective-permute-start | bytes 208904 | tf_op jit(solution)/shard_map/ppermute | solution.py:451
  6.4 4.4 %collective-permute-start.2 = (bf16[272,128]{1,0:T(8,128)(2,1)S(1)}, bf16[272,128]{1,0:T(8,128)(2,1)S(1)}, u32[]{:S(2)}, u32[]{:S(2)}) collective-permute-start(bf16[272,128]{1,0:T(8,128)(2,1)S(1)} %get-tuple-element.72), channel_id=1, source_target_pairs={{0,3},{1,2},{2,1},{3,0},{4,7},{5,6},{6,5},{7,4},{8,11},{9,10},{10,... | collective-permute-start | bytes 208904 | tf_op jit(solution)/shard_map/ppermute | solution.py:451
  8.6 4.7 %collective-permute-start.6 = (bf16[272,128]{1,0:T(8,128)(2,1)S(1)}, bf16[272,128]{1,0:T(8,128)(2,1)S(1)}, u32[]{:S(2)}, u32[]{:S(2)}) collective-permute-start(bf16[272,128]{1,0:T(8,128)(2,1)S(1)} %get-tuple-element.91), channel_id=1, source_target_pairs={{0,4},{1,5},{2,6},{3,7},{4,0},{5,1},{6,2},{7,3},{8,12},{9,13},{10,... | collective-permute-start | bytes 208904 | tf_op jit(solution)/shard_map/ppermute | solution.py:451
  10.9 4.6 %collective-permute-start.3 = (bf16[272,128]{1,0:T(8,128)(2,1)S(1)}, bf16[272,128]{1,0:T(8,128)(2,1)S(1)}, u32[]{:S(2)}, u32[]{:S(2)}) collective-permute-start(bf16[272,128]{1,0:T(8,128)(2,1)S(1)} %get-tuple-element.75), channel_id=1, source_target_pairs={{0,4},{1,5},{2,6},{3,7},{4,0},{5,1},{6,2},{7,3},{8,12},{9,13},{10,... | collective-permute-start | bytes 208904 | tf_op jit(solution)/shard_map/ppermute | solution.py:451
  13.4 4.9 %collective-permute-start.7 = (bf16[272,128]{1,0:T(8,128)(2,1)S(1)}, bf16[272,128]{1,0:T(8,128)(2,1)S(1)}, u32[]{:S(2)}, u32[]{:S(2)}) collective-permute-start(bf16[272,128]{1,0:T(8,128)(2,1)S(1)} %get-tuple-element.96), channel_id=1, source_target_pairs={{0,8},{1,9},{2,10},{3,11},{4,12},{5,13},{6,14},{7,15},{8,0},{9,1},... | collective-permute-start | bytes 208904 | tf_op jit(solution)/shard_map/ppermute | solution.py:451
  15.5 5.6 %collective-permute-start.4 = (bf16[272,128]{1,0:T(8,128)(2,1)S(1)}, bf16[272,128]{1,0:T(8,128)(2,1)S(1)}, u32[]{:S(2)}, u32[]{:S(2)}) collective-permute-start(bf16[272,128]{1,0:T(8,128)(2,1)S(1)} %get-tuple-element.80), channel_id=1, source_target_pairs={{0,8},{1,9},{2,10},{3,11},{4,12},{5,13},{6,14},{7,15},{8,0},{9,1},... | collective-permute-start | bytes 208904 | tf_op jit(solution)/shard_map/ppermute | solution.py:451
  18.3 6.6 %collective-permute-start.8 = (bf16[256,128]{1,0:T(8,128)(2,1)S(1)}, bf16[256,128]{1,0:T(8,128)(2,1)S(1)}, u32[]{:S(2)}, u32[]{:S(2)}) collective-permute-start(bf16[256,128]{1,0:T(8,128)(2,1)S(1)} %get-tuple-element.101), channel_id=1, source_target_pairs={{0,16},{1,17},{2,18},{3,19},{4,20},{5,21},{6,22},{7,23},{8,24},{9,... | collective-permute-start | bytes 196616 | tf_op jit(solution)/shard_map/ppermute | solution.py:451
  21.2 5.2 %collective-permute-start.10 = (bf16[256,128]{1,0:T(8,128)(2,1)S(1)}, bf16[256,128]{1,0:T(8,128)(2,1)S(1)}, u32[]{:S(2)}, u32[]{:S(2)}) collective-permute-start(bf16[256,128]{1,0:T(8,128)(2,1)S(1)} %get-tuple-element.85.after), channel_id=1, source_target_pairs={{0,16},{1,17},{2,18},{3,19},{4,20},{5,21},{6,22},{7,23},{8,24},{9,... | collective-permute-start | bytes 196616 | tf_op jit(solution)/shard_map/ppermute | solution.py:451
  25.0 1.5 %collective-permute-start.9 = (bf16[256,128]{1,0:T(8,128)(2,1)S(1)}, bf16[256,128]{1,0:T(8,128)(2,1)S(1)}, u32[]{:S(2)}, u32[]{:S(2)}) collective-permute-start(bf16[256,128]{1,0:T(8,128)(2,1)S(1)} %shard_map.146.refs_2_), channel_id=1, source_target_pairs={{0,1},{1,0},{2,3},{3,2},{4,5},{5,4},{6,7},{7,6},{8,9},{9,8},{10,11... | collective-permute-start | bytes 196616 | tf_op jit(solution)/shard_map/ppermute | solution.py:483
  26.4 1.3 %collective-permute-start.11 = (bf16[256,128]{1,0:T(8,128)(2,1)S(1)}, bf16[256,128]{1,0:T(8,128)(2,1)S(1)}, u32[]{:S(2)}, u32[]{:S(2)}) collective-permute-start(bf16[256,128]{1,0:T(8,128)(2,1)S(1)} %shard_map.149.refs_3_), channel_id=1, source_target_pairs={{0,1},{1,0},{2,3},{3,2},{4,5},{5,4},{6,7},{7,6},{8,9},{9,8},{10,11... | collective-permute-start | bytes 196616 | tf_op jit(solution)/shard_map/ppermute | solution.py:483
